TPU v7x, 32 devices: a whole 2x2x4 slice. The times are simulated.
32 devices in a mesh: dp: 8 (over z, y), expert: 4 (over x, core).
Axes of the slice: x: 2, y: 2, z: 4, core: 2. Of those that a mesh axis runs over, the one named last changes fastest.
Arguments:
- grad_parts: bfloat16 [8, 12, 704, 2048], P('dp', 'expert'), may hold values from -90 to 90
- momentum: float32 [12, 704, 2048], P('expert', 'dp'), may hold values from -6 to 6
Outputs:
- new_momentum: float32 [12, 704, 2048], P('expert', 'dp')
- muon_update: float32 [12, 704, 2048], P('expert', 'dp')
All inputs are finite; a program needn't handle non-finite values.
Results may differ from a plain program's by a relative error of at most 0.023.
Values may be sent and summed in bfloat16 or wider, within the bound.
No kernel may reach another device: no remote copies, remote signals or barrier semaphores. Data moves between devices by JAX's collectives and lax.ppermute only.
A program may use at most 128 MiB of HBM per device.

v0:
```python
import math

import jax
import jax.numpy as jnp
from jax import lax
from jax.sharding import PartitionSpec as P

NS_ITERS = 3


momentum_decay = 0.95
coef_a = 3.4445
coef_b = -4.775
coef_c = 2.0315


def broadcast(x, axis, root):
    mine = lax.axis_index(axis) == root
    return lax.psum(jnp.where(mine, x, jnp.zeros_like(x)), axis)


def orthogonalize(direction):
    flat = direction.astype(jnp.float32)
    norm_value = jnp.sqrt(jnp.sum(flat * flat))
    current = (flat / (norm_value + 1e-07)).astype(jnp.bfloat16)
    for step in range(NS_ITERS):
        gram = jnp.dot(current, current.T, preferred_element_type=jnp.float32).astype(jnp.bfloat16)
        square = jnp.dot(gram, gram, preferred_element_type=jnp.float32)
        poly = (coef_b * gram.astype(jnp.float32) + coef_c * square).astype(jnp.bfloat16)
        current = (
            coef_a * current.astype(jnp.float32)
            + jnp.dot(poly, current, preferred_element_type=jnp.float32)
        ).astype(jnp.bfloat16)
    return current


def local(grad_parts, momentum):
    partials = grad_parts[0]
    matrix_count = partials.shape[0]
    rows_whole = partials.shape[1]
    columns = partials.shape[2]
    ranks = lax.axis_size("dp")
    stride = ranks // matrix_count
    owner_ranks = [matrix * stride for matrix in range(matrix_count)]
    dp_rank = lax.axis_index("dp")
    summed = lax.psum_scatter(partials, "dp", scatter_dimension=1, tiled=True).astype(jnp.float32)
    shard_rows = summed.shape[1]
    total_sq = lax.psum(jnp.sum(summed * summed), ("dp", "expert"))
    entry_count = matrix_count * lax.axis_size("expert") * rows_whole * columns
    factor = jnp.minimum(1.0, lax.rsqrt(total_sq / entry_count + 1e-06))
    scaled = factor * summed
    new_momentum = momentum_decay * momentum + scaled
    direction = (scaled + momentum_decay * new_momentum).astype(jnp.bfloat16)
    gathered = lax.all_gather(direction, "dp", axis=1, tiled=True)
    selector = jnp.stack([dp_rank == owner for owner in owner_ranks]).astype(jnp.bfloat16)
    owned = jnp.tensordot(selector, gathered, axes=1, preferred_element_type=jnp.float32).astype(
        jnp.bfloat16
    )
    result = orthogonalize(owned)
    blocks_out = []
    for owner in owner_ranks:
        broadcast_full = broadcast(result, "dp", owner)
        blocks_out.append(
            lax.dynamic_slice_in_dim(broadcast_full, dp_rank * shard_rows, shard_rows, 0)
        )
    ortho = jnp.stack(blocks_out)
    muon_update = 0.2 * math.sqrt(max(rows_whole, columns)) * ortho.astype(jnp.float32)
    return (new_momentum, muon_update)


def solution(mesh):
    return jax.shard_map(
        local,
        mesh=mesh,
        in_specs=(P("dp", "expert", None, None), P("expert", "dp", None)),
        out_specs=(P("expert", "dp", None), P("expert", "dp", None)),
        check_vma=False,
    )
```

profile of v0, /device:TPU:0, one launch (start us, length us, event | category | flops | bytes accessed | tf_op | source)
XLA Modules:
  0.0 732.1 jit_solution(7370153273644001469)
XLA Ops:
  7.2 0.0 reduce-scatter.4.cloned.1.call-start
  7.2 13.6 %copy.6 = bf16[3,704,2048]{2,0,1:T(4,128)(2,1)} copy(bf16[3,704,2048]{2,1,0:T(8,128)(2,1)} %bitcast.42) | data formatting | bytes 17301504
  20.8 17.6 %copy.8 = bf16[88,8,3,2048]{3,1,2,0:T(8,128)(2,1)} copy(bf16[88,8,3,2048]{3,2,1,0:T(4,128)(2,1)} %bitcast.38) | data formatting | bytes 17301504
  38.4 0.0 reduce-scatter.4.cloned.1.call-update
  38.4 0.2 all-gather.2.cloned.1.call-start
  38.6 156.1 %reduce-scatter.4.cloned.1.call-done = bf16[88,6144]{1,0:T(8,128)(2,1)} async-done(((bf16[704,6144]{1,0:T(8,128)(2,1)}), bf16[88,6144]{1,0:T(8,128)(2,1)}) %reduce-scatter.4.cloned.1.call-update) | async-done | bytes 1081360
  194.8 3.3 reshape.7
  198.1 1.3 fusion.7
  199.4 39.1 %psum.28 = f32[]{:T(128)} all-reduce(f32[]{:T(128)} %fusion.7), channel_id=1, replica_groups=mesh['dp'=8,'expert'=4] {'dp','expert'}, use_global_device_ids=true, to_apply=%region_2.0 | all-reduce | flops 1 | bytes 8 | tf_op jit(solution)/shard_map/psum | solution.py:48
  239.2 4.4 fusion.6
  243.6 0.0 all-gather.2.cloned.1.call-update
  243.6 0.0 all-reduce.3.cloned.1.call-start
  243.7 128.4 %all-gather.2.cloned.1.call-done = bf16[3,704,2048]{2,1,0:T(8,128)(2,1)} async-done(((bf16[3,88,2048]{2,1,0:T(8,128)(2,1)}), bf16[3,704,2048]{2,1,0:T(8,128)(2,1)}) %all-gather.2.cloned.1.call-update) | async-done | bytes 8650768 | tf_op jit(solution)/shard_map/all_gather | solution.py:54
  372.1 24.9 %fusion = bf16[1,704,2048]{2,0,1:T(2,128)(2,1)S(1)} fusion(bf16[3,704,2048]{2,1,0:T(8,128)(2,1)} %all-gather.2.cloned.1.call-done, pred[1]{0:T(512)(128)(4,1)} %bitcast.3, pred[1]{0:T(512)(128)(4,1)} %bitcast.2, pred[1]{0:T(512)(128)(4,1)} %bitcast.1), kind=kOutput, calls=%fused_computation | convolution fusion | flops 8650758 | bytes 11534339 | tf_op jit(solution)/shard_map/dot_general | solution.py:56
  397.0 0.0 copy-start
  397.0 2.5 copy-done
  399.5 3.4 fusion.2
  403.5 5.0 fusion.3
  408.5 3.4 convolution_convert_fusion.2
  411.9 7.0 add_convert_fusion.2
  418.8 6.1 convolution_convert_fusion.1
  424.9 7.3 add_convert_fusion.1
  432.3 3.4 convolution_convert_fusion
  435.7 9.2 %broadcast_select_fusion.2 = (bf16[704,2048]{1,0:T(8,128)(2,1)}, bf16[704,2048]{1,0:T(8,128)(2,1)}, bf16[704,2048]{1,0:T(8,128)(2,1)}) fusion(pred[]{:T(512)} %eq.12, pred[]{:T(512)} %eq.14, pred[]{:T(512)} %eq.13, bf16[704,2048]{1,0:T(8,128)(2,1)S(1)} %add_convert_fusion.1, bf16[704,704]{1,0:T(8,128)(2,1)} %convolution_convert_fusion), kind=kOutput, calls=%fused_computation.12 | convolution fusion | flops 2740441088 | bytes 12525571 | tf_op jit(solution)/shard_map/dot_general | solution.py:32
  444.8 0.0 all-reduce.3.cloned.1.call-update
  444.8 276.5 %all-reduce.3.cloned.1.call-done = (bf16[704,2048]{1,0:T(8,128)(2,1)}, bf16[704,2048]{1,0:T(8,128)(2,1)}, bf16[704,2048]{1,0:T(8,128)(2,1)}) async-done(((bf16[704,2048]{1,0:T(8,128)(2,1)}, bf16[704,2048]{1,0:T(8,128)(2,1)}, bf16[704,2048]{1,0:T(8,128)(2,1)}), (bf16[704,2048]{1,0:T(8,128)(2,1)}, bf16[704,2048]{1,0:T(8,128)(2,1)}, bf16[704,2048]{1,0:T(8,128)(2,1)})) %all-reduce.3.cloned.1.call-update) | async-done | bytes 8650768 | tf_op jit(solution)/shard_map/psum | solution.py:19
  721.3 1.0 dynamic-slice_bitcast_fusion.2
  722.4 1.2 dynamic-slice_bitcast_fusion
  723.5 1.6 convert_multiply_fusion.3
Async XLA Ops:
  7.2 187.6 %reduce-scatter.4.cloned.1.call-start = ((), (), s32[]{:S(2)}) async-start(), calls=%async_computation.2 | async-start | bytes 9732096
  38.4 333.7 %all-gather.2.cloned.1.call-start = ((), (), s32[]{:S(2)}) async-start(), calls=%async_computation.1 | async-start | bytes 9732096 | tf_op jit(solution)/shard_map/all_gather | solution.py:54
  243.6 477.7 %all-reduce.3.cloned.1.call-start = ((), (), s32[]{:S(2)}) async-start(), calls=%async_computation.3 | async-start | bytes 17301504 | tf_op jit(solution)/shard_map/psum | solution.py:19
  397.0 2.5 copy-start
Sparse Core Ops, SparseCore 0:
  38.5 156.1 reduce-scatter.3
  243.7 128.3 all-gather.1
  445.0 276.3 all-reduce.2
where the time goes:
time: 741 us; the launch traced here: 732 us
  waiting for transfers between devices  561 us (76%)
  matrix products  61.2 us (8%)
  local copies, waits for them, and re-layouts  39.1 us (5%)
  blocking collectives  39.1 us (5%)
  other arithmetic  15.7 us (2%)
  between operations  15.6 us (2%)
    psum x1, waiting for transfers between devices, broadcast(): return lax.psum(jnp.where(mine, x, jnp.zeros_like(x)), axis)  276 us
    unnamed x4, waiting for transfers between devices  156 us
    all_gather x1, waiting for transfers between devices, local(): gathered = lax.all_gather(direction, 'dp', axis=1, tiled=True)  128 us
    psum x1, blocking collectives, local(): total_sq = lax.psum(jnp.sum(summed * summed), ('dp', 'expert'))  39.1 us
    unnamed x5, local copies, waits for them, and re-layouts  36.9 us
    dot_general x1, matrix products, local(): jnp.tensordot(selector, gathered, axes=1, preferred_element_type=jnp.floa...  24.9 us
    dot_general x3, matrix products, orthogonalize(): jnp.dot(poly, current, preferred_element_type=jnp.float32)  23.4 us
  transfers between devices with their start and end apart: 3, of which 3 were waited for; matrix products, arithmetic and copies ran while one was open for 0% of the time, Pallas kernels for 0%

commit v1 on v0

v1 whole, which is shorter than its diff:
```python
import math

import jax
import jax.numpy as jnp
from jax import lax
from jax.experimental import pallas as pl
from jax.experimental.pallas import tpu as pltpu
from jax.sharding import PartitionSpec as P

NS_ITERS = 3

momentum_decay = 0.95
coef_a = 3.4445
coef_b = -4.775
coef_c = 2.0315

BF16 = jnp.bfloat16
F32 = jnp.float32


def grid_of(ranks):
    log = ranks.bit_length() - 1
    ny = 2 ** (log // 2) if ranks >= 4 and ranks == 2**log else 1
    return ranks // ny, ny


def cycle_ranks(nz, ny):
    out = [z * ny for z in range(nz)]
    for r in range(nz):
        ys = list(range(1, ny))
        out += [(nz - 1 - r) * ny + y for y in (ys[::-1] if r % 2 else ys)]
    return out


def cycle_position(rank, nz, ny):
    z, y = rank // ny, rank % ny
    r = nz - 1 - z
    return jnp.where(y == 0, z, nz + r * (ny - 1) + jnp.where(r % 2 == 0, y - 1, ny - 1 - y))


def cycle_rank(position, nz, ny):
    q, m = position - nz, max(ny - 1, 1)
    r, k = q // m, q % m
    z = jnp.where(position < nz, position, nz - 1 - r)
    y = jnp.where(position < nz, 0, jnp.where(r % 2 == 0, k + 1, ny - 1 - k))
    return z * ny + y


def stream_widths(columns):
    wide = columns * 5 // 16 // 128 * 128
    return (wide, columns // 2 - wide)


def ring_reduce_scatter(partials, axis):
    ranks = lax.axis_size(axis)
    nz, ny = grid_of(ranks)
    cycle = cycle_ranks(nz, ny)
    pos = cycle_position(lax.axis_index(axis), nz, ny)
    mats, rows_whole, columns = partials.shape
    rows = rows_whole // ranks
    hops = list(zip(cycle, cycle[1:] + cycle[:1]))
    perms = {1: hops, -1: [(b, a) for a, b in hops]}
    widths = stream_widths(columns)
    starts, at = [], 0
    for w in widths:
        starts.append({1: at, -1: at + w})
        at += 2 * w

    def piece(g, d, step):
        dest = cycle_rank((pos - d * (1 + step)) % ranks, nz, ny)
        return lax.dynamic_slice(
            partials, (0, dest * rows, starts[g][d]), (mats, rows, widths[g])
        )

    acc = {(g, d): piece(g, d, 0) for g in range(len(widths)) for d in (1, -1)}
    for step in range(1, ranks):
        for g in range(len(widths)):
            got = {d: lax.ppermute(acc[g, d], axis, perms[d]) for d in (1, -1)}
            if g:
                got[1], got[-1], _, _ = lax.optimization_barrier(
                    (got[1], got[-1], acc[g - 1, 1], acc[g - 1, -1])
                )
            for d in (1, -1):
                total = got[d].astype(F32) + piece(g, d, step).astype(F32)
                acc[g, d] = total.astype(BF16) if step < ranks - 1 else total
    return [acc[g, d] for g in range(len(widths)) for d in (1, -1)]


def owner_ranks(mats, ranks):
    if mats == 3 and ranks == 8:
        return ((2, 4, 1), (3, 5, 6))
    stride = max(ranks // mats, 1)
    return tuple(
        tuple((m * stride + parity * (stride // 2)) % ranks for m in range(mats))
        for parity in (0, 1)
    )


def partner(rank, step, ranks, back=False):
    if ranks & (ranks - 1) == 0:
        return rank ^ step
    return (rank + (ranks - step if back else step)) % ranks


def owner_pairs(owners, step, ranks, experts):
    return [
        (partner(o, step, ranks, back=True) * experts + e, o * experts + e)
        for e in range(experts)
        for o in owners[e % 2]
    ]


def newton_schulz_body(count, block, scale, *refs):
    ins, outs = refs[:count], refs[count : 2 * count]
    d, a, q, qs = refs[2 * count :]
    rows = ins[0].shape[0]
    whole = d.shape[0]
    for i in range(count):
        d[i * rows : (i + 1) * rows, :] = ins[i][...]

    @pl.loop(0, whole // block)
    def _(i):
        r = pl.ds(pl.multiple_of(i * block, 16), block)
        a[r, :] = lax.dot_general(
            d[r, :], d[...], (((1,), (1,)), ((), ())), preferred_element_type=F32
        )

    gram = a[...]
    diagonal = lax.broadcasted_iota(jnp.int32, gram.shape, 0) == lax.broadcasted_iota(
        jnp.int32, gram.shape, 1
    )
    norm = jnp.sqrt(jnp.sum(jnp.where(diagonal, gram, 0.0)))
    inv = 1.0 / (norm + 1e-07)
    a[...] = (gram * inv) * inv
    for step in range(NS_ITERS):
        ab = a[...].astype(BF16)
        poly = coef_b * a[...] + coef_c * jnp.dot(ab, ab, preferred_element_type=F32)
        pb = poly.astype(BF16)
        if step == 0:
            q[...] = jnp.where(diagonal, poly + coef_a, poly)
        else:
            q[...] = coef_a * q[...] + jnp.dot(
                pb, q[...].astype(BF16), preferred_element_type=F32
            )
        if step < NS_ITERS - 1:
            t = jnp.dot(pb, ab, preferred_element_type=F32)
            a[...] = (
                (coef_a * coef_a) * a[...]
                + (2 * coef_a) * t
                + jnp.dot(pb, t.astype(BF16), preferred_element_type=F32)
            )
    qs[...] = (q[...] * (inv * scale)).astype(BF16)
    for i in range(count):
        outs[i][...] = jnp.dot(
            qs[i * rows : (i + 1) * rows, :], d[...], preferred_element_type=F32
        ).astype(BF16)


def newton_schulz(pieces, scale):
    count = len(pieces)
    rows, columns = pieces[0].shape
    whole = count * rows
    block = whole // 2 if whole % 32 == 0 else whole
    vmem = pl.BlockSpec(memory_space=pltpu.VMEM)
    return pl.pallas_call(
        lambda *refs: newton_schulz_body(count, block, scale, *refs),
        out_shape=[jax.ShapeDtypeStruct((rows, columns), BF16)] * count,
        in_specs=[vmem] * count,
        out_specs=[vmem] * count,
        scratch_shapes=[
            pltpu.VMEM((whole, columns), BF16),
            pltpu.VMEM((whole, whole), F32),
            pltpu.VMEM((whole, whole), F32),
            pltpu.VMEM((whole, whole), BF16),
        ],
        compiler_params=pltpu.CompilerParams(vmem_limit_bytes=50 * 2**20),
        name="newton_schulz",
        cost_estimate=pl.CostEstimate(
            flops=4 * whole * whole * columns + 18 * whole**3,
            bytes_accessed=4 * whole * columns,
            transcendentals=0,
        ),
    )(*pieces)


def local(grad_parts, momentum):
    partials = grad_parts[0]
    mats, rows_whole, columns = partials.shape
    ranks, experts = lax.axis_size("dp"), lax.axis_size("expert")
    rank, parity = lax.axis_index("dp"), lax.axis_index("expert") % 2
    both = ("dp", "expert")

    streams = ring_reduce_scatter(partials, "dp")
    square = sum(jnp.sum(s * s) for s in streams)
    squares = lax.all_to_all(
        jnp.full((ranks * experts, 1, 128), square), both, 0, 0, tiled=True
    )
    total = jnp.sum(squares[:, 0, 0])
    factor = jnp.minimum(1.0, lax.rsqrt(total / (mats * experts * rows_whole * columns) + 1e-06))
    summed = jnp.concatenate(streams, axis=2)
    scaled = factor * summed
    new_momentum = momentum_decay * momentum + scaled
    direction = (scaled + momentum_decay * new_momentum).astype(BF16)

    owners = owner_ranks(mats, ranks)
    owner = [jnp.where(parity == 0, owners[0][m], owners[1][m]) for m in range(mats)]
    far_first = list(range(ranks // 2, ranks)) + list(range(1, ranks // 2))
    pieces = [None] * ranks
    for step in [0] + far_first:
        target = partner(rank, step, ranks)
        which = sum(m * (target == owner[m]).astype(jnp.int32) for m in range(mats))
        mine = lax.dynamic_index_in_dim(direction, which, 0, keepdims=False)
        pieces[step] = (
            lax.ppermute(mine, both, owner_pairs(owners, step, ranks, experts)) if step else mine
        )
    result = newton_schulz(pieces, 0.2 * math.sqrt(max(rows_whole, columns)))
    back = [result[0]] + [None] * (ranks - 1)
    for step in far_first:
        pairs = owner_pairs(owners, step, ranks, experts)
        back[step] = lax.ppermute(result[step], both, [(b, a) for a, b in pairs])
    update = []
    for m in range(mats):
        mine = back[0]
        for step in range(1, ranks):
            mine = jnp.where(partner(rank, step, ranks) == owner[m], back[step], mine)
        update.append(mine.astype(F32))
    return (new_momentum, jnp.stack(update))


def solution(mesh):
    return jax.shard_map(
        local,
        mesh=mesh,
        in_specs=(P("dp", "expert", None, None), P("expert", "dp", None)),
        out_specs=(P("expert", "dp", None), P("expert", "dp", None)),
        check_vma=False,
    )
```

time: 741 us -> 202 us (0.27); the launches traced: 732 us -> 201 us
  waiting for transfers between devices: 561 us -> 75.4 us
  starting transfers between devices: 0.29 us -> 72.8 us
  matrix products: 61.2 us -> 0 us
  blocking collectives: 39.1 us -> 0 us
  local copies, waits for them, and re-layouts: 39.1 us -> 3.94 us
  Pallas kernels: 0 us -> 16.5 us
  other arithmetic: 15.7 us -> 27.9 us
  between operations: 15.6 us -> 4.47 us
    psum x1 -> x0, waiting for transfers between devices: 276 us -> none  [broadcast(): return lax.psum(jnp.where(mine, x, jnp.zeros_like(x)), axis)]
    unnamed x4 -> x0, waiting for transfers between devices: 156 us -> none
    all_gather x1 -> x0, waiting for transfers between devices: 128 us -> none  [local(): gathered = lax.all_gather(direction, 'dp', axis=1, tiled=True)]
    ppermute x0 -> x42, waiting for transfers between devices: none -> 68.4 us  [the longest x28 38 us: ring_reduce_scatter(): got = {d: lax.ppermute(acc[g, d], axis, perms[d]) for d in (1, -1)}]
    ppermute x0 -> x42, starting transfers between devices: none -> 67.7 us  [the longest x7 30.2 us: local(): lax.ppermute(mine, both, owner_pairs(owners, step, ranks, experts))]
    dot_general x7 -> x0, matrix products: 61.2 us -> none  [the longest x1 24.9 us: local(): jnp.tensordot(selector, gathered, axes=1, preferred_element_type=jnp.floa...]
    psum x1 -> x0, blocking collectives: 39.1 us -> none  [local(): total_sq = lax.psum(jnp.sum(summed * summed), ('dp', 'expert'))]
    unnamed x5 -> x14, local copies, waits for them, and re-layouts: 36.9 us -> 0.75 us
  transfers between devices with their start and end apart: 3 -> 43, of which waited for: 3 -> 25; matrix products, arithmetic and copies ran while one was open for 0% -> 9% of each run, Pallas kernels for 0% -> 0%
where the time goes in v1:
time: 202 us; the launch traced here: 201 us
  waiting for transfers between devices  75.4 us (37%)
  starting transfers between devices  72.8 us (36%)
  other arithmetic  27.9 us (14%)
  Pallas kernels  16.5 us (8%)
  between operations  4.47 us (2%)
  local copies, waits for them, and re-layouts  3.94 us (2%)
    ppermute x28, waiting for transfers between devices, ring_reduce_scatter(): got = {d: lax.ppermute(acc[g, d], axis, perms[d]) for d in (1, -1)}  38 us
    ppermute x7, starting transfers between devices, local(): lax.ppermute(mine, both, owner_pairs(owners, step, ranks, experts))  30.2 us
    ppermute x28, starting transfers between devices, ring_reduce_scatter(): got = {d: lax.ppermute(acc[g, d], axis, perms[d]) for d in (1, -1)}  30.2 us
    ppermute x7, waiting for transfers between devices, local(): back[step] = lax.ppermute(result[step], both, [(b, a) for a, b in pairs])  25.8 us
    pallas_call x1, Pallas kernels, newton_schulz(): pl.pallas_call(lambda *refs: newton_schulz_body(count, block, scale, *ref...  16.5 us
    convert_element_type x12, other arithmetic, ring_reduce_scatter(): acc[g, d] = total.astype(BF16) if step < ranks - 1 else total  14.4 us
    ppermute x7, starting transfers between devices, local(): back[step] = lax.ppermute(result[step], both, [(b, a) for a, b in pairs])  7.35 us
    all_to_all x1, waiting for transfers between devices, local(): lax.all_to_all(jnp.full((ranks * experts, 1, 128), square), both, 0, 0, t...  6.95 us
  transfers between devices with their start and end apart: 43, of which 25 were waited for; matrix products, arithmetic and copies ran while one was open for 9% of the time, Pallas kernels for 0%

profile of v1, /device:TPU:0, one launch (start us, length us, event | category | flops | bytes accessed | tf_op | source)
XLA Modules:
  0.0 201.0 jit_solution(1361470488945282584)
XLA Ops:
  1.9 3.0 %collective-permute-start.7 = (bf16[3,88,640]{2,1,0:T(8,128)(2,1)S(1)}, bf16[3,88,640]{2,1,0:T(8,128)(2,1)S(1)}, u32[]{:S(2)}, u32[]{:S(2)}) collective-permute-start(bf16[3,88,640]{2,1,0:T(8,128)(2,1)S(1)} %get-tuple-element.84), channel_id=1, source_target_pairs={{8,0},{16,8},{24,16},{28,24},{20,28},{12,20},{4,12},{0,4},{9,1},{1... | collective-permute-start | bytes 1013768 | tf_op jit(solution)/shard_map/ppermute | solution.py:78
  6.1 2.0 collective-permute-start.15
  8.2 5.5 %collective-permute-done.7 = bf16[3,88,640]{2,1,0:T(8,128)(2,1)S(1)} collective-permute-done((bf16[3,88,640]{2,1,0:T(8,128)(2,1)S(1)}, bf16[3,88,640]{2,1,0:T(8,128)(2,1)S(1)}, u32[]{:S(2)}, u32[]{:S(2)}) %collective-permute-start.7) | collective-permute-done | bytes 337952 | tf_op jit(solution)/shard_map/ppermute | solution.py:78
  13.7 2.0 %collective-permute-done = bf16[3,88,640]{2,1,0:T(8,128)(2,1)S(1)} collective-permute-done((bf16[3,88,640]{2,1,0:T(8,128)(2,1)S(1)}, bf16[3,88,640]{2,1,0:T(8,128)(2,1)S(1)}, u32[]{:S(2)}, u32[]{:S(2)}) %collective-permute-start) | collective-permute-done | bytes 337952 | tf_op jit(solution)/shard_map/ppermute | solution.py:78
  17.0 1.6 collective-permute-start.8
  20.3 1.6 collective-permute-start.17
  22.3 4.3 %collective-permute-done.8 = bf16[3,88,640]{2,1,0:T(8,128)(2,1)S(1)} collective-permute-done((bf16[3,88,640]{2,1,0:T(8,128)(2,1)S(1)}, bf16[3,88,640]{2,1,0:T(8,128)(2,1)S(1)}, u32[]{:S(2)}, u32[]{:S(2)}) %collective-permute-start.8) | collective-permute-done | bytes 337952 | tf_op jit(solution)/shard_map/ppermute | solution.py:78
  26.7 1.8 collective-permute-done.1
  36.0 2.5 %collective-permute-done.9 = bf16[3,88,640]{2,1,0:T(8,128)(2,1)S(1)} collective-permute-done((bf16[3,88,640]{2,1,0:T(8,128)(2,1)S(1)}, bf16[3,88,640]{2,1,0:T(8,128)(2,1)S(1)}, u32[]{:S(2)}, u32[]{:S(2)}) %collective-permute-start.9) | collective-permute-done | bytes 337952 | tf_op jit(solution)/shard_map/ppermute | solution.py:78
  41.3 1.6 collective-permute-start.10
  45.6 1.6 collective-permute-start.21
  47.6 2.5 %collective-permute-done.10 = bf16[3,88,640]{2,1,0:T(8,128)(2,1)S(1)} collective-permute-done((bf16[3,88,640]{2,1,0:T(8,128)(2,1)S(1)}, bf16[3,88,640]{2,1,0:T(8,128)(2,1)S(1)}, u32[]{:S(2)}, u32[]{:S(2)}) %collective-permute-start.10) | collective-permute-done | bytes 337952 | tf_op jit(solution)/shard_map/ppermute | solution.py:78
  52.9 1.6 collective-permute-start.11
  57.1 1.6 collective-permute-start.23
  59.2 2.5 %collective-permute-done.11 = bf16[3,88,640]{2,1,0:T(8,128)(2,1)S(1)} collective-permute-done((bf16[3,88,640]{2,1,0:T(8,128)(2,1)S(1)}, bf16[3,88,640]{2,1,0:T(8,128)(2,1)S(1)}, u32[]{:S(2)}, u32[]{:S(2)}) %collective-permute-start.11) | collective-permute-done | bytes 337952 | tf_op jit(solution)/shard_map/ppermute | solution.py:78
  64.5 1.6 collective-permute-start.12
  68.7 1.6 collective-permute-start.25
  70.8 2.5 %collective-permute-done.12 = bf16[3,88,640]{2,1,0:T(8,128)(2,1)S(1)} collective-permute-done((bf16[3,88,640]{2,1,0:T(8,128)(2,1)S(1)}, bf16[3,88,640]{2,1,0:T(8,128)(2,1)S(1)}, u32[]{:S(2)}, u32[]{:S(2)}) %collective-permute-start.12) | collective-permute-done | bytes 337952 | tf_op jit(solution)/shard_map/ppermute | solution.py:78
  76.1 1.7 collective-permute-start.13
  80.3 1.7 collective-permute-start.27
  82.4 2.2 %collective-permute-done.13 = bf16[3,88,640]{2,1,0:T(8,128)(2,1)S(1)} collective-permute-done((bf16[3,88,640]{2,1,0:T(8,128)(2,1)S(1)}, bf16[3,88,640]{2,1,0:T(8,128)(2,1)S(1)}, u32[]{:S(2)}, u32[]{:S(2)}) %collective-permute-start.13) | collective-permute-done | bytes 337952 | tf_op jit(solution)/shard_map/ppermute | solution.py:78
  86.1 2.2 %multiply_reduce_fusion = (f32[]{:T(128)}, f32[3,88,640]{2,1,0:T(8,128)S(1)}, f32[]{:T(128)}, f32[3,88,640]{2,1,0:T(8,128)S(1)}) fusion(bf16[1,3,704,2048]{3,2,1,0:T(8,128)(2,1)} %param.2, s32[]{:T(128)S(6)} %select_n.737, bf16[3,88,640]{2,1,0:T(8,128)(2,1)} %copy-done.1, s32[]{:T(128)S(6)} %select_n.705, bf16[3,88,640]{2,1,0:T(8,128)(2,1)} %collective-permute-done.6), kind=kLoop, calls=%fused_computation.30 | loop fusion | flops 1689598 | bytes 2703376 | tf_op jit(solution)/shard_map/reduce_sum | solution.py:194
  89.8 2.9 %multiply_reduce_fusion.3 = (f32[]{:T(128)}, f32[3,88,384]{2,1,0:T(8,128)}, f32[]{:T(128)}, f32[3,88,384]{2,1,0:T(8,128)}) fusion(bf16[1,3,704,2048]{3,2,1,0:T(8,128)(2,1)} %param.2, s32[]{:T(128)S(6)} %select_n.705, bf16[3,88,384]{2,1,0:T(8,128)(2,1)} %collective-permute-done.26, s32[]{:T(128)S(6)} %select_n.737, bf16[3,88,384]{2,1,0:T(8,128)(2,1)} %collective-permute-done.27), kind=kLoop, calls=%fused_computation.59 | loop fusion | flops 1013758 | bytes 1622032 | tf_op jit(solution)/shard_map/reduce_sum | solution.py:194
  94.5 5.1 %all-to-all-start = ((f32[32,1,128]{2,1,0:T(1,128)}), f32[32,1,128]{2,1,0:T(1,128)S(1)}, u32[]{:S(2)}, u32[]{:S(2)}) async-start(f32[32,1,128]{2,1,0:T(1,128)} %broadcast_in_dim.3), calls=%async_computation | async-start | bytes 32768 | tf_op jit(solution)/shard_map/all_to_all | solution.py:195
  99.7 6.9 %all-to-all-done = f32[32,1,128]{2,1,0:T(1,128)S(1)} async-done(((f32[32,1,128]{2,1,0:T(1,128)}), f32[32,1,128]{2,1,0:T(1,128)S(1)}, u32[]{:S(2)}, u32[]{:S(2)}) %all-to-all-start) | async-done | bytes 16416 | tf_op jit(solution)/shard_map/all_to_all | solution.py:195
  108.0 2.9 %add_convert_fusion = (bf16[3,88,2048]{2,1,0:T(8,128)(2,1)S(1)}, f32[3,88,2048]{2,1,0:T(8,128)}) fusion(f32[3,88,384]{2,1,0:T(8,128)} %get-tuple-element.57, f32[3,88,384]{2,1,0:T(8,128)} %get-tuple-element.51, f32[3,88,640]{2,1,0:T(8,128)S(1)} %get-tuple-element.53, f32[3,88,640]{2,1,0:T(8,128)S(1)} %get-tuple-element.59, f32[]{:T(128)S(6)} %min_shard_map.3, ...), kind=kLoop, calls=%fused_computation.1 | loop fusion | flops 4866048 | bytes 7569412 | tf_op jit(solution)/shard_map/convert_element_type | solution.py:203
  113.3 7.3 %collective-permute-start.31 = (bf16[88,2048]{1,0:T(8,128)(2,1)S(1)}, bf16[88,2048]{1,0:T(8,128)(2,1)S(1)}, u32[]{:S(2)}, u32[]{:S(2)}) collective-permute-start(bf16[88,2048]{1,0:T(8,128)(2,1)S(1)} %get-tuple-element.91), channel_id=1, source_target_pairs={{24,8},{0,16},{20,4},{29,13},{5,21},{9,25},{26,10},{2,18},{22,6},{... | collective-permute-start | bytes 1081352 | tf_op jit(solution)/shard_map/ppermute | solution.py:214
  121.3 18.7 %collective-permute-start.29 = (bf16[88,2048]{1,0:T(8,128)(2,1)S(1)}, bf16[88,2048]{1,0:T(8,128)(2,1)S(1)}, u32[]{:S(2)}, u32[]{:S(2)}) collective-permute-start(bf16[88,2048]{1,0:T(8,128)(2,1)S(1)} %get-tuple-element.93), channel_id=1, source_target_pairs={{0,8},{24,16},{12,4},{5,13},{29,21},{17,25},{2,10},{26,18},{14,6},... | collective-permute-start | bytes 1081352 | tf_op jit(solution)/shard_map/ppermute | solution.py:214
  141.7 3.3 %collective-permute-done.29.refs_2_ = bf16[88,2048]{1,0:T(8,128)(2,1)S(1)} collective-permute-done((bf16[88,2048]{1,0:T(8,128)(2,1)S(1)}, bf16[88,2048]{1,0:T(8,128)(2,1)S(1)}, u32[]{:S(2)}, u32[]{:S(2)}) %collective-permute-start.29) | collective-permute-done | bytes 360480 | tf_op jit(solution)/shard_map/ppermute | solution.py:214
  146.3 16.5 %newton_schulz.1 = (bf16[88,2048]{1,0:T(8,128)(2,1)S(1)}, bf16[88,2048]{1,0:T(8,128)(2,1)S(1)}, bf16[88,2048]{1,0:T(8,128)(2,1)S(1)}, bf16[88,2048]{1,0:T(8,128)...) custom-call(bf16[88,2048]{1,0:T(8,128)(2,1)S(1)} %get-tuple-element., ...), custom_call_target="tpu_custom_call" | custom-call | flops 10340532224 | bytes 5767168 | tf_op jit(solution)/shard_map/newton_schulz/pallas_call | solution.py:165
  170.3 24.7 %collective-permute-done.38 = bf16[88,2048]{1,0:T(8,128)(2,1)} collective-permute-done((bf16[88,2048]{1,0:T(8,128)(2,1)S(1)}, bf16[88,2048]{1,0:T(8,128)(2,1)}, u32[]{:S(2)}, u32[]{:S(2)}) %collective-permute-start.38) | collective-permute-done | bytes 360480 | tf_op jit(solution)/shard_map/ppermute | solution.py:220
  199.5 1.5 maximum_convert_fusion
  (93 shorter events, 57.1 us)
Async XLA Ops:
  1.9 11.8 %collective-permute-start.7 = (bf16[3,88,640]{2,1,0:T(8,128)(2,1)S(1)}, bf16[3,88,640]{2,1,0:T(8,128)(2,1)S(1)}, u32[]{:S(2)}, u32[]{:S(2)}) collective-permute-start(bf16[3,88,640]{2,1,0:T(8,128)(2,1)S(1)} %get-tuple-element.84), channel_id=1, source_target_pairs={{8,0},{16,8},{24,16},{28,24},{20,28},{12,20},{4,12},{0,4},{9,1},{1... | collective-permute-start | bytes 1013768 | tf_op jit(solution)/shard_map/ppermute | solution.py:78
  4.9 10.9 %collective-permute-start = (bf16[3,88,640]{2,1,0:T(8,128)(2,1)S(1)}, bf16[3,88,640]{2,1,0:T(8,128)(2,1)S(1)}, u32[]{:S(2)}, u32[]{:S(2)}) collective-permute-start(bf16[3,88,640]{2,1,0:T(8,128)(2,1)S(1)} %get-tuple-element.85), channel_id=1, source_target_pairs={{0,8},{8,16},{16,24},{24,28},{28,20},{20,12},{12,4},{4,0},{1,9},{9... | collective-permute-start | bytes 1013768 | tf_op jit(solution)/shard_map/ppermute | solution.py:78
  6.1 13.0 %collective-permute-start.15 = (bf16[3,88,384]{2,1,0:T(8,128)(2,1)S(1)}, bf16[3,88,384]{2,1,0:T(8,128)(2,1)S(1)}, u32[]{:S(2)}, u32[]{:S(2)}) collective-permute-start(bf16[3,88,384]{2,1,0:T(8,128)(2,1)S(1)} %get-tuple-element.86), channel_id=1, source_target_pairs={{8,0},{16,8},{24,16},{28,24},{20,28},{12,20},{4,12},{0,4},{9,1},{1... | collective-permute-start | bytes 608264 | tf_op jit(solution)/shard_map/ppermute | solution.py:78
  8.1 11.0 %collective-permute-start.14 = (bf16[3,88,384]{2,1,0:T(8,128)(2,1)S(1)}, bf16[3,88,384]{2,1,0:T(8,128)(2,1)S(1)}, u32[]{:S(2)}, u32[]{:S(2)}) collective-permute-start(bf16[3,88,384]{2,1,0:T(8,128)(2,1)S(1)} %get-tuple-element.87), channel_id=1, source_target_pairs={{0,8},{8,16},{16,24},{24,28},{28,20},{20,12},{12,4},{4,0},{1,9},{9... | collective-permute-start | bytes 608264 | tf_op jit(solution)/shard_map/ppermute | solution.py:78
  17.0 9.6 %collective-permute-start.8 = (bf16[3,88,640]{2,1,0:T(8,128)(2,1)S(1)}, bf16[3,88,640]{2,1,0:T(8,128)(2,1)S(1)}, u32[]{:S(2)}, u32[]{:S(2)}) collective-permute-start(bf16[3,88,640]{2,1,0:T(8,128)(2,1)S(1)} %get-tuple-element.82), channel_id=1, source_target_pairs={{8,0},{16,8},{24,16},{28,24},{20,28},{12,20},{4,12},{0,4},{9,1},{1... | collective-permute-start | bytes 1013768 | tf_op jit(solution)/shard_map/ppermute | solution.py:78
  18.6 9.8 %collective-permute-start.1 = (bf16[3,88,640]{2,1,0:T(8,128)(2,1)S(1)}, bf16[3,88,640]{2,1,0:T(8,128)(2,1)S(1)}, u32[]{:S(2)}, u32[]{:S(2)}) collective-permute-start(bf16[3,88,640]{2,1,0:T(8,128)(2,1)S(1)} %get-tuple-element.83), channel_id=1, source_target_pairs={{0,8},{8,16},{16,24},{24,28},{28,20},{20,12},{12,4},{4,0},{1,9},{9... | collective-permute-start | bytes 1013768 | tf_op jit(solution)/shard_map/ppermute | solution.py:78
  20.3 11.6 %collective-permute-start.17 = (bf16[3,88,384]{2,1,0:T(8,128)(2,1)S(1)}, bf16[3,88,384]{2,1,0:T(8,128)(2,1)S(1)}, u32[]{:S(2)}, u32[]{:S(2)}) collective-permute-start(bf16[3,88,384]{2,1,0:T(8,128)(2,1)S(1)} %get-tuple-element.80), channel_id=1, source_target_pairs={{8,0},{16,8},{24,16},{28,24},{20,28},{12,20},{4,12},{0,4},{9,1},{1... | collective-permute-start | bytes 608264 | tf_op jit(solution)/shard_map/ppermute | solution.py:78
  21.9 10.9 %collective-permute-start.16 = (bf16[3,88,384]{2,1,0:T(8,128)(2,1)S(1)}, bf16[3,88,384]{2,1,0:T(8,128)(2,1)S(1)}, u32[]{:S(2)}, u32[]{:S(2)}) collective-permute-start(bf16[3,88,384]{2,1,0:T(8,128)(2,1)S(1)} %get-tuple-element.81), channel_id=1, source_target_pairs={{0,8},{8,16},{16,24},{24,28},{28,20},{20,12},{12,4},{4,0},{1,9},{9... | collective-permute-start | bytes 608264 | tf_op jit(solution)/shard_map/ppermute | solution.py:78
  29.7 8.8 %collective-permute-start.9 = (bf16[3,88,640]{2,1,0:T(8,128)(2,1)S(1)}, bf16[3,88,640]{2,1,0:T(8,128)(2,1)S(1)}, u32[]{:S(2)}, u32[]{:S(2)}) collective-permute-start(bf16[3,88,640]{2,1,0:T(8,128)(2,1)S(1)} %get-tuple-element.78), channel_id=1, source_target_pairs={{8,0},{16,8},{24,16},{28,24},{20,28},{12,20},{4,12},{0,4},{9,1},{1... | collective-permute-start | bytes 1013768 | tf_op jit(solution)/shard_map/ppermute | solution.py:78
  30.9 9.1 %collective-permute-start.2 = (bf16[3,88,640]{2,1,0:T(8,128)(2,1)S(1)}, bf16[3,88,640]{2,1,0:T(8,128)(2,1)S(1)}, u32[]{:S(2)}, u32[]{:S(2)}) collective-permute-start(bf16[3,88,640]{2,1,0:T(8,128)(2,1)S(1)} %get-tuple-element.79), channel_id=1, source_target_pairs={{0,8},{8,16},{16,24},{24,28},{28,20},{20,12},{12,4},{4,0},{1,9},{9... | collective-permute-start | bytes 1013768 | tf_op jit(solution)/shard_map/ppermute | solution.py:78
  34.0 9.4 %collective-permute-start.19 = (bf16[3,88,384]{2,1,0:T(8,128)(2,1)S(1)}, bf16[3,88,384]{2,1,0:T(8,128)(2,1)S(1)}, u32[]{:S(2)}, u32[]{:S(2)}) collective-permute-start(bf16[3,88,384]{2,1,0:T(8,128)(2,1)S(1)} %get-tuple-element.76), channel_id=1, source_target_pairs={{8,0},{16,8},{24,16},{28,24},{20,28},{12,20},{4,12},{0,4},{9,1},{1... | collective-permute-start | bytes 608264 | tf_op jit(solution)/shard_map/ppermute | solution.py:78
  34.7 9.7 %collective-permute-start.18 = (bf16[3,88,384]{2,1,0:T(8,128)(2,1)S(1)}, bf16[3,88,384]{2,1,0:T(8,128)(2,1)S(1)}, u32[]{:S(2)}, u32[]{:S(2)}) collective-permute-start(bf16[3,88,384]{2,1,0:T(8,128)(2,1)S(1)} %get-tuple-element.77), channel_id=1, source_target_pairs={{0,8},{8,16},{16,24},{24,28},{28,20},{20,12},{12,4},{4,0},{1,9},{9... | collective-permute-start | bytes 608264 | tf_op jit(solution)/shard_map/ppermute | solution.py:78
  41.3 8.8 %collective-permute-start.10 = (bf16[3,88,640]{2,1,0:T(8,128)(2,1)S(1)}, bf16[3,88,640]{2,1,0:T(8,128)(2,1)S(1)}, u32[]{:S(2)}, u32[]{:S(2)}) collective-permute-start(bf16[3,88,640]{2,1,0:T(8,128)(2,1)S(1)} %get-tuple-element.74), channel_id=1, source_target_pairs={{8,0},{16,8},{24,16},{28,24},{20,28},{12,20},{4,12},{0,4},{9,1},{1... | collective-permute-start | bytes 1013768 | tf_op jit(solution)/shard_map/ppermute | solution.py:78
  45.6 9.4 %collective-permute-start.21 = (bf16[3,88,384]{2,1,0:T(8,128)(2,1)S(1)}, bf16[3,88,384]{2,1,0:T(8,128)(2,1)S(1)}, u32[]{:S(2)}, u32[]{:S(2)}) collective-permute-start(bf16[3,88,384]{2,1,0:T(8,128)(2,1)S(1)} %get-tuple-element.72), channel_id=1, source_target_pairs={{8,0},{16,8},{24,16},{28,24},{20,28},{12,20},{4,12},{0,4},{9,1},{1... | collective-permute-start | bytes 608264 | tf_op jit(solution)/shard_map/ppermute | solution.py:78
  47.2 8.8 %collective-permute-start.20 = (bf16[3,88,384]{2,1,0:T(8,128)(2,1)S(1)}, bf16[3,88,384]{2,1,0:T(8,128)(2,1)S(1)}, u32[]{:S(2)}, u32[]{:S(2)}) collective-permute-start(bf16[3,88,384]{2,1,0:T(8,128)(2,1)S(1)} %get-tuple-element.73), channel_id=1, source_target_pairs={{0,8},{8,16},{16,24},{24,28},{28,20},{20,12},{12,4},{4,0},{1,9},{9... | collective-permute-start | bytes 608264 | tf_op jit(solution)/shard_map/ppermute | solution.py:78
  52.9 8.8 %collective-permute-start.11 = (bf16[3,88,640]{2,1,0:T(8,128)(2,1)S(1)}, bf16[3,88,640]{2,1,0:T(8,128)(2,1)S(1)}, u32[]{:S(2)}, u32[]{:S(2)}) collective-permute-start(bf16[3,88,640]{2,1,0:T(8,128)(2,1)S(1)} %get-tuple-element.70), channel_id=1, source_target_pairs={{8,0},{16,8},{24,16},{28,24},{20,28},{12,20},{4,12},{0,4},{9,1},{1... | collective-permute-start | bytes 1013768 | tf_op jit(solution)/shard_map/ppermute | solution.py:78
  57.1 9.4 %collective-permute-start.23 = (bf16[3,88,384]{2,1,0:T(8,128)(2,1)S(1)}, bf16[3,88,384]{2,1,0:T(8,128)(2,1)S(1)}, u32[]{:S(2)}, u32[]{:S(2)}) collective-permute-start(bf16[3,88,384]{2,1,0:T(8,128)(2,1)S(1)} %get-tuple-element.68), channel_id=1, source_target_pairs={{8,0},{16,8},{24,16},{28,24},{20,28},{12,20},{4,12},{0,4},{9,1},{1... | collective-permute-start | bytes 608264 | tf_op jit(solution)/shard_map/ppermute | solution.py:78
  58.8 8.8 %collective-permute-start.22 = (bf16[3,88,384]{2,1,0:T(8,128)(2,1)S(1)}, bf16[3,88,384]{2,1,0:T(8,128)(2,1)S(1)}, u32[]{:S(2)}, u32[]{:S(2)}) collective-permute-start(bf16[3,88,384]{2,1,0:T(8,128)(2,1)S(1)} %get-tuple-element.69), channel_id=1, source_target_pairs={{0,8},{8,16},{16,24},{24,28},{28,20},{20,12},{12,4},{4,0},{1,9},{9... | collective-permute-start | bytes 608264 | tf_op jit(solution)/shard_map/ppermute | solution.py:78
  64.5 8.8 %collective-permute-start.12 = (bf16[3,88,640]{2,1,0:T(8,128)(2,1)S(1)}, bf16[3,88,640]{2,1,0:T(8,128)(2,1)S(1)}, u32[]{:S(2)}, u32[]{:S(2)}) collective-permute-start(bf16[3,88,640]{2,1,0:T(8,128)(2,1)S(1)} %get-tuple-element.66), channel_id=1, source_target_pairs={{8,0},{16,8},{24,16},{28,24},{20,28},{12,20},{4,12},{0,4},{9,1},{1... | collective-permute-start | bytes 1013768 | tf_op jit(solution)/shard_map/ppermute | solution.py:78
  68.7 9.4 %collective-permute-start.25 = (bf16[3,88,384]{2,1,0:T(8,128)(2,1)S(1)}, bf16[3,88,384]{2,1,0:T(8,128)(2,1)S(1)}, u32[]{:S(2)}, u32[]{:S(2)}) collective-permute-start(bf16[3,88,384]{2,1,0:T(8,128)(2,1)S(1)} %get-tuple-element.64), channel_id=1, source_target_pairs={{8,0},{16,8},{24,16},{28,24},{20,28},{12,20},{4,12},{0,4},{9,1},{1... | collective-permute-start | bytes 608264 | tf_op jit(solution)/shard_map/ppermute | solution.py:78
  70.4 8.8 %collective-permute-start.24 = (bf16[3,88,384]{2,1,0:T(8,128)(2,1)S(1)}, bf16[3,88,384]{2,1,0:T(8,128)(2,1)S(1)}, u32[]{:S(2)}, u32[]{:S(2)}) collective-permute-start(bf16[3,88,384]{2,1,0:T(8,128)(2,1)S(1)} %get-tuple-element.65), channel_id=1, source_target_pairs={{0,8},{8,16},{16,24},{24,28},{28,20},{20,12},{12,4},{4,0},{1,9},{9... | collective-permute-start | bytes 608264 | tf_op jit(solution)/shard_map/ppermute | solution.py:78
  94.5 12.1 %all-to-all-start = ((f32[32,1,128]{2,1,0:T(1,128)}), f32[32,1,128]{2,1,0:T(1,128)S(1)}, u32[]{:S(2)}, u32[]{:S(2)}) async-start(f32[32,1,128]{2,1,0:T(1,128)} %broadcast_in_dim.3), calls=%async_computation | async-start | bytes 32768 | tf_op jit(solution)/shard_map/all_to_all | solution.py:195
  111.3 10.1 %collective-permute-start.34 = (bf16[88,2048]{1,0:T(8,128)(2,1)S(1)}, bf16[88,2048]{1,0:T(8,128)(2,1)S(1)}, u32[]{:S(2)}, u32[]{:S(2)}) collective-permute-start(bf16[88,2048]{1,0:T(8,128)(2,1)S(1)} %get-tuple-element.88), channel_id=1, source_target_pairs={{20,8},{12,16},{24,4},{17,13},{9,21},{5,25},{22,10},{14,18},{26,6}... | collective-permute-start | bytes 1081352 | tf_op jit(solution)/shard_map/ppermute | solution.py:214
  111.9 28.1 %collective-permute-start.33 = (bf16[88,2048]{1,0:T(8,128)(2,1)S(1)}, bf16[88,2048]{1,0:T(8,128)(2,1)S(1)}, u32[]{:S(2)}, u32[]{:S(2)}) collective-permute-start(bf16[88,2048]{1,0:T(8,128)(2,1)S(1)} %get-tuple-element.89), channel_id=1, source_target_pairs={{16,8},{8,16},{28,4},{21,13},{13,21},{1,25},{18,10},{10,18},{30,6}... | collective-permute-start | bytes 1081352 | tf_op jit(solution)/shard_map/ppermute | solution.py:214
  112.6 29.0 %collective-permute-start.32 = (bf16[88,2048]{1,0:T(8,128)(2,1)S(1)}, bf16[88,2048]{1,0:T(8,128)(2,1)S(1)}, u32[]{:S(2)}, u32[]{:S(2)}) collective-permute-start(bf16[88,2048]{1,0:T(8,128)(2,1)S(1)} %get-tuple-element.90), channel_id=1, source_target_pairs={{28,8},{4,16},{16,4},{25,13},{1,21},{13,25},{30,10},{6,18},{18,6},... | collective-permute-start | bytes 1081352 | tf_op jit(solution)/shard_map/ppermute | solution.py:214
  113.3 28.3 %collective-permute-start.31 = (bf16[88,2048]{1,0:T(8,128)(2,1)S(1)}, bf16[88,2048]{1,0:T(8,128)(2,1)S(1)}, u32[]{:S(2)}, u32[]{:S(2)}) collective-permute-start(bf16[88,2048]{1,0:T(8,128)(2,1)S(1)} %get-tuple-element.91), channel_id=1, source_target_pairs={{24,8},{0,16},{20,4},{29,13},{5,21},{9,25},{26,10},{2,18},{22,6},{... | collective-permute-start | bytes 1081352 | tf_op jit(solution)/shard_map/ppermute | solution.py:214
  120.6 21.0 %collective-permute-start.30 = (bf16[88,2048]{1,0:T(8,128)(2,1)S(1)}, bf16[88,2048]{1,0:T(8,128)(2,1)S(1)}, u32[]{:S(2)}, u32[]{:S(2)}) collective-permute-start(bf16[88,2048]{1,0:T(8,128)(2,1)S(1)} %get-tuple-element.92), channel_id=1, source_target_pairs={{4,8},{28,16},{8,4},{1,13},{25,21},{21,25},{6,10},{30,18},{10,6},{... | collective-permute-start | bytes 1081352 | tf_op jit(solution)/shard_map/ppermute | solution.py:214
  121.3 23.7 %collective-permute-start.29 = (bf16[88,2048]{1,0:T(8,128)(2,1)S(1)}, bf16[88,2048]{1,0:T(8,128)(2,1)S(1)}, u32[]{:S(2)}, u32[]{:S(2)}) collective-permute-start(bf16[88,2048]{1,0:T(8,128)(2,1)S(1)} %get-tuple-element.93), channel_id=1, source_target_pairs={{0,8},{24,16},{12,4},{5,13},{29,21},{17,25},{2,10},{26,18},{14,6},... | collective-permute-start | bytes 1081352 | tf_op jit(solution)/shard_map/ppermute | solution.py:214
  164.9 30.1 %collective-permute-start.38 = (bf16[88,2048]{1,0:T(8,128)(2,1)S(1)}, bf16[88,2048]{1,0:T(8,128)(2,1)}, u32[]{:S(2)}, u32[]{:S(2)}) collective-permute-start(bf16[88,2048]{1,0:T(8,128)(2,1)S(1)} %get-tuple-element.41), channel_id=1, source_target_pairs={{8,24},{16,0},{4,20},{13,29},{21,5},{25,9},{10,26},{18,2},{6,22},{... | collective-permute-start | bytes 1081352 | tf_op jit(solution)/shard_map/ppermute | solution.py:220
  166.2 28.8 %collective-permute-start.39 = (bf16[88,2048]{1,0:T(8,128)(2,1)S(1)}, bf16[88,2048]{1,0:T(8,128)(2,1)}, u32[]{:S(2)}, u32[]{:S(2)}) collective-permute-start(bf16[88,2048]{1,0:T(8,128)(2,1)S(1)} %get-tuple-element.42), channel_id=1, source_target_pairs={{8,4},{16,28},{4,8},{13,1},{21,25},{25,21},{10,6},{18,30},{6,10},{... | collective-permute-start | bytes 1081352 | tf_op jit(solution)/shard_map/ppermute | solution.py:220
  167.7 28.4 %collective-permute-start.40 = (bf16[88,2048]{1,0:T(8,128)(2,1)S(1)}, bf16[88,2048]{1,0:T(8,128)(2,1)}, u32[]{:S(2)}, u32[]{:S(2)}) collective-permute-start(bf16[88,2048]{1,0:T(8,128)(2,1)S(1)} %get-tuple-element.43), channel_id=1, source_target_pairs={{8,0},{16,24},{4,12},{13,5},{21,29},{25,17},{10,2},{18,26},{6,14},... | collective-permute-start | bytes 1081352 | tf_op jit(solution)/shard_map/ppermute | solution.py:220
  169.0 27.1 %collective-permute-start.41 = (bf16[88,2048]{1,0:T(8,128)(2,1)S(1)}, bf16[88,2048]{1,0:T(8,128)(2,1)}, u32[]{:S(2)}, u32[]{:S(2)}) collective-permute-start(bf16[88,2048]{1,0:T(8,128)(2,1)S(1)} %get-tuple-element.44), channel_id=1, source_target_pairs={{8,12},{16,20},{4,0},{13,9},{21,17},{25,29},{10,14},{18,22},{6,2},... | collective-permute-start | bytes 1081352 | tf_op jit(solution)/shard_map/ppermute | solution.py:220
  (18 other events, 151.9 us)

commit v2 on v1

--- a/solution.py
+++ b/solution.py
@@ -1,3 +1,4 @@
+import functools
 import math
 
 import jax
@@ -73,17 +74,223 @@
         )
 
     acc = {(g, d): piece(g, d, 0) for g in range(len(widths)) for d in (1, -1)}
+    last = {}
     for step in range(1, ranks):
         for g in range(len(widths)):
             got = {d: lax.ppermute(acc[g, d], axis, perms[d]) for d in (1, -1)}
-            if g:
+            if g and step < ranks - 1:
                 got[1], got[-1], _, _ = lax.optimization_barrier(
                     (got[1], got[-1], acc[g - 1, 1], acc[g - 1, -1])
                 )
             for d in (1, -1):
-                total = got[d].astype(F32) + piece(g, d, step).astype(F32)
-                acc[g, d] = total.astype(BF16) if step < ranks - 1 else total
-    return [acc[g, d] for g in range(len(widths)) for d in (1, -1)]
+                if step < ranks - 1:
+                    acc[g, d] = (got[d].astype(F32) + piece(g, d, step).astype(F32)).astype(BF16)
+                else:
+                    last[g, d] = (got[d], starts[g][d])
+    return [[last[g, d] for d in (1, -1)] for g in range(len(widths))]
+
+
+VMEM = pl.BlockSpec(memory_space=pltpu.VMEM)
+HBM = pl.BlockSpec(memory_space=pltpu.HBM)
+SMALL = pltpu.CompilerParams(vmem_limit_bytes=12 * 2**20)
+
+
+def in_hbm(x):
+    return pltpu.with_memory_space_constraint(x, pltpu.HBM)
+
+
+def lane_sums(x):
+    x = jnp.sum(x, axis=0)
+    return sum(x[:, c : c + 128] for c in range(0, x.shape[1], 128))
+
+
+def add_and_square(arrived, own, before, copies, later=()):
+    count, fetch = len(arrived), isinstance(own, tuple)
+    mats, rows, _ = arrived[0].shape
+    partials, axis, columns = own if fetch else (None, None, ())
+    shapes = [x.shape for x in arrived] + [shape for shape, _ in later]
+    columns = list(columns) + [c for _, c in later]
+
+    def body(*refs):
+        refs = list(refs)
+        take = lambda n: [refs.pop(0) for _ in range(n)]
+        got, (whole,) = take(count), take(1) if fetch else (None,)
+        addends = [] if fetch else take(count)
+        start = take(1) if before is not None else None
+        outs, (squares_out,), extra = take(count), take(1), take(len(later))
+        loads = []
+        if fetch:
+            addends, sems = take(count), refs.pop(0)
+            first = pl.multiple_of(lax.axis_index(axis) * rows, 8)
+            for i, (ref, c) in enumerate(zip(addends + extra, columns)):
+                source = whole.at[:, pl.ds(first, rows), c : c + ref.shape[2]]
+                loads.append(pltpu.make_async_copy(source, ref, sems.at[i]))
+                loads[-1].start()
+        squares = start[0][...] if start else jnp.zeros((rows, 128), F32)
+        for i in range(count):
+            if fetch:
+                loads[i].wait()
+            x = got[i][...].astype(F32) + addends[i][...].astype(F32)
+            outs[i][...] = x
+            squares = squares + lane_sums(x * x)
+        for load in loads[count:]:
+            load.wait()
+        if copies:
+            squares = jnp.broadcast_to(jnp.sum(squares), squares_out.shape)
+        squares_out[...] = squares
+
+    shape = (copies, 1, 128) if copies else (rows, 128)
+    operands = list(arrived) + ([in_hbm(partials)] if fetch else list(own))
+    specs = [VMEM] * count + ([HBM] if fetch else [VMEM] * count)
+    if before is not None:
+        operands, specs = operands + [before], specs + [VMEM]
+    outs = pl.pallas_call(
+        body,
+        out_shape=[jax.ShapeDtypeStruct(x.shape, F32) for x in arrived]
+        + [jax.ShapeDtypeStruct(shape, F32)]
+        + [jax.ShapeDtypeStruct(shape, BF16) for shape, _ in later],
+        in_specs=specs,
+        out_specs=[VMEM] * (count + 1 + len(later)),
+        scratch_shapes=[pltpu.VMEM(x.shape, BF16) for x in arrived]
+        + [pltpu.SemaphoreType.DMA((len(shapes),))]
+        if fetch
+        else [],
+        compiler_params=SMALL,
+        name="add_and_square",
+    )(*operands)
+    return outs[:count], outs[count], list(outs[count + 1 :])
+
+
+def finish_sums(groups, partials, axis, copies):
+    rows = groups[0][0][0].shape[1]
+    streams, squares = [], None
+    if rows % 8 == 0:
+        first, second = [[x for x, _ in g] for g in groups], [[c for _, c in g] for g in groups]
+        later = [(x.shape, c) for x, c in groups[1]]
+        head, squares, own = add_and_square(
+            first[0], (partials, axis, second[0]), None, 0, later
+        )
+        tail, squares, _ = add_and_square(first[1], own, squares, copies)
+        return list(head) + list(tail), squares
+    for g, group in enumerate(groups):
+        own = [
+            lax.dynamic_slice(partials, (0, lax.axis_index(axis) * rows, c), x.shape)
+            for x, c in group
+        ]
+        last = copies if g == len(groups) - 1 else 0
+        summed, squares, _ = add_and_square([x for x, _ in group], own, squares, last)
+        streams += summed
+    return streams, squares
+
+
+def clip_factor(squares_ref, entries):
+    total = jnp.sum(squares_ref[...], axis=0)
+    return jnp.minimum(1.0, lax.rsqrt(total / entries + 1e-06))
+
+
+def column_tiles(streams):
+    at = 0
+    for i, s in enumerate(streams):
+        for c in range(0, s.shape[-1], 128):
+            yield i, slice(c, c + 128), slice(at + c, at + c + 128)
+        at += s.shape[-1]
+
+
+def load_rows(source, target, sems):
+    loads = [
+        pltpu.make_async_copy(source.at[m], target.at[m], sems.at[m]) for m in range(target.shape[0])
+    ]
+    for load in loads:
+        load.start()
+    return loads
+
+
+def my_owners(owners, axes):
+    odd = lax.axis_index(axes[1]) % 2 == 1
+    return lax.axis_index(axes[0]), [jnp.where(odd, b, a) for a, b in zip(*owners)]
+
+
+def direction_pieces(squares, streams, momentum, order, owners, axes, entries):
+    mats, rows, columns = momentum.shape
+    ranks = rounds = len(order)
+    count = len(streams)
+
+    def body(squares_ref, *refs):
+        ins, whole, outs = refs[:count], refs[count], refs[count + 1 : -2]
+        mom, sems = refs[-2:]
+        loads = load_rows(whole, mom, sems)
+        factor = jnp.broadcast_to(clip_factor(squares_ref, entries), (rows, 128))
+        for load in loads:
+            load.wait()
+        rank, owner = my_owners(owners, axes)
+        for step in range(rounds):
+            target = partner(rank, order[step], ranks)
+            m = functools.reduce(lambda a, b: jnp.where(owner[b] == target, b, a), range(mats), -1)
+
+            @pl.when(m >= 0)
+            def _(m=m, step=step):
+                for i, here, there in column_tiles(streams):
+                    scaled = factor * ins[i][m, :, here]
+                    new = momentum_decay * mom[m, :, there] + scaled
+                    outs[step][:, there] = (scaled + momentum_decay * new).astype(BF16)
+
+    return pl.pallas_call(
+        body,
+        out_shape=[jax.ShapeDtypeStruct((rows, columns), BF16)] * rounds,
+        in_specs=[VMEM] * (count + 1) + [HBM],
+        out_specs=[VMEM] * rounds,
+        scratch_shapes=[pltpu.VMEM(momentum.shape, F32), pltpu.SemaphoreType.DMA((mats,))],
+        compiler_params=SMALL,
+        name="direction_pieces",
+    )(squares, *streams, in_hbm(momentum))
+
+
+def momentum_step(squares, streams, momentum, entries):
+    count = len(streams)
+    mats, rows, _ = momentum.shape
+
+    def body(squares_ref, *refs):
+        ins, whole, out, mom, sems = refs[:count], *refs[count:]
+        loads = load_rows(whole, mom, sems)
+        factor = jnp.broadcast_to(clip_factor(squares_ref, entries), (rows, 128))
+        for m in range(mats):
+            loads[m].wait()
+            for i, here, there in column_tiles(streams):
+                out[m, :, there] = momentum_decay * mom[m, :, there] + factor * ins[i][m, :, here]
+
+    return pl.pallas_call(
+        body,
+        out_shape=jax.ShapeDtypeStruct(momentum.shape, F32),
+        in_specs=[VMEM] * (count + 1) + [HBM],
+        out_specs=VMEM,
+        scratch_shapes=[pltpu.VMEM(momentum.shape, F32), pltpu.SemaphoreType.DMA((mats,))],
+        compiler_params=SMALL,
+        name="momentum_step",
+    )(squares, *streams, in_hbm(momentum))
+
+
+def pick_rows(arrived, order, owners, axes):
+    rows, columns = arrived[0].shape
+    mats, ranks = len(owners[0]), len(order)
+
+    def body(*refs):
+        out = refs[-1]
+        rank, owner = my_owners(owners, axes)
+        for m in range(mats):
+            for at, step in enumerate(order):
+
+                @pl.when(partner(owner[m], step, ranks, back=True) == rank)
+                def _(m=m, at=at):
+                    out[m] = refs[at][...].astype(F32)
+
+    return pl.pallas_call(
+        body,
+        out_shape=jax.ShapeDtypeStruct((mats, rows, columns), F32),
+        in_specs=[VMEM] * len(arrived),
+        out_specs=VMEM,
+        compiler_params=SMALL,
+        name="pick_rows",
+    )(*arrived)
 
 
 def owner_ranks(mats, ranks):
@@ -110,7 +317,29 @@
     ]
 
 
-def newton_schulz_body(count, block, scale, *refs):
+def rounds_of(ranks, back):
+    if ranks != 8:
+        return list(range(ranks)), {}
+    return ([0, 1, 4, 5, 6, 7, 2, 3], {2: 1, 3: 4}) if back else ([0, 1, 4, 5, 2, 3, 6, 7], {6: 1, 7: 2})
+
+
+def exchange(pieces, axes, owners, ranks, experts, back):
+    order, after = rounds_of(ranks, back)
+    out = {0: pieces[0]}
+    for at, step in enumerate(order):
+        if step == 0:
+            continue
+        piece = pieces[at]
+        if step in after:
+            piece, _ = lax.optimization_barrier((piece, out[after[step]]))
+        pairs = owner_pairs(owners, step, ranks, experts)
+        if back:
+            pairs = [(b, a) for a, b in pairs]
+        out[step] = lax.ppermute(piece, axes, pairs)
+    return [out[step] for step in order]
+
+
+def newton_schulz_body(count, place, block, scale, *refs):
     ins, outs = refs[:count], refs[count : 2 * count]
     d, a, q, qs = refs[2 * count :]
     rows = ins[0].shape[0]
@@ -150,20 +379,20 @@
                 + jnp.dot(pb, t.astype(BF16), preferred_element_type=F32)
             )
     qs[...] = (q[...] * (inv * scale)).astype(BF16)
-    for i in range(count):
+    for i, j in enumerate(place):
         outs[i][...] = jnp.dot(
-            qs[i * rows : (i + 1) * rows, :], d[...], preferred_element_type=F32
+            qs[j * rows : (j + 1) * rows, :], d[...], preferred_element_type=F32
         ).astype(BF16)
 
 
-def newton_schulz(pieces, scale):
+def newton_schulz(pieces, place, scale):
     count = len(pieces)
     rows, columns = pieces[0].shape
     whole = count * rows
     block = whole // 2 if whole % 32 == 0 else whole
     vmem = pl.BlockSpec(memory_space=pltpu.VMEM)
     return pl.pallas_call(
-        lambda *refs: newton_schulz_body(count, block, scale, *refs),
+        lambda *refs: newton_schulz_body(count, place, block, scale, *refs),
         out_shape=[jax.ShapeDtypeStruct((rows, columns), BF16)] * count,
         in_specs=[vmem] * count,
         out_specs=[vmem] * count,
@@ -173,7 +402,7 @@
             pltpu.VMEM((whole, whole), F32),
             pltpu.VMEM((whole, whole), BF16),
         ],
-        compiler_params=pltpu.CompilerParams(vmem_limit_bytes=50 * 2**20),
+        compiler_params=pltpu.CompilerParams(vmem_limit_bytes=28 * 2**20),
         name="newton_schulz",
         cost_estimate=pl.CostEstimate(
             flops=4 * whole * whole * columns + 18 * whole**3,
@@ -187,44 +416,23 @@
     partials = grad_parts[0]
     mats, rows_whole, columns = partials.shape
     ranks, experts = lax.axis_size("dp"), lax.axis_size("expert")
-    rank, parity = lax.axis_index("dp"), lax.axis_index("expert") % 2
     both = ("dp", "expert")
 
-    streams = ring_reduce_scatter(partials, "dp")
-    square = sum(jnp.sum(s * s) for s in streams)
-    squares = lax.all_to_all(
-        jnp.full((ranks * experts, 1, 128), square), both, 0, 0, tiled=True
-    )
-    total = jnp.sum(squares[:, 0, 0])
-    factor = jnp.minimum(1.0, lax.rsqrt(total / (mats * experts * rows_whole * columns) + 1e-06))
-    summed = jnp.concatenate(streams, axis=2)
-    scaled = factor * summed
-    new_momentum = momentum_decay * momentum + scaled
-    direction = (scaled + momentum_decay * new_momentum).astype(BF16)
+    groups = ring_reduce_scatter(partials, "dp")
+    streams, square = finish_sums(groups, partials, "dp", ranks * experts)
+    squares = lax.all_to_all(square, both, 0, 0, tiled=True)
+    entries = mats * experts * rows_whole * columns
 
     owners = owner_ranks(mats, ranks)
-    owner = [jnp.where(parity == 0, owners[0][m], owners[1][m]) for m in range(mats)]
-    far_first = list(range(ranks // 2, ranks)) + list(range(1, ranks // 2))
-    pieces = [None] * ranks
-    for step in [0] + far_first:
-        target = partner(rank, step, ranks)
-        which = sum(m * (target == owner[m]).astype(jnp.int32) for m in range(mats))
-        mine = lax.dynamic_index_in_dim(direction, which, 0, keepdims=False)
-        pieces[step] = (
-            lax.ppermute(mine, both, owner_pairs(owners, step, ranks, experts)) if step else mine
-        )
-    result = newton_schulz(pieces, 0.2 * math.sqrt(max(rows_whole, columns)))
-    back = [result[0]] + [None] * (ranks - 1)
-    for step in far_first:
-        pairs = owner_pairs(owners, step, ranks, experts)
-        back[step] = lax.ppermute(result[step], both, [(b, a) for a, b in pairs])
-    update = []
-    for m in range(mats):
-        mine = back[0]
-        for step in range(1, ranks):
-            mine = jnp.where(partner(rank, step, ranks) == owner[m], back[step], mine)
-        update.append(mine.astype(F32))
-    return (new_momentum, jnp.stack(update))
+    there, _ = rounds_of(ranks, back=False)
+    here, _ = rounds_of(ranks, back=True)
+    mine = direction_pieces(squares, streams, momentum, there, owners, both, entries)
+    new_momentum = momentum_step(squares, streams, momentum, entries)
+    pieces = exchange(mine, both, owners, ranks, experts, back=False)
+    place = [there.index(step) for step in here]
+    result = newton_schulz(pieces, place, 0.2 * math.sqrt(max(rows_whole, columns)))
+    arrived = exchange(result, both, owners, ranks, experts, back=True)
+    return (new_momentum, pick_rows(arrived, here, owners, both))
 
 
 def solution(mesh):

time: 202 us -> 185 us (0.916); the launches traced: 201 us -> 182 us
  starting transfers between devices: 72.8 us -> 44.7 us
  other arithmetic: 27.9 us -> 14.4 us
  blocking collectives: 0 us -> 11.7 us
  waiting for transfers between devices: 75.4 us -> 84.6 us
  Pallas kernels: 16.5 us -> 23.3 us
  between operations: 4.47 us -> 1 us
    ppermute x14, starting transfers between devices: 37.6 us -> 14.6 us  [exchange(): out[step] = lax.ppermute(piece, axes, pairs)]
    ppermute x14, waiting for transfers between devices: 30.4 us -> 45 us  [exchange(): out[step] = lax.ppermute(piece, axes, pairs)]
    all_to_all x0 -> x1, blocking collectives: none -> 11.7 us  [local(): squares = lax.all_to_all(square, both, 0, 0, tiled=True)]
    all_to_all x1 -> x0, waiting for transfers between devices: 6.95 us -> none  [local(): lax.all_to_all(jnp.full((ranks * experts, 1, 128), square), both, 0, 0, t...]
    pallas_call x1 -> x6, Pallas kernels: 16.5 us -> 23.3 us  [the longest x1 15.1 us: newton_schulz(): pl.pallas_call(lambda *refs: newton_schulz_body(count, place, block, scal...]
    reduce_sum x3 -> x0, other arithmetic: 5.7 us -> none  [the longest x2 5.06 us: local(): square = sum((jnp.sum(s * s) for s in streams))]
    all_to_all x1 -> x0, starting transfers between devices: 5.06 us -> none  [local(): lax.all_to_all(jnp.full((ranks * experts, 1, 128), square), both, 0, 0, t...]
    another operation x4 -> x0, other arithmetic: 4.91 us -> none  [local(): return (new_momentum, jnp.stack(update))]
  transfers between devices with their start and end apart: 43 -> 42, of which waited for: 25 -> 26; matrix products, arithmetic and copies ran while one was open for 9% -> 8% of each run, Pallas kernels for 0% -> 2%
where the time goes in v2:
time: 185 us; the launch traced here: 182 us
  waiting for transfers between devices  84.6 us (46%)
  starting transfers between devices  44.7 us (24%)
  Pallas kernels  23.3 us (13%)
  other arithmetic  14.4 us (8%)
  blocking collectives  11.7 us (6%)
  local copies, waits for them, and re-layouts  2.23 us (1%)
    ppermute x14, waiting for transfers between devices, exchange(): out[step] = lax.ppermute(piece, axes, pairs)  45 us
    ppermute x28, waiting for transfers between devices, ring_reduce_scatter(): got = {d: lax.ppermute(acc[g, d], axis, perms[d]) for d in (1, -1)}  39.5 us
    ppermute x28, starting transfers between devices, ring_reduce_scatter(): got = {d: lax.ppermute(acc[g, d], axis, perms[d]) for d in (1, -1)}  30.2 us
    pallas_call x1, Pallas kernels, newton_schulz(): pl.pallas_call(lambda *refs: newton_schulz_body(count, place, block, scal...  15.1 us
    ppermute x14, starting transfers between devices, exchange(): out[step] = lax.ppermute(piece, axes, pairs)  14.6 us
    convert_element_type x12, other arithmetic, ring_reduce_scatter(): (got[d].astype(F32) + piece(g, d, step).astype(F32)).astype(BF16)  14.4 us
    all_to_all x1, blocking collectives, local(): squares = lax.all_to_all(square, both, 0, 0, tiled=True)  11.7 us
  transfers between devices with their start and end apart: 42, of which 26 were waited for; matrix products, arithmetic and copies ran while one was open for 8% of the time, Pallas kernels for 2%

profile of v2, /device:TPU:0, one launch (start us, length us, event | category | flops | bytes accessed | tf_op | source)
XLA Modules:
  0.0 181.9 jit_solution(8203112658144537561)
XLA Ops:
  1.9 3.0 %collective-permute-start.3 = (bf16[3,88,640]{2,1,0:T(8,128)(2,1)S(1)}, bf16[3,88,640]{2,1,0:T(8,128)(2,1)S(1)}, u32[]{:S(2)}, u32[]{:S(2)}) collective-permute-start(bf16[3,88,640]{2,1,0:T(8,128)(2,1)S(1)} %get-tuple-element.106), channel_id=1, source_target_pairs={{8,0},{16,8},{24,16},{28,24},{20,28},{12,20},{4,12},{0,4},{9,1},{1... | collective-permute-start | bytes 1013768 | tf_op jit(solution)/shard_map/ppermute | solution.py:80
  6.1 2.0 %collective-permute-start.1 = (bf16[3,88,384]{2,1,0:T(8,128)(2,1)S(1)}, bf16[3,88,384]{2,1,0:T(8,128)(2,1)S(1)}, u32[]{:S(2)}, u32[]{:S(2)}) collective-permute-start(bf16[3,88,384]{2,1,0:T(8,128)(2,1)S(1)} %get-tuple-element.108), channel_id=1, source_target_pairs={{8,0},{16,8},{24,16},{28,24},{20,28},{12,20},{4,12},{0,4},{9,1},{1... | collective-permute-start | bytes 608264 | tf_op jit(solution)/shard_map/ppermute | solution.py:80
  8.2 5.5 %collective-permute-done.3 = bf16[3,88,640]{2,1,0:T(8,128)(2,1)S(1)} collective-permute-done((bf16[3,88,640]{2,1,0:T(8,128)(2,1)S(1)}, bf16[3,88,640]{2,1,0:T(8,128)(2,1)S(1)}, u32[]{:S(2)}, u32[]{:S(2)}) %collective-permute-start.3) | collective-permute-done | bytes 337952 | tf_op jit(solution)/shard_map/ppermute | solution.py:80
  13.7 2.0 %collective-permute-done.2 = bf16[3,88,640]{2,1,0:T(8,128)(2,1)S(1)} collective-permute-done((bf16[3,88,640]{2,1,0:T(8,128)(2,1)S(1)}, bf16[3,88,640]{2,1,0:T(8,128)(2,1)S(1)}, u32[]{:S(2)}, u32[]{:S(2)}) %collective-permute-start.2) | collective-permute-done | bytes 337952 | tf_op jit(solution)/shard_map/ppermute | solution.py:80
  17.0 1.6 collective-permute-start.7
  20.3 1.6 collective-permute-start.5
  22.3 4.3 %collective-permute-done.7 = bf16[3,88,640]{2,1,0:T(8,128)(2,1)S(1)} collective-permute-done((bf16[3,88,640]{2,1,0:T(8,128)(2,1)S(1)}, bf16[3,88,640]{2,1,0:T(8,128)(2,1)S(1)}, u32[]{:S(2)}, u32[]{:S(2)}) %collective-permute-start.7) | collective-permute-done | bytes 337952 | tf_op jit(solution)/shard_map/ppermute | solution.py:80
  26.7 1.8 collective-permute-done.6
  36.0 2.5 %collective-permute-done.11 = bf16[3,88,640]{2,1,0:T(8,128)(2,1)S(1)} collective-permute-done((bf16[3,88,640]{2,1,0:T(8,128)(2,1)S(1)}, bf16[3,88,640]{2,1,0:T(8,128)(2,1)S(1)}, u32[]{:S(2)}, u32[]{:S(2)}) %collective-permute-start.11) | collective-permute-done | bytes 337952 | tf_op jit(solution)/shard_map/ppermute | solution.py:80
  41.3 1.6 collective-permute-start.15
  45.5 1.6 collective-permute-start.13
  47.6 2.5 %collective-permute-done.15 = bf16[3,88,640]{2,1,0:T(8,128)(2,1)S(1)} collective-permute-done((bf16[3,88,640]{2,1,0:T(8,128)(2,1)S(1)}, bf16[3,88,640]{2,1,0:T(8,128)(2,1)S(1)}, u32[]{:S(2)}, u32[]{:S(2)}) %collective-permute-start.15) | collective-permute-done | bytes 337952 | tf_op jit(solution)/shard_map/ppermute | solution.py:80
  52.9 1.6 collective-permute-start.19
  57.1 1.6 collective-permute-start.17
  59.2 2.5 %collective-permute-done.19 = bf16[3,88,640]{2,1,0:T(8,128)(2,1)S(1)} collective-permute-done((bf16[3,88,640]{2,1,0:T(8,128)(2,1)S(1)}, bf16[3,88,640]{2,1,0:T(8,128)(2,1)S(1)}, u32[]{:S(2)}, u32[]{:S(2)}) %collective-permute-start.19) | collective-permute-done | bytes 337952 | tf_op jit(solution)/shard_map/ppermute | solution.py:80
  64.5 1.6 collective-permute-start.23
  68.7 1.6 collective-permute-start.21
  70.8 2.5 %collective-permute-done.23 = bf16[3,88,640]{2,1,0:T(8,128)(2,1)S(1)} collective-permute-done((bf16[3,88,640]{2,1,0:T(8,128)(2,1)S(1)}, bf16[3,88,640]{2,1,0:T(8,128)(2,1)S(1)}, u32[]{:S(2)}, u32[]{:S(2)}) %collective-permute-start.23) | collective-permute-done | bytes 337952 | tf_op jit(solution)/shard_map/ppermute | solution.py:80
  76.1 1.7 collective-permute-start.27
  80.3 1.7 collective-permute-start.25
  82.4 2.2 %collective-permute-done.27.refs_1_ = bf16[3,88,640]{2,1,0:T(8,128)(2,1)S(1)} collective-permute-done((bf16[3,88,640]{2,1,0:T(8,128)(2,1)S(1)}, bf16[3,88,640]{2,1,0:T(8,128)(2,1)S(1)}, u32[]{:S(2)}, u32[]{:S(2)}) %collective-permute-start.27) | collective-permute-done | bytes 337952 | tf_op jit(solution)/shard_map/ppermute | solution.py:80
  88.7 11.7 %all_to_all.5.squares_ref = f32[32,1,128]{2,1,0:T(1,128)S(1)} all-to-all(f32[32,1,128]{2,1,0:T(1,128)S(1)} %get-tuple-element.57), channel_id=1, replica_groups=mesh['dp'=8,'expert'=4] {'dp','expert'}, dimensions={0} | all-to-all | bytes 32768 | tf_op jit(solution)/shard_map/all_to_all | solution.py:423
  100.3 2.1 %direction_pieces.1 = (bf16[88,2048]{1,0:T(8,128)(2,1)S(1)}, bf16[88,2048]{1,0:T(8,128)(2,1)S(1)}, bf16[88,2048]{1,0:T(8,128)(2,1)S(1)}, bf16[88,2048]{1,0:T(8,1...) custom-call(f32[32,1,128]{2,1,0:T(1,128)S(1)} %all_to_all.5.squares_, ...), custom_call_target="tpu_custom_call" | custom-call | tf_op jit(solution)/shard_map/direction_pieces/pallas_call | solution.py:237
  102.4 2.5 %collective-permute-start.28 = (bf16[88,2048]{1,0:T(8,128)(2,1)S(1)}, bf16[88,2048]{1,0:T(8,128)(2,1)S(1)}, u32[]{:S(2)}, u32[]{:S(2)}) collective-permute-start(bf16[88,2048]{1,0:T(8,128)(2,1)S(1)} %get-tuple-element.63), channel_id=1, source_target_pairs={{12,8},{20,16},{0,4},{9,13},{17,21},{29,25},{14,10},{22,18},{2,6},... | collective-permute-start | bytes 1081352 | tf_op jit(solution)/shard_map/ppermute | solution.py:338
  110.5 3.0 %collective-permute-done.31.refs_4_ = bf16[88,2048]{1,0:T(8,128)(2,1)S(1)} collective-permute-done((bf16[88,2048]{1,0:T(8,128)(2,1)S(1)}, bf16[88,2048]{1,0:T(8,128)(2,1)S(1)}, u32[]{:S(2)}, u32[]{:S(2)}) %collective-permute-start.31) | collective-permute-done | bytes 360480 | tf_op jit(solution)/shard_map/ppermute | solution.py:338
  114.4 6.9 %collective-permute-done.29.refs_2_ = bf16[88,2048]{1,0:T(8,128)(2,1)S(1)} collective-permute-done((bf16[88,2048]{1,0:T(8,128)(2,1)S(1)}, bf16[88,2048]{1,0:T(8,128)(2,1)S(1)}, u32[]{:S(2)}, u32[]{:S(2)}) %collective-permute-start.29) | collective-permute-done | bytes 360480 | tf_op jit(solution)/shard_map/ppermute | solution.py:338
  121.2 15.1 %newton_schulz.1 = (bf16[88,2048]{1,0:T(8,128)(2,1)S(1)}, bf16[88,2048]{1,0:T(8,128)(2,1)S(1)}, bf16[88,2048]{1,0:T(8,128)(2,1)S(1)}, bf16[88,2048]{1,0:T(8,128)...) custom-call(bf16[88,2048]{1,0:T(8,128)(2,1)S(1)} %get-tuple-element., ...), custom_call_target="tpu_custom_call" | custom-call | flops 10340532224 | bytes 5767168 | tf_op jit(solution)/shard_map/newton_schulz/pallas_call | solution.py:394
  141.0 12.4 %collective-permute-done.35.refs_1_ = bf16[88,2048]{1,0:T(8,128)(2,1)S(1)} collective-permute-done((bf16[88,2048]{1,0:T(8,128)(2,1)S(1)}, bf16[88,2048]{1,0:T(8,128)(2,1)S(1)}, u32[]{:S(2)}, u32[]{:S(2)}) %collective-permute-start.35) | collective-permute-done | bytes 360480 | tf_op jit(solution)/shard_map/ppermute | solution.py:338
  154.7 18.0 %collective-permute-done.36.refs_2_ = bf16[88,2048]{1,0:T(8,128)(2,1)S(1)} collective-permute-done((bf16[88,2048]{1,0:T(8,128)(2,1)S(1)}, bf16[88,2048]{1,0:T(8,128)(2,1)S(1)}, u32[]{:S(2)}, u32[]{:S(2)}) %collective-permute-start.36) | collective-permute-done | bytes 360480 | tf_op jit(solution)/shard_map/ppermute | solution.py:338
  173.4 3.0 %momentum_step.1 = f32[3,88,2048]{2,1,0:T(8,128)} custom-call(f32[32,1,128]{2,1,0:T(1,128)S(1)} %all_to_all.5.squares_ref, f32[3,88,640]{2,1,0:T(8,128)S(1)} %get-tuple-element.58.refs_0_, f32[3,88,640]{2,1,0:T(8,128)S(1)} %get-tuple-element.59.refs_1_, f32[3,88,384]{2,1,0:T(8,128)S(1)} %get-tuple-element.60.refs_2_, ...), custom_call_target="tpu_custom_call" | custom-call | tf_op jit(solution)/shard_map/momentum_step/pallas_call | solution.py:261
  176.5 3.9 %collective-permute-done.40.refs_6_ = bf16[88,2048]{1,0:T(8,128)(2,1)S(1)} collective-permute-done((bf16[88,2048]{1,0:T(8,128)(2,1)S(1)}, bf16[88,2048]{1,0:T(8,128)(2,1)S(1)}, u32[]{:S(2)}, u32[]{:S(2)}) %collective-permute-start.40) | collective-permute-done | bytes 360480 | tf_op jit(solution)/shard_map/ppermute | solution.py:338
  180.3 1.6 pick_rows.1
  (73 shorter events, 53.5 us)
Async XLA Ops:
  1.9 11.8 %collective-permute-start.3 = (bf16[3,88,640]{2,1,0:T(8,128)(2,1)S(1)}, bf16[3,88,640]{2,1,0:T(8,128)(2,1)S(1)}, u32[]{:S(2)}, u32[]{:S(2)}) collective-permute-start(bf16[3,88,640]{2,1,0:T(8,128)(2,1)S(1)} %get-tuple-element.106), channel_id=1, source_target_pairs={{8,0},{16,8},{24,16},{28,24},{20,28},{12,20},{4,12},{0,4},{9,1},{1... | collective-permute-start | bytes 1013768 | tf_op jit(solution)/shard_map/ppermute | solution.py:80
  4.9 10.9 %collective-permute-start.2 = (bf16[3,88,640]{2,1,0:T(8,128)(2,1)S(1)}, bf16[3,88,640]{2,1,0:T(8,128)(2,1)S(1)}, u32[]{:S(2)}, u32[]{:S(2)}) collective-permute-start(bf16[3,88,640]{2,1,0:T(8,128)(2,1)S(1)} %get-tuple-element.107), channel_id=1, source_target_pairs={{0,8},{8,16},{16,24},{24,28},{28,20},{20,12},{12,4},{4,0},{1,9},{9... | collective-permute-start | bytes 1013768 | tf_op jit(solution)/shard_map/ppermute | solution.py:80
  6.1 13.0 %collective-permute-start.1 = (bf16[3,88,384]{2,1,0:T(8,128)(2,1)S(1)}, bf16[3,88,384]{2,1,0:T(8,128)(2,1)S(1)}, u32[]{:S(2)}, u32[]{:S(2)}) collective-permute-start(bf16[3,88,384]{2,1,0:T(8,128)(2,1)S(1)} %get-tuple-element.108), channel_id=1, source_target_pairs={{8,0},{16,8},{24,16},{28,24},{20,28},{12,20},{4,12},{0,4},{9,1},{1... | collective-permute-start | bytes 608264 | tf_op jit(solution)/shard_map/ppermute | solution.py:80
  8.1 11.0 %collective-permute-start = (bf16[3,88,384]{2,1,0:T(8,128)(2,1)S(1)}, bf16[3,88,384]{2,1,0:T(8,128)(2,1)S(1)}, u32[]{:S(2)}, u32[]{:S(2)}) collective-permute-start(bf16[3,88,384]{2,1,0:T(8,128)(2,1)S(1)} %get-tuple-element.109), channel_id=1, source_target_pairs={{0,8},{8,16},{16,24},{24,28},{28,20},{20,12},{12,4},{4,0},{1,9},{9... | collective-permute-start | bytes 608264 | tf_op jit(solution)/shard_map/ppermute | solution.py:80
  17.0 9.6 %collective-permute-start.7 = (bf16[3,88,640]{2,1,0:T(8,128)(2,1)S(1)}, bf16[3,88,640]{2,1,0:T(8,128)(2,1)S(1)}, u32[]{:S(2)}, u32[]{:S(2)}) collective-permute-start(bf16[3,88,640]{2,1,0:T(8,128)(2,1)S(1)} %get-tuple-element.104), channel_id=1, source_target_pairs={{8,0},{16,8},{24,16},{28,24},{20,28},{12,20},{4,12},{0,4},{9,1},{1... | collective-permute-start | bytes 1013768 | tf_op jit(solution)/shard_map/ppermute | solution.py:80
  18.6 9.8 %collective-permute-start.6 = (bf16[3,88,640]{2,1,0:T(8,128)(2,1)S(1)}, bf16[3,88,640]{2,1,0:T(8,128)(2,1)S(1)}, u32[]{:S(2)}, u32[]{:S(2)}) collective-permute-start(bf16[3,88,640]{2,1,0:T(8,128)(2,1)S(1)} %get-tuple-element.105), channel_id=1, source_target_pairs={{0,8},{8,16},{16,24},{24,28},{28,20},{20,12},{12,4},{4,0},{1,9},{9... | collective-permute-start | bytes 1013768 | tf_op jit(solution)/shard_map/ppermute | solution.py:80
  20.3 11.6 %collective-permute-start.5 = (bf16[3,88,384]{2,1,0:T(8,128)(2,1)S(1)}, bf16[3,88,384]{2,1,0:T(8,128)(2,1)S(1)}, u32[]{:S(2)}, u32[]{:S(2)}) collective-permute-start(bf16[3,88,384]{2,1,0:T(8,128)(2,1)S(1)} %get-tuple-element.102), channel_id=1, source_target_pairs={{8,0},{16,8},{24,16},{28,24},{20,28},{12,20},{4,12},{0,4},{9,1},{1... | collective-permute-start | bytes 608264 | tf_op jit(solution)/shard_map/ppermute | solution.py:80
  21.9 10.9 %collective-permute-start.4 = (bf16[3,88,384]{2,1,0:T(8,128)(2,1)S(1)}, bf16[3,88,384]{2,1,0:T(8,128)(2,1)S(1)}, u32[]{:S(2)}, u32[]{:S(2)}) collective-permute-start(bf16[3,88,384]{2,1,0:T(8,128)(2,1)S(1)} %get-tuple-element.103), channel_id=1, source_target_pairs={{0,8},{8,16},{16,24},{24,28},{28,20},{20,12},{12,4},{4,0},{1,9},{9... | collective-permute-start | bytes 608264 | tf_op jit(solution)/shard_map/ppermute | solution.py:80
  29.7 8.8 %collective-permute-start.11 = (bf16[3,88,640]{2,1,0:T(8,128)(2,1)S(1)}, bf16[3,88,640]{2,1,0:T(8,128)(2,1)S(1)}, u32[]{:S(2)}, u32[]{:S(2)}) collective-permute-start(bf16[3,88,640]{2,1,0:T(8,128)(2,1)S(1)} %get-tuple-element.100), channel_id=1, source_target_pairs={{8,0},{16,8},{24,16},{28,24},{20,28},{12,20},{4,12},{0,4},{9,1},{1... | collective-permute-start | bytes 1013768 | tf_op jit(solution)/shard_map/ppermute | solution.py:80
  30.9 9.1 %collective-permute-start.10 = (bf16[3,88,640]{2,1,0:T(8,128)(2,1)S(1)}, bf16[3,88,640]{2,1,0:T(8,128)(2,1)S(1)}, u32[]{:S(2)}, u32[]{:S(2)}) collective-permute-start(bf16[3,88,640]{2,1,0:T(8,128)(2,1)S(1)} %get-tuple-element.101), channel_id=1, source_target_pairs={{0,8},{8,16},{16,24},{24,28},{28,20},{20,12},{12,4},{4,0},{1,9},{9... | collective-permute-start | bytes 1013768 | tf_op jit(solution)/shard_map/ppermute | solution.py:80
  34.0 9.4 %collective-permute-start.9 = (bf16[3,88,384]{2,1,0:T(8,128)(2,1)S(1)}, bf16[3,88,384]{2,1,0:T(8,128)(2,1)S(1)}, u32[]{:S(2)}, u32[]{:S(2)}) collective-permute-start(bf16[3,88,384]{2,1,0:T(8,128)(2,1)S(1)} %get-tuple-element.98), channel_id=1, source_target_pairs={{8,0},{16,8},{24,16},{28,24},{20,28},{12,20},{4,12},{0,4},{9,1},{1... | collective-permute-start | bytes 608264 | tf_op jit(solution)/shard_map/ppermute | solution.py:80
  34.7 9.7 %collective-permute-start.8 = (bf16[3,88,384]{2,1,0:T(8,128)(2,1)S(1)}, bf16[3,88,384]{2,1,0:T(8,128)(2,1)S(1)}, u32[]{:S(2)}, u32[]{:S(2)}) collective-permute-start(bf16[3,88,384]{2,1,0:T(8,128)(2,1)S(1)} %get-tuple-element.99), channel_id=1, source_target_pairs={{0,8},{8,16},{16,24},{24,28},{28,20},{20,12},{12,4},{4,0},{1,9},{9... | collective-permute-start | bytes 608264 | tf_op jit(solution)/shard_map/ppermute | solution.py:80
  41.3 8.8 %collective-permute-start.15 = (bf16[3,88,640]{2,1,0:T(8,128)(2,1)S(1)}, bf16[3,88,640]{2,1,0:T(8,128)(2,1)S(1)}, u32[]{:S(2)}, u32[]{:S(2)}) collective-permute-start(bf16[3,88,640]{2,1,0:T(8,128)(2,1)S(1)} %get-tuple-element.96), channel_id=1, source_target_pairs={{8,0},{16,8},{24,16},{28,24},{20,28},{12,20},{4,12},{0,4},{9,1},{1... | collective-permute-start | bytes 1013768 | tf_op jit(solution)/shard_map/ppermute | solution.py:80
  45.5 9.4 %collective-permute-start.13 = (bf16[3,88,384]{2,1,0:T(8,128)(2,1)S(1)}, bf16[3,88,384]{2,1,0:T(8,128)(2,1)S(1)}, u32[]{:S(2)}, u32[]{:S(2)}) collective-permute-start(bf16[3,88,384]{2,1,0:T(8,128)(2,1)S(1)} %get-tuple-element.94), channel_id=1, source_target_pairs={{8,0},{16,8},{24,16},{28,24},{20,28},{12,20},{4,12},{0,4},{9,1},{1... | collective-permute-start | bytes 608264 | tf_op jit(solution)/shard_map/ppermute | solution.py:80
  47.2 8.8 %collective-permute-start.12 = (bf16[3,88,384]{2,1,0:T(8,128)(2,1)S(1)}, bf16[3,88,384]{2,1,0:T(8,128)(2,1)S(1)}, u32[]{:S(2)}, u32[]{:S(2)}) collective-permute-start(bf16[3,88,384]{2,1,0:T(8,128)(2,1)S(1)} %get-tuple-element.95), channel_id=1, source_target_pairs={{0,8},{8,16},{16,24},{24,28},{28,20},{20,12},{12,4},{4,0},{1,9},{9... | collective-permute-start | bytes 608264 | tf_op jit(solution)/shard_map/ppermute | solution.py:80
  52.9 8.8 %collective-permute-start.19 = (bf16[3,88,640]{2,1,0:T(8,128)(2,1)S(1)}, bf16[3,88,640]{2,1,0:T(8,128)(2,1)S(1)}, u32[]{:S(2)}, u32[]{:S(2)}) collective-permute-start(bf16[3,88,640]{2,1,0:T(8,128)(2,1)S(1)} %get-tuple-element.92), channel_id=1, source_target_pairs={{8,0},{16,8},{24,16},{28,24},{20,28},{12,20},{4,12},{0,4},{9,1},{1... | collective-permute-start | bytes 1013768 | tf_op jit(solution)/shard_map/ppermute | solution.py:80
  57.1 9.4 %collective-permute-start.17 = (bf16[3,88,384]{2,1,0:T(8,128)(2,1)S(1)}, bf16[3,88,384]{2,1,0:T(8,128)(2,1)S(1)}, u32[]{:S(2)}, u32[]{:S(2)}) collective-permute-start(bf16[3,88,384]{2,1,0:T(8,128)(2,1)S(1)} %get-tuple-element.90), channel_id=1, source_target_pairs={{8,0},{16,8},{24,16},{28,24},{20,28},{12,20},{4,12},{0,4},{9,1},{1... | collective-permute-start | bytes 608264 | tf_op jit(solution)/shard_map/ppermute | solution.py:80
  58.8 8.8 %collective-permute-start.16 = (bf16[3,88,384]{2,1,0:T(8,128)(2,1)S(1)}, bf16[3,88,384]{2,1,0:T(8,128)(2,1)S(1)}, u32[]{:S(2)}, u32[]{:S(2)}) collective-permute-start(bf16[3,88,384]{2,1,0:T(8,128)(2,1)S(1)} %get-tuple-element.91), channel_id=1, source_target_pairs={{0,8},{8,16},{16,24},{24,28},{28,20},{20,12},{12,4},{4,0},{1,9},{9... | collective-permute-start | bytes 608264 | tf_op jit(solution)/shard_map/ppermute | solution.py:80
  64.5 8.8 %collective-permute-start.23 = (bf16[3,88,640]{2,1,0:T(8,128)(2,1)S(1)}, bf16[3,88,640]{2,1,0:T(8,128)(2,1)S(1)}, u32[]{:S(2)}, u32[]{:S(2)}) collective-permute-start(bf16[3,88,640]{2,1,0:T(8,128)(2,1)S(1)} %get-tuple-element.88), channel_id=1, source_target_pairs={{8,0},{16,8},{24,16},{28,24},{20,28},{12,20},{4,12},{0,4},{9,1},{1... | collective-permute-start | bytes 1013768 | tf_op jit(solution)/shard_map/ppermute | solution.py:80
  66.1 8.7 %collective-permute-start.22 = (bf16[3,88,640]{2,1,0:T(8,128)(2,1)S(1)}, bf16[3,88,640]{2,1,0:T(8,128)(2,1)S(1)}, u32[]{:S(2)}, u32[]{:S(2)}) collective-permute-start(bf16[3,88,640]{2,1,0:T(8,128)(2,1)S(1)} %get-tuple-element.89), channel_id=1, source_target_pairs={{0,8},{8,16},{16,24},{24,28},{28,20},{20,12},{12,4},{4,0},{1,9},{9... | collective-permute-start | bytes 1013768 | tf_op jit(solution)/shard_map/ppermute | solution.py:80
  68.7 9.4 %collective-permute-start.21 = (bf16[3,88,384]{2,1,0:T(8,128)(2,1)S(1)}, bf16[3,88,384]{2,1,0:T(8,128)(2,1)S(1)}, u32[]{:S(2)}, u32[]{:S(2)}) collective-permute-start(bf16[3,88,384]{2,1,0:T(8,128)(2,1)S(1)} %get-tuple-element.86), channel_id=1, source_target_pairs={{8,0},{16,8},{24,16},{28,24},{20,28},{12,20},{4,12},{0,4},{9,1},{1... | collective-permute-start | bytes 608264 | tf_op jit(solution)/shard_map/ppermute | solution.py:80
  70.4 8.8 %collective-permute-start.20 = (bf16[3,88,384]{2,1,0:T(8,128)(2,1)S(1)}, bf16[3,88,384]{2,1,0:T(8,128)(2,1)S(1)}, u32[]{:S(2)}, u32[]{:S(2)}) collective-permute-start(bf16[3,88,384]{2,1,0:T(8,128)(2,1)S(1)} %get-tuple-element.87), channel_id=1, source_target_pairs={{0,8},{8,16},{16,24},{24,28},{28,20},{20,12},{12,4},{4,0},{1,9},{9... | collective-permute-start | bytes 608264 | tf_op jit(solution)/shard_map/ppermute | solution.py:80
  106.2 15.0 %collective-permute-start.29 = (bf16[88,2048]{1,0:T(8,128)(2,1)S(1)}, bf16[88,2048]{1,0:T(8,128)(2,1)S(1)}, u32[]{:S(2)}, u32[]{:S(2)}) collective-permute-start(bf16[88,2048]{1,0:T(8,128)(2,1)S(1)} %get-tuple-element.64), channel_id=1, source_target_pairs={{24,8},{0,16},{20,4},{29,13},{5,21},{9,25},{26,10},{2,18},{22,6},{... | collective-permute-start | bytes 1081352 | tf_op jit(solution)/shard_map/ppermute | solution.py:338
  107.6 13.7 %collective-permute-start.30 = (bf16[88,2048]{1,0:T(8,128)(2,1)S(1)}, bf16[88,2048]{1,0:T(8,128)(2,1)S(1)}, u32[]{:S(2)}, u32[]{:S(2)}) collective-permute-start(bf16[88,2048]{1,0:T(8,128)(2,1)S(1)} %get-tuple-element.65), channel_id=1, source_target_pairs={{28,8},{4,16},{16,4},{25,13},{1,21},{13,25},{30,10},{6,18},{18,6},... | collective-permute-start | bytes 1081352 | tf_op jit(solution)/shard_map/ppermute | solution.py:338
  108.3 13.0 %collective-permute-start.32 = (bf16[88,2048]{1,0:T(8,128)(2,1)S(1)}, bf16[88,2048]{1,0:T(8,128)(2,1)S(1)}, u32[]{:S(2)}, u32[]{:S(2)}) collective-permute-start(bf16[88,2048]{1,0:T(8,128)(2,1)S(1)} %get-tuple-element.67), channel_id=1, source_target_pairs={{4,8},{28,16},{8,4},{1,13},{25,21},{21,25},{6,10},{30,18},{10,6},{... | collective-permute-start | bytes 1081352 | tf_op jit(solution)/shard_map/ppermute | solution.py:338
  109.8 11.4 %collective-permute-start.33 = (bf16[88,2048]{1,0:T(8,128)(2,1)S(1)}, bf16[88,2048]{1,0:T(8,128)(2,1)S(1)}, u32[]{:S(2)}, u32[]{:S(2)}) collective-permute-start(bf16[88,2048]{1,0:T(8,128)(2,1)S(1)} %get-tuple-element.69), channel_id=1, source_target_pairs={{16,8},{8,16},{28,4},{21,13},{13,21},{1,25},{18,10},{10,18},{30,6}... | collective-permute-start | bytes 1081352 | tf_op jit(solution)/shard_map/ppermute | solution.py:338
  136.4 17.0 %collective-permute-start.35 = (bf16[88,2048]{1,0:T(8,128)(2,1)S(1)}, bf16[88,2048]{1,0:T(8,128)(2,1)S(1)}, u32[]{:S(2)}, u32[]{:S(2)}) collective-permute-start(bf16[88,2048]{1,0:T(8,128)(2,1)S(1)} %get-tuple-element.73), channel_id=1, source_target_pairs={{8,12},{16,20},{4,0},{13,9},{21,17},{25,29},{10,14},{18,22},{6,2},... | collective-permute-start | bytes 1081352 | tf_op jit(solution)/shard_map/ppermute | solution.py:338
  137.7 35.1 %collective-permute-start.36 = (bf16[88,2048]{1,0:T(8,128)(2,1)S(1)}, bf16[88,2048]{1,0:T(8,128)(2,1)S(1)}, u32[]{:S(2)}, u32[]{:S(2)}) collective-permute-start(bf16[88,2048]{1,0:T(8,128)(2,1)S(1)} %get-tuple-element.74), channel_id=1, source_target_pairs={{8,24},{16,0},{4,20},{13,29},{21,5},{25,9},{10,26},{18,2},{6,22},{... | collective-permute-start | bytes 1081352 | tf_op jit(solution)/shard_map/ppermute | solution.py:338
  139.0 37.5 %collective-permute-start.37 = (bf16[88,2048]{1,0:T(8,128)(2,1)S(1)}, bf16[88,2048]{1,0:T(8,128)(2,1)S(1)}, u32[]{:S(2)}, u32[]{:S(2)}) collective-permute-start(bf16[88,2048]{1,0:T(8,128)(2,1)S(1)} %get-tuple-element.75), channel_id=1, source_target_pairs={{8,28},{16,4},{4,16},{13,25},{21,1},{25,13},{10,30},{18,6},{6,18},... | collective-permute-start | bytes 1081352 | tf_op jit(solution)/shard_map/ppermute | solution.py:338
  139.6 36.8 %collective-permute-start.38 = (bf16[88,2048]{1,0:T(8,128)(2,1)S(1)}, bf16[88,2048]{1,0:T(8,128)(2,1)S(1)}, u32[]{:S(2)}, u32[]{:S(2)}) collective-permute-start(bf16[88,2048]{1,0:T(8,128)(2,1)S(1)} %get-tuple-element.76), channel_id=1, source_target_pairs={{8,16},{16,8},{4,28},{13,21},{21,13},{25,1},{10,18},{18,10},{6,30}... | collective-permute-start | bytes 1081352 | tf_op jit(solution)/shard_map/ppermute | solution.py:338
  140.3 36.1 %collective-permute-start.39 = (bf16[88,2048]{1,0:T(8,128)(2,1)S(1)}, bf16[88,2048]{1,0:T(8,128)(2,1)S(1)}, u32[]{:S(2)}, u32[]{:S(2)}) collective-permute-start(bf16[88,2048]{1,0:T(8,128)(2,1)S(1)} %get-tuple-element.77), channel_id=1, source_target_pairs={{8,20},{16,12},{4,24},{13,17},{21,9},{25,5},{10,22},{18,14},{6,26}... | collective-permute-start | bytes 1081352 | tf_op jit(solution)/shard_map/ppermute | solution.py:338
  153.4 27.0 %collective-permute-start.40 = (bf16[88,2048]{1,0:T(8,128)(2,1)S(1)}, bf16[88,2048]{1,0:T(8,128)(2,1)S(1)}, u32[]{:S(2)}, u32[]{:S(2)}) collective-permute-start(bf16[88,2048]{1,0:T(8,128)(2,1)S(1)} %get-tuple-element.79), channel_id=1, source_target_pairs={{8,0},{16,24},{4,12},{13,5},{21,29},{25,17},{10,2},{18,26},{6,14},... | collective-permute-start | bytes 1081352 | tf_op jit(solution)/shard_map/ppermute | solution.py:338
  (10 other events, 78.8 us)

commit v3 on v2

--- a/solution.py
+++ b/solution.py
@@ -281,7 +281,7 @@
 
                 @pl.when(partner(owner[m], step, ranks, back=True) == rank)
                 def _(m=m, at=at):
-                    out[m] = refs[at][...].astype(F32)
+                    out[m] = refs[at][:rows, :].astype(F32)
 
     return pl.pallas_call(
         body,
@@ -303,6 +303,10 @@
     )
 
 
+def relayed(mats, ranks):
+    return ((1, 4), (3, 6)) if mats == 3 and ranks == 8 else ((), ())
+
+
 def partner(rank, step, ranks, back=False):
     if ranks & (ranks - 1) == 0:
         return rank ^ step
@@ -320,40 +324,68 @@
 def rounds_of(ranks, back):
     if ranks != 8:
         return list(range(ranks)), {}
-    return ([0, 1, 4, 5, 6, 7, 2, 3], {2: 1, 3: 4}) if back else ([0, 1, 4, 5, 2, 3, 6, 7], {6: 1, 7: 2})
-
-
-def exchange(pieces, axes, owners, ranks, experts, back):
+    return ([0, 1, 4, 5, 6, 7, 2, 3], {2: (1,), 3: (1,)}) if back else ([0, 1, 4, 5, 6, 7, 2, 3], {6: (1,), 7: (1,)})
+
+
+def exchange(pieces, axes, owners, ranks, experts, relays=None):
+    back = relays is not None
     order, after = rounds_of(ranks, back)
+    by_way = back and any(relays)
     out = {0: pieces[0]}
     for at, step in enumerate(order):
         if step == 0:
             continue
         piece = pieces[at]
-        if step in after:
-            piece, _ = lax.optimization_barrier((piece, out[after[step]]))
         pairs = owner_pairs(owners, step, ranks, experts)
         if back:
             pairs = [(b, a) for a, b in pairs]
+        if by_way and step == ranks - 1:
+            hops = {o * experts + e: (o ^ 1) * experts + e for e in range(experts) for o in relays[e % 2]}
+            pairs = [(hops.get(a, a), b) for a, b in pairs]
+            piece = relay_rows(out[1], piece, relays, axes)
+        if step in after:
+            piece, *_ = lax.optimization_barrier((piece, *[out[x] for x in after[step]]))
         out[step] = lax.ppermute(piece, axes, pairs)
     return [out[step] for step in order]
 
 
-def newton_schulz_body(count, place, block, scale, *refs):
+def relay_rows(passing, mine, relays, axes):
+    rows = mine.shape[0]
+
+    def body(passing_ref, mine_ref, out_ref):
+        rank, odd = lax.axis_index(axes[0]), lax.axis_index(axes[1]) % 2 == 1
+        passes = functools.reduce(
+            jnp.logical_or,
+            [rank == jnp.where(odd, b ^ 1, a ^ 1) for a, b in zip(*relays)],
+        )
+
+        @pl.when(passes)
+        def _():
+            out_ref[...] = passing_ref[rows:, :]
+
+        @pl.when(jnp.logical_not(passes))
+        def _():
+            out_ref[...] = mine_ref[...]
+
+    return pl.pallas_call(
+        body,
+        out_shape=jax.ShapeDtypeStruct(mine.shape, mine.dtype),
+        in_specs=[VMEM] * 2,
+        out_specs=VMEM,
+        compiler_params=SMALL,
+        name="relay_rows",
+    )(passing, mine)
+
+
+def newton_schulz_body(count, place, scale, *refs):
     ins, outs = refs[:count], refs[count : 2 * count]
     d, a, q, qs = refs[2 * count :]
     rows = ins[0].shape[0]
-    whole = d.shape[0]
+    whole, columns = d.shape
     for i in range(count):
         d[i * rows : (i + 1) * rows, :] = ins[i][...]
 
-    @pl.loop(0, whole // block)
-    def _(i):
-        r = pl.ds(pl.multiple_of(i * block, 16), block)
-        a[r, :] = lax.dot_general(
-            d[r, :], d[...], (((1,), (1,)), ((), ())), preferred_element_type=F32
-        )
-
+    a[...] = lax.dot_general(d[...], d[...], (((1,), (1,)), ((), ())), preferred_element_type=F32)
     gram = a[...]
     diagonal = lax.broadcasted_iota(jnp.int32, gram.shape, 0) == lax.broadcasted_iota(
         jnp.int32, gram.shape, 1
@@ -379,21 +411,24 @@
                 + jnp.dot(pb, t.astype(BF16), preferred_element_type=F32)
             )
     qs[...] = (q[...] * (inv * scale)).astype(BF16)
-    for i, j in enumerate(place):
-        outs[i][...] = jnp.dot(
-            qs[j * rows : (j + 1) * rows, :], d[...], preferred_element_type=F32
-        ).astype(BF16)
+    width = next(w for w in (512, 256, 128, columns) if columns % w == 0)
+    for c in range(0, columns, width):
+        x = jnp.dot(qs[...], d[:, c : c + width], preferred_element_type=F32)
+        for out, parts in zip(outs, place):
+            for i, j in enumerate(parts):
+                out[i * rows : (i + 1) * rows, c : c + width] = x[
+                    j * rows : (j + 1) * rows, :
+                ].astype(BF16)
 
 
 def newton_schulz(pieces, place, scale):
     count = len(pieces)
     rows, columns = pieces[0].shape
     whole = count * rows
-    block = whole // 2 if whole % 32 == 0 else whole
     vmem = pl.BlockSpec(memory_space=pltpu.VMEM)
     return pl.pallas_call(
-        lambda *refs: newton_schulz_body(count, place, block, scale, *refs),
-        out_shape=[jax.ShapeDtypeStruct((rows, columns), BF16)] * count,
+        lambda *refs: newton_schulz_body(count, place, scale, *refs),
+        out_shape=[jax.ShapeDtypeStruct((len(p) * rows, columns), BF16) for p in place],
         in_specs=[vmem] * count,
         out_specs=[vmem] * count,
         scratch_shapes=[
@@ -428,10 +463,13 @@
     here, _ = rounds_of(ranks, back=True)
     mine = direction_pieces(squares, streams, momentum, there, owners, both, entries)
     new_momentum = momentum_step(squares, streams, momentum, entries)
-    pieces = exchange(mine, both, owners, ranks, experts, back=False)
-    place = [there.index(step) for step in here]
+    pieces = exchange(mine, both, owners, ranks, experts)
+    relays = relayed(mats, ranks)
+    place = [[there.index(step)] for step in here]
+    if any(relays):
+        place[here.index(1)] += place[here.index(ranks - 1)]
     result = newton_schulz(pieces, place, 0.2 * math.sqrt(max(rows_whole, columns)))
-    arrived = exchange(result, both, owners, ranks, experts, back=True)
+    arrived = exchange(result, both, owners, ranks, experts, relays)
     return (new_momentum, pick_rows(arrived, here, owners, both))
 
 

time: 185 us -> 180 us (0.973)
  waiting for transfers between devices: 84.6 us -> 78.1 us
    ppermute x14, waiting for transfers between devices: 45 us -> 38.6 us  [exchange(): out[step] = lax.ppermute(piece, axes, pairs)]
    pallas_call x1 -> x2, Pallas kernels: 15.1 us -> 14.9 us  [the longest x1 14.9 us: newton_schulz(): pl.pallas_call(lambda *refs: newton_schulz_body(count, place, scale, *ref...]
  transfers between devices with their start and end apart: 42 -> 42, of which waited for: 26 -> 25; matrix products, arithmetic and copies ran while one was open for 8% -> 9% of each run, Pallas kernels for 2% -> 2%
where the time goes in v3:
time: 180 us; the launch traced here: 176 us
  waiting for transfers between devices  78.1 us (43%)
  starting transfers between devices  46 us (26%)
  Pallas kernels  23.1 us (13%)
  other arithmetic  14.4 us (8%)
  blocking collectives  11.7 us (6%)
  local copies, waits for them, and re-layouts  2.23 us (1%)
    ppermute x28, waiting for transfers between devices, ring_reduce_scatter(): got = {d: lax.ppermute(acc[g, d], axis, perms[d]) for d in (1, -1)}  39.5 us
    ppermute x14, waiting for transfers between devices, exchange(): out[step] = lax.ppermute(piece, axes, pairs)  38.6 us
    ppermute x28, starting transfers between devices, ring_reduce_scatter(): got = {d: lax.ppermute(acc[g, d], axis, perms[d]) for d in (1, -1)}  30.2 us
    ppermute x14, starting transfers between devices, exchange(): out[step] = lax.ppermute(piece, axes, pairs)  15.8 us
    pallas_call x1, Pallas kernels, newton_schulz(): pl.pallas_call(lambda *refs: newton_schulz_body(count, place, scale, *ref...  14.9 us
    convert_element_type x12, other arithmetic, ring_reduce_scatter(): (got[d].astype(F32) + piece(g, d, step).astype(F32)).astype(BF16)  14.4 us
    all_to_all x1, blocking collectives, local(): squares = lax.all_to_all(square, both, 0, 0, tiled=True)  11.7 us
  transfers between devices with their start and end apart: 42, of which 25 were waited for; matrix products, arithmetic and copies ran while one was open for 9% of the time, Pallas kernels for 2%

profile of v3, /device:TPU:0, one launch (start us, length us, event | category | flops | bytes accessed | tf_op | source)
XLA Modules:
  0.0 176.5 jit_solution(15374031970825329989)
XLA Ops:
  1.9 3.0 %collective-permute-start.3 = (bf16[3,88,640]{2,1,0:T(8,128)(2,1)S(1)}, bf16[3,88,640]{2,1,0:T(8,128)(2,1)S(1)}, u32[]{:S(2)}, u32[]{:S(2)}) collective-permute-start(bf16[3,88,640]{2,1,0:T(8,128)(2,1)S(1)} %get-tuple-element.106), channel_id=1, source_target_pairs={{8,0},{16,8},{24,16},{28,24},{20,28},{12,20},{4,12},{0,4},{9,1},{1... | collective-permute-start | bytes 1013768 | tf_op jit(solution)/shard_map/ppermute | solution.py:80
  6.1 2.0 %collective-permute-start.1 = (bf16[3,88,384]{2,1,0:T(8,128)(2,1)S(1)}, bf16[3,88,384]{2,1,0:T(8,128)(2,1)S(1)}, u32[]{:S(2)}, u32[]{:S(2)}) collective-permute-start(bf16[3,88,384]{2,1,0:T(8,128)(2,1)S(1)} %get-tuple-element.108), channel_id=1, source_target_pairs={{8,0},{16,8},{24,16},{28,24},{20,28},{12,20},{4,12},{0,4},{9,1},{1... | collective-permute-start | bytes 608264 | tf_op jit(solution)/shard_map/ppermute | solution.py:80
  8.2 5.5 %collective-permute-done.3 = bf16[3,88,640]{2,1,0:T(8,128)(2,1)S(1)} collective-permute-done((bf16[3,88,640]{2,1,0:T(8,128)(2,1)S(1)}, bf16[3,88,640]{2,1,0:T(8,128)(2,1)S(1)}, u32[]{:S(2)}, u32[]{:S(2)}) %collective-permute-start.3) | collective-permute-done | bytes 337952 | tf_op jit(solution)/shard_map/ppermute | solution.py:80
  13.7 2.0 %collective-permute-done.2 = bf16[3,88,640]{2,1,0:T(8,128)(2,1)S(1)} collective-permute-done((bf16[3,88,640]{2,1,0:T(8,128)(2,1)S(1)}, bf16[3,88,640]{2,1,0:T(8,128)(2,1)S(1)}, u32[]{:S(2)}, u32[]{:S(2)}) %collective-permute-start.2) | collective-permute-done | bytes 337952 | tf_op jit(solution)/shard_map/ppermute | solution.py:80
  17.0 1.6 collective-permute-start.7
  20.3 1.6 collective-permute-start.5
  22.3 4.3 %collective-permute-done.7 = bf16[3,88,640]{2,1,0:T(8,128)(2,1)S(1)} collective-permute-done((bf16[3,88,640]{2,1,0:T(8,128)(2,1)S(1)}, bf16[3,88,640]{2,1,0:T(8,128)(2,1)S(1)}, u32[]{:S(2)}, u32[]{:S(2)}) %collective-permute-start.7) | collective-permute-done | bytes 337952 | tf_op jit(solution)/shard_map/ppermute | solution.py:80
  26.7 1.8 %collective-permute-done.6 = bf16[3,88,640]{2,1,0:T(8,128)(2,1)S(1)} collective-permute-done((bf16[3,88,640]{2,1,0:T(8,128)(2,1)S(1)}, bf16[3,88,640]{2,1,0:T(8,128)(2,1)S(1)}, u32[]{:S(2)}, u32[]{:S(2)}) %collective-permute-start.6) | collective-permute-done | bytes 337952 | tf_op jit(solution)/shard_map/ppermute | solution.py:80
  36.0 2.5 %collective-permute-done.11 = bf16[3,88,640]{2,1,0:T(8,128)(2,1)S(1)} collective-permute-done((bf16[3,88,640]{2,1,0:T(8,128)(2,1)S(1)}, bf16[3,88,640]{2,1,0:T(8,128)(2,1)S(1)}, u32[]{:S(2)}, u32[]{:S(2)}) %collective-permute-start.11) | collective-permute-done | bytes 337952 | tf_op jit(solution)/shard_map/ppermute | solution.py:80
  41.3 1.6 collective-permute-start.15
  45.5 1.6 collective-permute-start.13
  47.6 2.5 %collective-permute-done.15 = bf16[3,88,640]{2,1,0:T(8,128)(2,1)S(1)} collective-permute-done((bf16[3,88,640]{2,1,0:T(8,128)(2,1)S(1)}, bf16[3,88,640]{2,1,0:T(8,128)(2,1)S(1)}, u32[]{:S(2)}, u32[]{:S(2)}) %collective-permute-start.15) | collective-permute-done | bytes 337952 | tf_op jit(solution)/shard_map/ppermute | solution.py:80
  52.9 1.6 collective-permute-start.19
  57.1 1.6 collective-permute-start.17
  59.2 2.5 %collective-permute-done.19 = bf16[3,88,640]{2,1,0:T(8,128)(2,1)S(1)} collective-permute-done((bf16[3,88,640]{2,1,0:T(8,128)(2,1)S(1)}, bf16[3,88,640]{2,1,0:T(8,128)(2,1)S(1)}, u32[]{:S(2)}, u32[]{:S(2)}) %collective-permute-start.19) | collective-permute-done | bytes 337952 | tf_op jit(solution)/shard_map/ppermute | solution.py:80
  64.5 1.6 collective-permute-start.23
  68.7 1.6 collective-permute-start.21
  70.8 2.5 %collective-permute-done.23 = bf16[3,88,640]{2,1,0:T(8,128)(2,1)S(1)} collective-permute-done((bf16[3,88,640]{2,1,0:T(8,128)(2,1)S(1)}, bf16[3,88,640]{2,1,0:T(8,128)(2,1)S(1)}, u32[]{:S(2)}, u32[]{:S(2)}) %collective-permute-start.23) | collective-permute-done | bytes 337952 | tf_op jit(solution)/shard_map/ppermute | solution.py:80
  76.1 1.7 collective-permute-start.27
  80.3 1.7 collective-permute-start.25
  82.4 2.2 %collective-permute-done.27.refs_1_ = bf16[3,88,640]{2,1,0:T(8,128)(2,1)S(1)} collective-permute-done((bf16[3,88,640]{2,1,0:T(8,128)(2,1)S(1)}, bf16[3,88,640]{2,1,0:T(8,128)(2,1)S(1)}, u32[]{:S(2)}, u32[]{:S(2)}) %collective-permute-start.27) | collective-permute-done | bytes 337952 | tf_op jit(solution)/shard_map/ppermute | solution.py:80
  88.7 11.7 %all_to_all.5.squares_ref = f32[32,1,128]{2,1,0:T(1,128)S(1)} all-to-all(f32[32,1,128]{2,1,0:T(1,128)S(1)} %get-tuple-element.57), channel_id=1, replica_groups=mesh['dp'=8,'expert'=4] {'dp','expert'}, dimensions={0} | all-to-all | bytes 32768 | tf_op jit(solution)/shard_map/all_to_all | solution.py:458
  100.3 2.1 %direction_pieces.1 = (bf16[88,2048]{1,0:T(8,128)(2,1)S(1)}, bf16[88,2048]{1,0:T(8,128)(2,1)S(1)}, bf16[88,2048]{1,0:T(8,128)(2,1)S(1)}, bf16[88,2048]{1,0:T(8,1...) custom-call(f32[32,1,128]{2,1,0:T(1,128)S(1)} %all_to_all.5.squares_, ...), custom_call_target="tpu_custom_call" | custom-call | tf_op jit(solution)/shard_map/direction_pieces/pallas_call | solution.py:237
  102.4 2.5 %collective-permute-start.28 = (bf16[88,2048]{1,0:T(8,128)(2,1)S(1)}, bf16[88,2048]{1,0:T(8,128)(2,1)S(1)}, u32[]{:S(2)}, u32[]{:S(2)}) collective-permute-start(bf16[88,2048]{1,0:T(8,128)(2,1)S(1)} %get-tuple-element.63), channel_id=1, source_target_pairs={{12,8},{20,16},{0,4},{9,13},{17,21},{29,25},{14,10},{22,18},{2,6},... | collective-permute-start | bytes 1081352 | tf_op jit(solution)/shard_map/ppermute | solution.py:348
  107.0 1.9 %collective-permute-start.33 = (bf16[88,2048]{1,0:T(8,128)(2,1)S(1)}, bf16[88,2048]{1,0:T(8,128)(2,1)S(1)}, u32[]{:S(2)}, u32[]{:S(2)}) collective-permute-start(bf16[88,2048]{1,0:T(8,128)(2,1)S(1)} %get-tuple-element.70), channel_id=1, source_target_pairs={{0,8},{24,16},{12,4},{5,13},{29,21},{17,25},{2,10},{26,18},{14,6},... | collective-permute-start | bytes 1081352 | tf_op jit(solution)/shard_map/ppermute | solution.py:348
  110.5 4.4 %collective-permute-done.29.refs_2_ = bf16[88,2048]{1,0:T(8,128)(2,1)S(1)} collective-permute-done((bf16[88,2048]{1,0:T(8,128)(2,1)S(1)}, bf16[88,2048]{1,0:T(8,128)(2,1)S(1)}, u32[]{:S(2)}, u32[]{:S(2)}) %collective-permute-start.29) | collective-permute-done | bytes 360480 | tf_op jit(solution)/shard_map/ppermute | solution.py:348
  115.8 6.9 %collective-permute-done.33.refs_6_ = bf16[88,2048]{1,0:T(8,128)(2,1)S(1)} collective-permute-done((bf16[88,2048]{1,0:T(8,128)(2,1)S(1)}, bf16[88,2048]{1,0:T(8,128)(2,1)S(1)}, u32[]{:S(2)}, u32[]{:S(2)}) %collective-permute-start.33) | collective-permute-done | bytes 360480 | tf_op jit(solution)/shard_map/ppermute | solution.py:348
  122.7 14.9 %newton_schulz.1 = (bf16[88,2048]{1,0:T(8,128)(2,1)S(1)}, bf16[176,2048]{1,0:T(8,128)(2,1)S(1)}, bf16[88,2048]{1,0:T(8,128)(2,1)S(1)}, bf16[88,2048]{1,0:T(8,128...) custom-call(bf16[88,2048]{1,0:T(8,128)(2,1)S(1)} %get-tuple-element., ...), custom_call_target="tpu_custom_call" | custom-call | flops 10340532224 | bytes 5767168 | tf_op jit(solution)/shard_map/newton_schulz/pallas_call | solution.py:429
  141.5 24.0 %collective-permute-done.35.passing_ref.refs_1_ = bf16[176,2048]{1,0:T(8,128)(2,1)S(1)} collective-permute-done((bf16[176,2048]{1,0:T(8,128)(2,1)S(1)}, bf16[176,2048]{1,0:T(8,128)(2,1)S(1)}, u32[]{:S(2)}, u32[]{:S(2)}) %collective-permute-start.35) | collective-permute-done | bytes 720928 | tf_op jit(solution)/shard_map/ppermute | solution.py:348
  168.9 3.0 %momentum_step.1 = f32[3,88,2048]{2,1,0:T(8,128)} custom-call(f32[32,1,128]{2,1,0:T(1,128)S(1)} %all_to_all.5.squares_ref, f32[3,88,640]{2,1,0:T(8,128)S(1)} %get-tuple-element.58.refs_0_, f32[3,88,640]{2,1,0:T(8,128)S(1)} %get-tuple-element.59.refs_1_, f32[3,88,384]{2,1,0:T(8,128)S(1)} %get-tuple-element.60.refs_2_, ...), custom_call_target="tpu_custom_call" | custom-call | tf_op jit(solution)/shard_map/momentum_step/pallas_call | solution.py:261
  171.9 3.0 %collective-permute-done.40.refs_6_ = bf16[88,2048]{1,0:T(8,128)(2,1)S(1)} collective-permute-done((bf16[88,2048]{1,0:T(8,128)(2,1)S(1)}, bf16[88,2048]{1,0:T(8,128)(2,1)S(1)}, u32[]{:S(2)}, u32[]{:S(2)}) %collective-permute-start.40) | collective-permute-done | bytes 360480 | tf_op jit(solution)/shard_map/ppermute | solution.py:348
  174.9 1.6 pick_rows.1
  (74 shorter events, 52.3 us)
Async XLA Ops:
  1.9 11.8 %collective-permute-start.3 = (bf16[3,88,640]{2,1,0:T(8,128)(2,1)S(1)}, bf16[3,88,640]{2,1,0:T(8,128)(2,1)S(1)}, u32[]{:S(2)}, u32[]{:S(2)}) collective-permute-start(bf16[3,88,640]{2,1,0:T(8,128)(2,1)S(1)} %get-tuple-element.106), channel_id=1, source_target_pairs={{8,0},{16,8},{24,16},{28,24},{20,28},{12,20},{4,12},{0,4},{9,1},{1... | collective-permute-start | bytes 1013768 | tf_op jit(solution)/shard_map/ppermute | solution.py:80
  4.9 10.9 %collective-permute-start.2 = (bf16[3,88,640]{2,1,0:T(8,128)(2,1)S(1)}, bf16[3,88,640]{2,1,0:T(8,128)(2,1)S(1)}, u32[]{:S(2)}, u32[]{:S(2)}) collective-permute-start(bf16[3,88,640]{2,1,0:T(8,128)(2,1)S(1)} %get-tuple-element.107), channel_id=1, source_target_pairs={{0,8},{8,16},{16,24},{24,28},{28,20},{20,12},{12,4},{4,0},{1,9},{9... | collective-permute-start | bytes 1013768 | tf_op jit(solution)/shard_map/ppermute | solution.py:80
  6.1 13.0 %collective-permute-start.1 = (bf16[3,88,384]{2,1,0:T(8,128)(2,1)S(1)}, bf16[3,88,384]{2,1,0:T(8,128)(2,1)S(1)}, u32[]{:S(2)}, u32[]{:S(2)}) collective-permute-start(bf16[3,88,384]{2,1,0:T(8,128)(2,1)S(1)} %get-tuple-element.108), channel_id=1, source_target_pairs={{8,0},{16,8},{24,16},{28,24},{20,28},{12,20},{4,12},{0,4},{9,1},{1... | collective-permute-start | bytes 608264 | tf_op jit(solution)/shard_map/ppermute | solution.py:80
  8.1 11.0 %collective-permute-start = (bf16[3,88,384]{2,1,0:T(8,128)(2,1)S(1)}, bf16[3,88,384]{2,1,0:T(8,128)(2,1)S(1)}, u32[]{:S(2)}, u32[]{:S(2)}) collective-permute-start(bf16[3,88,384]{2,1,0:T(8,128)(2,1)S(1)} %get-tuple-element.109), channel_id=1, source_target_pairs={{0,8},{8,16},{16,24},{24,28},{28,20},{20,12},{12,4},{4,0},{1,9},{9... | collective-permute-start | bytes 608264 | tf_op jit(solution)/shard_map/ppermute | solution.py:80
  17.0 9.6 %collective-permute-start.7 = (bf16[3,88,640]{2,1,0:T(8,128)(2,1)S(1)}, bf16[3,88,640]{2,1,0:T(8,128)(2,1)S(1)}, u32[]{:S(2)}, u32[]{:S(2)}) collective-permute-start(bf16[3,88,640]{2,1,0:T(8,128)(2,1)S(1)} %get-tuple-element.104), channel_id=1, source_target_pairs={{8,0},{16,8},{24,16},{28,24},{20,28},{12,20},{4,12},{0,4},{9,1},{1... | collective-permute-start | bytes 1013768 | tf_op jit(solution)/shard_map/ppermute | solution.py:80
  18.6 9.8 %collective-permute-start.6 = (bf16[3,88,640]{2,1,0:T(8,128)(2,1)S(1)}, bf16[3,88,640]{2,1,0:T(8,128)(2,1)S(1)}, u32[]{:S(2)}, u32[]{:S(2)}) collective-permute-start(bf16[3,88,640]{2,1,0:T(8,128)(2,1)S(1)} %get-tuple-element.105), channel_id=1, source_target_pairs={{0,8},{8,16},{16,24},{24,28},{28,20},{20,12},{12,4},{4,0},{1,9},{9... | collective-permute-start | bytes 1013768 | tf_op jit(solution)/shard_map/ppermute | solution.py:80
  20.3 11.6 %collective-permute-start.5 = (bf16[3,88,384]{2,1,0:T(8,128)(2,1)S(1)}, bf16[3,88,384]{2,1,0:T(8,128)(2,1)S(1)}, u32[]{:S(2)}, u32[]{:S(2)}) collective-permute-start(bf16[3,88,384]{2,1,0:T(8,128)(2,1)S(1)} %get-tuple-element.102), channel_id=1, source_target_pairs={{8,0},{16,8},{24,16},{28,24},{20,28},{12,20},{4,12},{0,4},{9,1},{1... | collective-permute-start | bytes 608264 | tf_op jit(solution)/shard_map/ppermute | solution.py:80
  21.9 10.9 %collective-permute-start.4 = (bf16[3,88,384]{2,1,0:T(8,128)(2,1)S(1)}, bf16[3,88,384]{2,1,0:T(8,128)(2,1)S(1)}, u32[]{:S(2)}, u32[]{:S(2)}) collective-permute-start(bf16[3,88,384]{2,1,0:T(8,128)(2,1)S(1)} %get-tuple-element.103), channel_id=1, source_target_pairs={{0,8},{8,16},{16,24},{24,28},{28,20},{20,12},{12,4},{4,0},{1,9},{9... | collective-permute-start | bytes 608264 | tf_op jit(solution)/shard_map/ppermute | solution.py:80
  29.7 8.8 %collective-permute-start.11 = (bf16[3,88,640]{2,1,0:T(8,128)(2,1)S(1)}, bf16[3,88,640]{2,1,0:T(8,128)(2,1)S(1)}, u32[]{:S(2)}, u32[]{:S(2)}) collective-permute-start(bf16[3,88,640]{2,1,0:T(8,128)(2,1)S(1)} %get-tuple-element.100), channel_id=1, source_target_pairs={{8,0},{16,8},{24,16},{28,24},{20,28},{12,20},{4,12},{0,4},{9,1},{1... | collective-permute-start | bytes 1013768 | tf_op jit(solution)/shard_map/ppermute | solution.py:80
  30.9 9.1 %collective-permute-start.10 = (bf16[3,88,640]{2,1,0:T(8,128)(2,1)S(1)}, bf16[3,88,640]{2,1,0:T(8,128)(2,1)S(1)}, u32[]{:S(2)}, u32[]{:S(2)}) collective-permute-start(bf16[3,88,640]{2,1,0:T(8,128)(2,1)S(1)} %get-tuple-element.101), channel_id=1, source_target_pairs={{0,8},{8,16},{16,24},{24,28},{28,20},{20,12},{12,4},{4,0},{1,9},{9... | collective-permute-start | bytes 1013768 | tf_op jit(solution)/shard_map/ppermute | solution.py:80
  34.0 9.4 %collective-permute-start.9 = (bf16[3,88,384]{2,1,0:T(8,128)(2,1)S(1)}, bf16[3,88,384]{2,1,0:T(8,128)(2,1)S(1)}, u32[]{:S(2)}, u32[]{:S(2)}) collective-permute-start(bf16[3,88,384]{2,1,0:T(8,128)(2,1)S(1)} %get-tuple-element.98), channel_id=1, source_target_pairs={{8,0},{16,8},{24,16},{28,24},{20,28},{12,20},{4,12},{0,4},{9,1},{1... | collective-permute-start | bytes 608264 | tf_op jit(solution)/shard_map/ppermute | solution.py:80
  34.7 9.7 %collective-permute-start.8 = (bf16[3,88,384]{2,1,0:T(8,128)(2,1)S(1)}, bf16[3,88,384]{2,1,0:T(8,128)(2,1)S(1)}, u32[]{:S(2)}, u32[]{:S(2)}) collective-permute-start(bf16[3,88,384]{2,1,0:T(8,128)(2,1)S(1)} %get-tuple-element.99), channel_id=1, source_target_pairs={{0,8},{8,16},{16,24},{24,28},{28,20},{20,12},{12,4},{4,0},{1,9},{9... | collective-permute-start | bytes 608264 | tf_op jit(solution)/shard_map/ppermute | solution.py:80
  41.3 8.8 %collective-permute-start.15 = (bf16[3,88,640]{2,1,0:T(8,128)(2,1)S(1)}, bf16[3,88,640]{2,1,0:T(8,128)(2,1)S(1)}, u32[]{:S(2)}, u32[]{:S(2)}) collective-permute-start(bf16[3,88,640]{2,1,0:T(8,128)(2,1)S(1)} %get-tuple-element.96), channel_id=1, source_target_pairs={{8,0},{16,8},{24,16},{28,24},{20,28},{12,20},{4,12},{0,4},{9,1},{1... | collective-permute-start | bytes 1013768 | tf_op jit(solution)/shard_map/ppermute | solution.py:80
  45.5 9.4 %collective-permute-start.13 = (bf16[3,88,384]{2,1,0:T(8,128)(2,1)S(1)}, bf16[3,88,384]{2,1,0:T(8,128)(2,1)S(1)}, u32[]{:S(2)}, u32[]{:S(2)}) collective-permute-start(bf16[3,88,384]{2,1,0:T(8,128)(2,1)S(1)} %get-tuple-element.94), channel_id=1, source_target_pairs={{8,0},{16,8},{24,16},{28,24},{20,28},{12,20},{4,12},{0,4},{9,1},{1... | collective-permute-start | bytes 608264 | tf_op jit(solution)/shard_map/ppermute | solution.py:80
  47.2 8.8 %collective-permute-start.12 = (bf16[3,88,384]{2,1,0:T(8,128)(2,1)S(1)}, bf16[3,88,384]{2,1,0:T(8,128)(2,1)S(1)}, u32[]{:S(2)}, u32[]{:S(2)}) collective-permute-start(bf16[3,88,384]{2,1,0:T(8,128)(2,1)S(1)} %get-tuple-element.95), channel_id=1, source_target_pairs={{0,8},{8,16},{16,24},{24,28},{28,20},{20,12},{12,4},{4,0},{1,9},{9... | collective-permute-start | bytes 608264 | tf_op jit(solution)/shard_map/ppermute | solution.py:80
  52.9 8.8 %collective-permute-start.19 = (bf16[3,88,640]{2,1,0:T(8,128)(2,1)S(1)}, bf16[3,88,640]{2,1,0:T(8,128)(2,1)S(1)}, u32[]{:S(2)}, u32[]{:S(2)}) collective-permute-start(bf16[3,88,640]{2,1,0:T(8,128)(2,1)S(1)} %get-tuple-element.92), channel_id=1, source_target_pairs={{8,0},{16,8},{24,16},{28,24},{20,28},{12,20},{4,12},{0,4},{9,1},{1... | collective-permute-start | bytes 1013768 | tf_op jit(solution)/shard_map/ppermute | solution.py:80
  57.1 9.4 %collective-permute-start.17 = (bf16[3,88,384]{2,1,0:T(8,128)(2,1)S(1)}, bf16[3,88,384]{2,1,0:T(8,128)(2,1)S(1)}, u32[]{:S(2)}, u32[]{:S(2)}) collective-permute-start(bf16[3,88,384]{2,1,0:T(8,128)(2,1)S(1)} %get-tuple-element.90), channel_id=1, source_target_pairs={{8,0},{16,8},{24,16},{28,24},{20,28},{12,20},{4,12},{0,4},{9,1},{1... | collective-permute-start | bytes 608264 | tf_op jit(solution)/shard_map/ppermute | solution.py:80
  58.8 8.8 %collective-permute-start.16 = (bf16[3,88,384]{2,1,0:T(8,128)(2,1)S(1)}, bf16[3,88,384]{2,1,0:T(8,128)(2,1)S(1)}, u32[]{:S(2)}, u32[]{:S(2)}) collective-permute-start(bf16[3,88,384]{2,1,0:T(8,128)(2,1)S(1)} %get-tuple-element.91), channel_id=1, source_target_pairs={{0,8},{8,16},{16,24},{24,28},{28,20},{20,12},{12,4},{4,0},{1,9},{9... | collective-permute-start | bytes 608264 | tf_op jit(solution)/shard_map/ppermute | solution.py:80
  64.5 8.8 %collective-permute-start.23 = (bf16[3,88,640]{2,1,0:T(8,128)(2,1)S(1)}, bf16[3,88,640]{2,1,0:T(8,128)(2,1)S(1)}, u32[]{:S(2)}, u32[]{:S(2)}) collective-permute-start(bf16[3,88,640]{2,1,0:T(8,128)(2,1)S(1)} %get-tuple-element.88), channel_id=1, source_target_pairs={{8,0},{16,8},{24,16},{28,24},{20,28},{12,20},{4,12},{0,4},{9,1},{1... | collective-permute-start | bytes 1013768 | tf_op jit(solution)/shard_map/ppermute | solution.py:80
  66.1 8.7 %collective-permute-start.22 = (bf16[3,88,640]{2,1,0:T(8,128)(2,1)S(1)}, bf16[3,88,640]{2,1,0:T(8,128)(2,1)S(1)}, u32[]{:S(2)}, u32[]{:S(2)}) collective-permute-start(bf16[3,88,640]{2,1,0:T(8,128)(2,1)S(1)} %get-tuple-element.89), channel_id=1, source_target_pairs={{0,8},{8,16},{16,24},{24,28},{28,20},{20,12},{12,4},{4,0},{1,9},{9... | collective-permute-start | bytes 1013768 | tf_op jit(solution)/shard_map/ppermute | solution.py:80
  68.7 9.4 %collective-permute-start.21 = (bf16[3,88,384]{2,1,0:T(8,128)(2,1)S(1)}, bf16[3,88,384]{2,1,0:T(8,128)(2,1)S(1)}, u32[]{:S(2)}, u32[]{:S(2)}) collective-permute-start(bf16[3,88,384]{2,1,0:T(8,128)(2,1)S(1)} %get-tuple-element.86), channel_id=1, source_target_pairs={{8,0},{16,8},{24,16},{28,24},{20,28},{12,20},{4,12},{0,4},{9,1},{1... | collective-permute-start | bytes 608264 | tf_op jit(solution)/shard_map/ppermute | solution.py:80
  70.4 8.8 %collective-permute-start.20 = (bf16[3,88,384]{2,1,0:T(8,128)(2,1)S(1)}, bf16[3,88,384]{2,1,0:T(8,128)(2,1)S(1)}, u32[]{:S(2)}, u32[]{:S(2)}) collective-permute-start(bf16[3,88,384]{2,1,0:T(8,128)(2,1)S(1)} %get-tuple-element.87), channel_id=1, source_target_pairs={{0,8},{8,16},{16,24},{24,28},{28,20},{20,12},{12,4},{4,0},{1,9},{9... | collective-permute-start | bytes 608264 | tf_op jit(solution)/shard_map/ppermute | solution.py:80
  104.9 10.0 %collective-permute-start.29 = (bf16[88,2048]{1,0:T(8,128)(2,1)S(1)}, bf16[88,2048]{1,0:T(8,128)(2,1)S(1)}, u32[]{:S(2)}, u32[]{:S(2)}) collective-permute-start(bf16[88,2048]{1,0:T(8,128)(2,1)S(1)} %get-tuple-element.64), channel_id=1, source_target_pairs={{24,8},{0,16},{20,4},{29,13},{5,21},{9,25},{26,10},{2,18},{22,6},{... | collective-permute-start | bytes 1081352 | tf_op jit(solution)/shard_map/ppermute | solution.py:348
  106.3 9.5 %collective-permute-start.30 = (bf16[88,2048]{1,0:T(8,128)(2,1)S(1)}, bf16[88,2048]{1,0:T(8,128)(2,1)S(1)}, u32[]{:S(2)}, u32[]{:S(2)}) collective-permute-start(bf16[88,2048]{1,0:T(8,128)(2,1)S(1)} %get-tuple-element.65), channel_id=1, source_target_pairs={{28,8},{4,16},{16,4},{25,13},{1,21},{13,25},{30,10},{6,18},{18,6},... | collective-permute-start | bytes 1081352 | tf_op jit(solution)/shard_map/ppermute | solution.py:348
  107.0 15.7 %collective-permute-start.33 = (bf16[88,2048]{1,0:T(8,128)(2,1)S(1)}, bf16[88,2048]{1,0:T(8,128)(2,1)S(1)}, u32[]{:S(2)}, u32[]{:S(2)}) collective-permute-start(bf16[88,2048]{1,0:T(8,128)(2,1)S(1)} %get-tuple-element.70), channel_id=1, source_target_pairs={{0,8},{24,16},{12,4},{5,13},{29,21},{17,25},{2,10},{26,18},{14,6},... | collective-permute-start | bytes 1081352 | tf_op jit(solution)/shard_map/ppermute | solution.py:348
  108.9 13.8 %collective-permute-start.34 = (bf16[88,2048]{1,0:T(8,128)(2,1)S(1)}, bf16[88,2048]{1,0:T(8,128)(2,1)S(1)}, u32[]{:S(2)}, u32[]{:S(2)}) collective-permute-start(bf16[88,2048]{1,0:T(8,128)(2,1)S(1)} %get-tuple-element.71), channel_id=1, source_target_pairs={{4,8},{28,16},{8,4},{1,13},{25,21},{21,25},{6,10},{30,18},{10,6},{... | collective-permute-start | bytes 1081352 | tf_op jit(solution)/shard_map/ppermute | solution.py:348
  109.8 12.8 %collective-permute-start.31 = (bf16[88,2048]{1,0:T(8,128)(2,1)S(1)}, bf16[88,2048]{1,0:T(8,128)(2,1)S(1)}, u32[]{:S(2)}, u32[]{:S(2)}) collective-permute-start(bf16[88,2048]{1,0:T(8,128)(2,1)S(1)} %get-tuple-element.67), channel_id=1, source_target_pairs={{16,8},{8,16},{28,4},{21,13},{13,21},{1,25},{18,10},{10,18},{30,6}... | collective-permute-start | bytes 1081352 | tf_op jit(solution)/shard_map/ppermute | solution.py:348
  137.5 28.0 %collective-permute-start.35 = (bf16[176,2048]{1,0:T(8,128)(2,1)S(1)}, bf16[176,2048]{1,0:T(8,128)(2,1)S(1)}, u32[]{:S(2)}, u32[]{:S(2)}) collective-permute-start(bf16[176,2048]{1,0:T(8,128)(2,1)S(1)} %get-tuple-element.73), channel_id=1, source_target_pairs={{8,12},{16,20},{4,0},{13,9},{21,17},{25,29},{10,14},{18,22},{6,2},... | collective-permute-start | bytes 2162696 | tf_op jit(solution)/shard_map/ppermute | solution.py:348
  138.8 28.7 %collective-permute-start.36 = (bf16[88,2048]{1,0:T(8,128)(2,1)S(1)}, bf16[88,2048]{1,0:T(8,128)(2,1)S(1)}, u32[]{:S(2)}, u32[]{:S(2)}) collective-permute-start(bf16[88,2048]{1,0:T(8,128)(2,1)S(1)} %get-tuple-element.74), channel_id=1, source_target_pairs={{8,24},{16,0},{4,20},{13,29},{21,5},{25,9},{10,26},{18,2},{6,22},{... | collective-permute-start | bytes 1081352 | tf_op jit(solution)/shard_map/ppermute | solution.py:348
  140.1 31.8 %collective-permute-start.37 = (bf16[88,2048]{1,0:T(8,128)(2,1)S(1)}, bf16[88,2048]{1,0:T(8,128)(2,1)S(1)}, u32[]{:S(2)}, u32[]{:S(2)}) collective-permute-start(bf16[88,2048]{1,0:T(8,128)(2,1)S(1)} %get-tuple-element.75), channel_id=1, source_target_pairs={{8,28},{16,4},{4,16},{13,25},{21,1},{25,13},{10,30},{18,6},{6,18},... | collective-permute-start | bytes 1081352 | tf_op jit(solution)/shard_map/ppermute | solution.py:348
  140.8 31.1 %collective-permute-start.38 = (bf16[88,2048]{1,0:T(8,128)(2,1)S(1)}, bf16[88,2048]{1,0:T(8,128)(2,1)S(1)}, u32[]{:S(2)}, u32[]{:S(2)}) collective-permute-start(bf16[88,2048]{1,0:T(8,128)(2,1)S(1)} %get-tuple-element.76), channel_id=1, source_target_pairs={{8,16},{16,8},{4,28},{13,21},{21,13},{25,1},{10,18},{18,10},{6,30}... | collective-permute-start | bytes 1081352 | tf_op jit(solution)/shard_map/ppermute | solution.py:348
  165.5 9.4 %collective-permute-start.40 = (bf16[88,2048]{1,0:T(8,128)(2,1)S(1)}, bf16[88,2048]{1,0:T(8,128)(2,1)S(1)}, u32[]{:S(2)}, u32[]{:S(2)}) collective-permute-start(bf16[88,2048]{1,0:T(8,128)(2,1)S(1)} %get-tuple-element.79), channel_id=1, source_target_pairs={{8,0},{16,24},{4,12},{13,5},{21,29},{25,17},{10,2},{18,26},{6,14},... | collective-permute-start | bytes 1081352 | tf_op jit(solution)/shard_map/ppermute | solution.py:348
  (10 other events, 78.1 us)

commit v4 on v3

--- a/solution.py
+++ b/solution.py
@@ -377,66 +377,131 @@
     )(passing, mine)
 
 
-def newton_schulz_body(count, place, scale, *refs):
-    ins, outs = refs[:count], refs[count : 2 * count]
-    d, a, q, qs = refs[2 * count :]
-    rows = ins[0].shape[0]
-    whole, columns = d.shape
-    for i in range(count):
-        d[i * rows : (i + 1) * rows, :] = ins[i][...]
-
-    a[...] = lax.dot_general(d[...], d[...], (((1,), (1,)), ((), ())), preferred_element_type=F32)
-    gram = a[...]
-    diagonal = lax.broadcasted_iota(jnp.int32, gram.shape, 0) == lax.broadcasted_iota(
-        jnp.int32, gram.shape, 1
-    )
-    norm = jnp.sqrt(jnp.sum(jnp.where(diagonal, gram, 0.0)))
-    inv = 1.0 / (norm + 1e-07)
-    a[...] = (gram * inv) * inv
-    for step in range(NS_ITERS):
-        ab = a[...].astype(BF16)
-        poly = coef_b * a[...] + coef_c * jnp.dot(ab, ab, preferred_element_type=F32)
-        pb = poly.astype(BF16)
-        if step == 0:
-            q[...] = jnp.where(diagonal, poly + coef_a, poly)
-        else:
-            q[...] = coef_a * q[...] + jnp.dot(
-                pb, q[...].astype(BF16), preferred_element_type=F32
-            )
-        if step < NS_ITERS - 1:
-            t = jnp.dot(pb, ab, preferred_element_type=F32)
-            a[...] = (
-                (coef_a * coef_a) * a[...]
-                + (2 * coef_a) * t
-                + jnp.dot(pb, t.astype(BF16), preferred_element_type=F32)
-            )
-    qs[...] = (q[...] * (inv * scale)).astype(BF16)
+def rows_of(order, rows):
+    return {step: slice(i * rows, (i + 1) * rows) for i, step in enumerate(order)}
+
+
+def stage_of(ranks):
+    return ([0, 2, 3, 1, 4, 5, 6, 7], 6, 3) if ranks == 8 else (list(range(ranks)), 0, 0)
+
+
+def gram_width(height):
+    return height // 128 * 128
+
+
+def first_gram(pieces, place, whole):
+    rows, columns = pieces[0].shape
+    height = len(pieces) * rows
+    width = gram_width(height)
+
+    def body(*refs):
+        ins, (d, gram) = refs[:-2], refs[-2:]
+        for ref, at in zip(ins, place):
+            d[at, :] = ref[...]
+        gram[...] = gram_product(d[:height, :], d[:width, :])
+
+    return pl.pallas_call(
+        body,
+        out_shape=[
+            jax.ShapeDtypeStruct((whole, columns), BF16),
+            jax.ShapeDtypeStruct((height, width), F32),
+        ],
+        in_specs=[VMEM] * len(pieces),
+        out_specs=[VMEM] * 2,
+        compiler_params=SMALL,
+        name="first_gram",
+        cost_estimate=pl.CostEstimate(
+            flops=2 * height * width * columns, bytes_accessed=0, transcendentals=0
+        ),
+    )(*pieces)
+
+
+def gram_product(x, y):
+    return lax.dot_general(x, y, (((1,), (1,)), ((), ())), preferred_element_type=F32)
+
+
+def product_rows(qs, d, outs, base, rows):
+    columns = d.shape[1]
     width = next(w for w in (512, 256, 128, columns) if columns % w == 0)
     for c in range(0, columns, width):
-        x = jnp.dot(qs[...], d[:, c : c + width], preferred_element_type=F32)
-        for out, parts in zip(outs, place):
-            for i, j in enumerate(parts):
-                out[i * rows : (i + 1) * rows, c : c + width] = x[
-                    j * rows : (j + 1) * rows, :
-                ].astype(BF16)
-
-
-def newton_schulz(pieces, place, scale):
-    count = len(pieces)
+        x = jnp.dot(qs, d[:, c : c + width], preferred_element_type=F32)
+        for ref, parts in outs:
+            for i, part in enumerate(parts):
+                at = part.start - base
+                ref[i * rows : (i + 1) * rows, c : c + width] = x[at : at + rows, :].astype(BF16)
+
+
+def newton_schulz(pieces, groups, order, early, late, scale):
     rows, columns = pieces[0].shape
-    whole = count * rows
-    vmem = pl.BlockSpec(memory_space=pltpu.VMEM)
-    return pl.pallas_call(
-        lambda *refs: newton_schulz_body(count, place, scale, *refs),
-        out_shape=[jax.ShapeDtypeStruct((len(p) * rows, columns), BF16) for p in place],
-        in_specs=[vmem] * count,
-        out_specs=[vmem] * count,
-        scratch_shapes=[
-            pltpu.VMEM((whole, columns), BF16),
-            pltpu.VMEM((whole, whole), F32),
-            pltpu.VMEM((whole, whole), F32),
-            pltpu.VMEM((whole, whole), BF16),
-        ],
+    whole = len(order) * rows
+    place = rows_of(order, rows)
+    height, split = early * rows, late * rows
+    width = gram_width(height)
+    head = [g for g in groups if g[0] not in order[:late]]
+    tail = [g for g in groups if g[0] in order[:late]]
+
+    def body(*refs):
+        refs = list(refs)
+        take = lambda n: [refs.pop(0) for _ in range(n)]
+        _, gram = take(2) if early else (None, None)
+        ins, (d, qs), outs = take(len(order) - early), take(2), take(len(head))
+        a, q = refs
+        for step, ref in zip(order[early:], ins):
+            d[place[step], :] = ref[...]
+        if early:
+            a[:height, :width] = gram[...]
+            a[:height, width:] = gram_product(d[:height, :], d[width:, :])
+            a[height:, :] = gram_product(d[height:, :], d[...])
+        else:
+            a[...] = gram_product(d[...], d[...])
+        diagonal = lax.broadcasted_iota(jnp.int32, a.shape, 0) == lax.broadcasted_iota(
+            jnp.int32, a.shape, 1
+        )
+        norm = jnp.sqrt(jnp.sum(jnp.where(diagonal, a[...], 0.0)))
+        inv = 1.0 / (norm + 1e-07)
+        a[...] = (a[...] * inv) * inv
+        for step in range(NS_ITERS):
+            ab = a[...].astype(BF16)
+            poly = coef_b * a[...] + coef_c * jnp.dot(ab, ab, preferred_element_type=F32)
+            pb = poly.astype(BF16)
+            if step == 0:
+                q[...] = jnp.where(diagonal, poly + coef_a, poly)
+            else:
+                q[...] = coef_a * q[...] + jnp.dot(
+                    pb, q[...].astype(BF16), preferred_element_type=F32
+                )
+            if step < NS_ITERS - 1:
+                t = jnp.dot(pb, ab, preferred_element_type=F32)
+                a[...] = (
+                    (coef_a * coef_a) * a[...]
+                    + (2 * coef_a) * t
+                    + jnp.dot(pb, t.astype(BF16), preferred_element_type=F32)
+                )
+        if split:
+            qs[...] = (q[:split, :] * (inv * scale)).astype(BF16)
+        left = (q[split:, :] * (inv * scale)).astype(BF16)
+        parts = [(ref, [place[step] for step in g]) for ref, g in zip(outs, head)]
+        product_rows(left, d, parts, split, rows)
+
+    def shapes(lists):
+        return [jax.ShapeDtypeStruct((len(g) * rows, columns), BF16) for g in lists]
+
+    soon = [step for step in pieces if step in order[:early]]
+    firsts = []
+    if early:
+        firsts = list(first_gram([pieces[x] for x in soon], [place[x] for x in soon], whole))
+    operands = firsts + [pieces[step] for step in order[early:]]
+    d, qs, *done = pl.pallas_call(
+        body,
+        out_shape=[
+            jax.ShapeDtypeStruct((whole, columns), BF16),
+            jax.ShapeDtypeStruct((split or rows, whole), BF16),
+        ]
+        + shapes(head),
+        in_specs=[VMEM] * len(operands),
+        out_specs=[VMEM] * (2 + len(head)),
+        scratch_shapes=[pltpu.VMEM((whole, whole), F32), pltpu.VMEM((whole, whole), F32)],
+        input_output_aliases={0: 0} if early else {},
         compiler_params=pltpu.CompilerParams(vmem_limit_bytes=28 * 2**20),
         name="newton_schulz",
         cost_estimate=pl.CostEstimate(
@@ -444,7 +509,27 @@
             bytes_accessed=4 * whole * columns,
             transcendentals=0,
         ),
-    )(*pieces)
+    )(*operands)
+    result = {g[0]: x for g, x in zip(head, done)}
+    if tail:
+
+        def last_body(qs_ref, d_ref, *outs):
+            parts = [(ref, [place[step] for step in g]) for ref, g in zip(outs, tail)]
+            product_rows(qs_ref[...], d_ref, parts, 0, rows)
+
+        done = pl.pallas_call(
+            last_body,
+            out_shape=shapes(tail),
+            in_specs=[VMEM] * 2,
+            out_specs=[VMEM] * len(tail),
+            compiler_params=SMALL,
+            name="last_rows",
+            cost_estimate=pl.CostEstimate(
+                flops=2 * split * whole * columns, bytes_accessed=0, transcendentals=0
+            ),
+        )(qs, d)
+        result |= {g[0]: x for g, x in zip(tail, done)}
+    return [result[g[0]] for g in groups]
 
 
 def local(grad_parts, momentum):
@@ -465,10 +550,15 @@
     new_momentum = momentum_step(squares, streams, momentum, entries)
     pieces = exchange(mine, both, owners, ranks, experts)
     relays = relayed(mats, ranks)
-    place = [[there.index(step)] for step in here]
+    groups = [[step] for step in here]
     if any(relays):
-        place[here.index(1)] += place[here.index(ranks - 1)]
-    result = newton_schulz(pieces, place, 0.2 * math.sqrt(max(rows_whole, columns)))
+        groups[here.index(1)].append(ranks - 1)
+    result = newton_schulz(
+        dict(zip(there, pieces)),
+        groups,
+        *stage_of(ranks),
+        0.2 * math.sqrt(max(rows_whole, columns)),
+    )
     arrived = exchange(result, both, owners, ranks, experts, relays)
     return (new_momentum, pick_rows(arrived, here, owners, both))
 

time: 180 us -> 177 us (0.983)
  waiting for transfers between devices: 78.1 us -> 75.7 us
    ppermute x14, waiting for transfers between devices: 38.6 us -> 36.2 us  [exchange(): out[step] = lax.ppermute(piece, axes, pairs)]
    pallas_call x1 -> x3, Pallas kernels: 14.9 us -> 14.4 us  [the longest x1 12 us: newton_schulz(): pl.pallas_call(body, out_shape=[jax.ShapeDtypeStruct((whole, columns), BF...]
  transfers between devices with their start and end apart: 42 -> 42, of which waited for: 25 -> 25; matrix products, arithmetic and copies ran while one was open for 9% -> 9% of each run, Pallas kernels for 2% -> 4%
where the time goes in v4:
time: 177 us; the launch traced here: 174 us
  waiting for transfers between devices  75.7 us (43%)
  starting transfers between devices  46 us (26%)
  Pallas kernels  22.7 us (13%)
  other arithmetic  14.4 us (8%)
  blocking collectives  11.7 us (7%)
  local copies, waits for them, and re-layouts  2.23 us (1%)
    ppermute x28, waiting for transfers between devices, ring_reduce_scatter(): got = {d: lax.ppermute(acc[g, d], axis, perms[d]) for d in (1, -1)}  39.5 us
    ppermute x14, waiting for transfers between devices, exchange(): out[step] = lax.ppermute(piece, axes, pairs)  36.2 us
    ppermute x28, starting transfers between devices, ring_reduce_scatter(): got = {d: lax.ppermute(acc[g, d], axis, perms[d]) for d in (1, -1)}  30.2 us
    ppermute x14, starting transfers between devices, exchange(): out[step] = lax.ppermute(piece, axes, pairs)  15.8 us
    convert_element_type x12, other arithmetic, ring_reduce_scatter(): (got[d].astype(F32) + piece(g, d, step).astype(F32)).astype(BF16)  14.4 us
    pallas_call x1, Pallas kernels, newton_schulz(): pl.pallas_call(body, out_shape=[jax.ShapeDtypeStruct((whole, columns), BF...  12 us
    all_to_all x1, blocking collectives, local(): squares = lax.all_to_all(square, both, 0, 0, tiled=True)  11.7 us
  transfers between devices with their start and end apart: 42, of which 25 were waited for; matrix products, arithmetic and copies ran while one was open for 9% of the time, Pallas kernels for 4%

profile of v4, /device:TPU:0, one launch (start us, length us, event | category | flops | bytes accessed | tf_op | source)
XLA Modules:
  0.0 173.6 jit_solution(15569926994177739064)
XLA Ops:
  1.9 3.0 %collective-permute-start.3 = (bf16[3,88,640]{2,1,0:T(8,128)(2,1)S(1)}, bf16[3,88,640]{2,1,0:T(8,128)(2,1)S(1)}, u32[]{:S(2)}, u32[]{:S(2)}) collective-permute-start(bf16[3,88,640]{2,1,0:T(8,128)(2,1)S(1)} %get-tuple-element.114), channel_id=1, source_target_pairs={{8,0},{16,8},{24,16},{28,24},{20,28},{12,20},{4,12},{0,4},{9,1},{1... | collective-permute-start | bytes 1013768 | tf_op jit(solution)/shard_map/ppermute | solution.py:80
  6.1 2.0 %collective-permute-start.1 = (bf16[3,88,384]{2,1,0:T(8,128)(2,1)S(1)}, bf16[3,88,384]{2,1,0:T(8,128)(2,1)S(1)}, u32[]{:S(2)}, u32[]{:S(2)}) collective-permute-start(bf16[3,88,384]{2,1,0:T(8,128)(2,1)S(1)} %get-tuple-element.116), channel_id=1, source_target_pairs={{8,0},{16,8},{24,16},{28,24},{20,28},{12,20},{4,12},{0,4},{9,1},{1... | collective-permute-start | bytes 608264 | tf_op jit(solution)/shard_map/ppermute | solution.py:80
  8.2 5.5 %collective-permute-done.3 = bf16[3,88,640]{2,1,0:T(8,128)(2,1)S(1)} collective-permute-done((bf16[3,88,640]{2,1,0:T(8,128)(2,1)S(1)}, bf16[3,88,640]{2,1,0:T(8,128)(2,1)S(1)}, u32[]{:S(2)}, u32[]{:S(2)}) %collective-permute-start.3) | collective-permute-done | bytes 337952 | tf_op jit(solution)/shard_map/ppermute | solution.py:80
  13.7 2.0 %collective-permute-done.2 = bf16[3,88,640]{2,1,0:T(8,128)(2,1)S(1)} collective-permute-done((bf16[3,88,640]{2,1,0:T(8,128)(2,1)S(1)}, bf16[3,88,640]{2,1,0:T(8,128)(2,1)S(1)}, u32[]{:S(2)}, u32[]{:S(2)}) %collective-permute-start.2) | collective-permute-done | bytes 337952 | tf_op jit(solution)/shard_map/ppermute | solution.py:80
  17.0 1.6 collective-permute-start.7
  20.3 1.6 collective-permute-start.5
  22.3 4.3 %collective-permute-done.7 = bf16[3,88,640]{2,1,0:T(8,128)(2,1)S(1)} collective-permute-done((bf16[3,88,640]{2,1,0:T(8,128)(2,1)S(1)}, bf16[3,88,640]{2,1,0:T(8,128)(2,1)S(1)}, u32[]{:S(2)}, u32[]{:S(2)}) %collective-permute-start.7) | collective-permute-done | bytes 337952 | tf_op jit(solution)/shard_map/ppermute | solution.py:80
  26.7 1.8 %collective-permute-done.6 = bf16[3,88,640]{2,1,0:T(8,128)(2,1)S(1)} collective-permute-done((bf16[3,88,640]{2,1,0:T(8,128)(2,1)S(1)}, bf16[3,88,640]{2,1,0:T(8,128)(2,1)S(1)}, u32[]{:S(2)}, u32[]{:S(2)}) %collective-permute-start.6) | collective-permute-done | bytes 337952 | tf_op jit(solution)/shard_map/ppermute | solution.py:80
  36.0 2.5 %collective-permute-done.11 = bf16[3,88,640]{2,1,0:T(8,128)(2,1)S(1)} collective-permute-done((bf16[3,88,640]{2,1,0:T(8,128)(2,1)S(1)}, bf16[3,88,640]{2,1,0:T(8,128)(2,1)S(1)}, u32[]{:S(2)}, u32[]{:S(2)}) %collective-permute-start.11) | collective-permute-done | bytes 337952 | tf_op jit(solution)/shard_map/ppermute | solution.py:80
  41.3 1.6 collective-permute-start.15
  45.5 1.6 collective-permute-start.13
  47.6 2.5 %collective-permute-done.15 = bf16[3,88,640]{2,1,0:T(8,128)(2,1)S(1)} collective-permute-done((bf16[3,88,640]{2,1,0:T(8,128)(2,1)S(1)}, bf16[3,88,640]{2,1,0:T(8,128)(2,1)S(1)}, u32[]{:S(2)}, u32[]{:S(2)}) %collective-permute-start.15) | collective-permute-done | bytes 337952 | tf_op jit(solution)/shard_map/ppermute | solution.py:80
  52.9 1.6 collective-permute-start.19
  57.1 1.6 collective-permute-start.17
  59.2 2.5 %collective-permute-done.19 = bf16[3,88,640]{2,1,0:T(8,128)(2,1)S(1)} collective-permute-done((bf16[3,88,640]{2,1,0:T(8,128)(2,1)S(1)}, bf16[3,88,640]{2,1,0:T(8,128)(2,1)S(1)}, u32[]{:S(2)}, u32[]{:S(2)}) %collective-permute-start.19) | collective-permute-done | bytes 337952 | tf_op jit(solution)/shard_map/ppermute | solution.py:80
  64.5 1.6 collective-permute-start.23
  68.7 1.6 collective-permute-start.21
  70.8 2.5 %collective-permute-done.23 = bf16[3,88,640]{2,1,0:T(8,128)(2,1)S(1)} collective-permute-done((bf16[3,88,640]{2,1,0:T(8,128)(2,1)S(1)}, bf16[3,88,640]{2,1,0:T(8,128)(2,1)S(1)}, u32[]{:S(2)}, u32[]{:S(2)}) %collective-permute-start.23) | collective-permute-done | bytes 337952 | tf_op jit(solution)/shard_map/ppermute | solution.py:80
  76.1 1.7 collective-permute-start.27
  80.3 1.7 %collective-permute-start.25 = (bf16[3,88,384]{2,1,0:T(8,128)(2,1)S(1)}, bf16[3,88,384]{2,1,0:T(8,128)(2,1)S(1)}, u32[]{:S(2)}, u32[]{:S(2)}) collective-permute-start(bf16[3,88,384]{2,1,0:T(8,128)(2,1)S(1)} %get-tuple-element.90), channel_id=1, source_target_pairs={{8,0},{16,8},{24,16},{28,24},{20,28},{12,20},{4,12},{0,4},{9,1},{1... | collective-permute-start | bytes 608264 | tf_op jit(solution)/shard_map/ppermute | solution.py:80
  82.4 2.2 %collective-permute-done.27.refs_1_ = bf16[3,88,640]{2,1,0:T(8,128)(2,1)S(1)} collective-permute-done((bf16[3,88,640]{2,1,0:T(8,128)(2,1)S(1)}, bf16[3,88,640]{2,1,0:T(8,128)(2,1)S(1)}, u32[]{:S(2)}, u32[]{:S(2)}) %collective-permute-start.27) | collective-permute-done | bytes 337952 | tf_op jit(solution)/shard_map/ppermute | solution.py:80
  88.7 11.7 %all_to_all.5.squares_ref = f32[32,1,128]{2,1,0:T(1,128)S(1)} all-to-all(f32[32,1,128]{2,1,0:T(1,128)S(1)} %get-tuple-element.61), channel_id=1, replica_groups=mesh['dp'=8,'expert'=4] {'dp','expert'}, dimensions={0} | all-to-all | bytes 32768 | tf_op jit(solution)/shard_map/all_to_all | solution.py:543
  100.3 2.1 %direction_pieces.1 = (bf16[88,2048]{1,0:T(8,128)(2,1)S(1)}, bf16[88,2048]{1,0:T(8,128)(2,1)S(1)}, bf16[88,2048]{1,0:T(8,128)(2,1)S(1)}, bf16[88,2048]{1,0:T(8,1...) custom-call(f32[32,1,128]{2,1,0:T(1,128)S(1)} %all_to_all.5.squares_, ...), custom_call_target="tpu_custom_call" | custom-call | tf_op jit(solution)/shard_map/direction_pieces/pallas_call | solution.py:237
  102.4 2.5 %collective-permute-start.28 = (bf16[88,2048]{1,0:T(8,128)(2,1)S(1)}, bf16[88,2048]{1,0:T(8,128)(2,1)S(1)}, u32[]{:S(2)}, u32[]{:S(2)}) collective-permute-start(bf16[88,2048]{1,0:T(8,128)(2,1)S(1)} %get-tuple-element.67), channel_id=1, source_target_pairs={{12,8},{20,16},{0,4},{9,13},{17,21},{29,25},{14,10},{22,18},{2,6},... | collective-permute-start | bytes 1081352 | tf_op jit(solution)/shard_map/ppermute | solution.py:348
  107.0 1.9 %collective-permute-start.31 = (bf16[88,2048]{1,0:T(8,128)(2,1)S(1)}, bf16[88,2048]{1,0:T(8,128)(2,1)S(1)}, u32[]{:S(2)}, u32[]{:S(2)}) collective-permute-start(bf16[88,2048]{1,0:T(8,128)(2,1)S(1)} %get-tuple-element.70), channel_id=1, source_target_pairs={{0,8},{24,16},{12,4},{5,13},{29,21},{17,25},{2,10},{26,18},{14,6},... | collective-permute-start | bytes 1081352 | tf_op jit(solution)/shard_map/ppermute | solution.py:348
  110.5 4.4 %collective-permute-done.29.refs_2_ = bf16[88,2048]{1,0:T(8,128)(2,1)S(1)} collective-permute-done((bf16[88,2048]{1,0:T(8,128)(2,1)S(1)}, bf16[88,2048]{1,0:T(8,128)(2,1)S(1)}, u32[]{:S(2)}, u32[]{:S(2)}) %collective-permute-start.29) | collective-permute-done | bytes 360480 | tf_op jit(solution)/shard_map/ppermute | solution.py:348
  115.8 6.9 %collective-permute-done.31.refs_4_ = bf16[88,2048]{1,0:T(8,128)(2,1)S(1)} collective-permute-done((bf16[88,2048]{1,0:T(8,128)(2,1)S(1)}, bf16[88,2048]{1,0:T(8,128)(2,1)S(1)}, u32[]{:S(2)}, u32[]{:S(2)}) %collective-permute-start.31) | collective-permute-done | bytes 360480 | tf_op jit(solution)/shard_map/ppermute | solution.py:348
  124.0 12.0 %newton_schulz.1 = (bf16[704,2048]{1,0:T(8,128)(2,1)S(1)}, bf16[264,704]{1,0:T(8,128)(2,1)S(1)}, bf16[176,2048]{1,0:T(8,128)(2,1)S(1)}, bf16[88,2048]{1,0:T(8,12...) custom-call(bf16[704,2048]{1,0:T(8,128)(2,1)S(1)} %get-tuple-element, ...), custom_call_target="tpu_custom_call", output_to_operand_aliasing={{0}: (0, {})} | custom-call | flops 10340532224 | bytes 5767168 | tf_op jit(solution)/shard_map/newton_schulz/pallas_call | solution.py:494
  141.1 21.3 %collective-permute-done.35.passing_ref.refs_1_ = bf16[176,2048]{1,0:T(8,128)(2,1)S(1)} collective-permute-done((bf16[176,2048]{1,0:T(8,128)(2,1)S(1)}, bf16[176,2048]{1,0:T(8,128)(2,1)S(1)}, u32[]{:S(2)}, u32[]{:S(2)}) %collective-permute-start.35) | collective-permute-done | bytes 720928 | tf_op jit(solution)/shard_map/ppermute | solution.py:348
  165.7 3.0 %momentum_step.1 = f32[3,88,2048]{2,1,0:T(8,128)} custom-call(f32[32,1,128]{2,1,0:T(1,128)S(1)} %all_to_all.5.squares_ref, f32[3,88,640]{2,1,0:T(8,128)S(1)} %get-tuple-element.62.refs_0_, f32[3,88,640]{2,1,0:T(8,128)S(1)} %get-tuple-element.63.refs_1_, f32[3,88,384]{2,1,0:T(8,128)S(1)} %get-tuple-element.64.refs_2_, ...), custom_call_target="tpu_custom_call" | custom-call | tf_op jit(solution)/shard_map/momentum_step/pallas_call | solution.py:261
  168.7 3.3 %collective-permute-done.40.refs_6_ = bf16[88,2048]{1,0:T(8,128)(2,1)S(1)} collective-permute-done((bf16[88,2048]{1,0:T(8,128)(2,1)S(1)}, bf16[88,2048]{1,0:T(8,128)(2,1)S(1)}, u32[]{:S(2)}, u32[]{:S(2)}) %collective-permute-start.40) | collective-permute-done | bytes 360480 | tf_op jit(solution)/shard_map/ppermute | solution.py:348
  172.1 1.6 pick_rows.1
  (76 shorter events, 54.7 us)
Async XLA Ops:
  1.9 11.8 %collective-permute-start.3 = (bf16[3,88,640]{2,1,0:T(8,128)(2,1)S(1)}, bf16[3,88,640]{2,1,0:T(8,128)(2,1)S(1)}, u32[]{:S(2)}, u32[]{:S(2)}) collective-permute-start(bf16[3,88,640]{2,1,0:T(8,128)(2,1)S(1)} %get-tuple-element.114), channel_id=1, source_target_pairs={{8,0},{16,8},{24,16},{28,24},{20,28},{12,20},{4,12},{0,4},{9,1},{1... | collective-permute-start | bytes 1013768 | tf_op jit(solution)/shard_map/ppermute | solution.py:80
  4.9 10.9 %collective-permute-start.2 = (bf16[3,88,640]{2,1,0:T(8,128)(2,1)S(1)}, bf16[3,88,640]{2,1,0:T(8,128)(2,1)S(1)}, u32[]{:S(2)}, u32[]{:S(2)}) collective-permute-start(bf16[3,88,640]{2,1,0:T(8,128)(2,1)S(1)} %get-tuple-element.115), channel_id=1, source_target_pairs={{0,8},{8,16},{16,24},{24,28},{28,20},{20,12},{12,4},{4,0},{1,9},{9... | collective-permute-start | bytes 1013768 | tf_op jit(solution)/shard_map/ppermute | solution.py:80
  6.1 13.0 %collective-permute-start.1 = (bf16[3,88,384]{2,1,0:T(8,128)(2,1)S(1)}, bf16[3,88,384]{2,1,0:T(8,128)(2,1)S(1)}, u32[]{:S(2)}, u32[]{:S(2)}) collective-permute-start(bf16[3,88,384]{2,1,0:T(8,128)(2,1)S(1)} %get-tuple-element.116), channel_id=1, source_target_pairs={{8,0},{16,8},{24,16},{28,24},{20,28},{12,20},{4,12},{0,4},{9,1},{1... | collective-permute-start | bytes 608264 | tf_op jit(solution)/shard_map/ppermute | solution.py:80
  8.1 11.0 %collective-permute-start = (bf16[3,88,384]{2,1,0:T(8,128)(2,1)S(1)}, bf16[3,88,384]{2,1,0:T(8,128)(2,1)S(1)}, u32[]{:S(2)}, u32[]{:S(2)}) collective-permute-start(bf16[3,88,384]{2,1,0:T(8,128)(2,1)S(1)} %get-tuple-element.117), channel_id=1, source_target_pairs={{0,8},{8,16},{16,24},{24,28},{28,20},{20,12},{12,4},{4,0},{1,9},{9... | collective-permute-start | bytes 608264 | tf_op jit(solution)/shard_map/ppermute | solution.py:80
  17.0 9.6 %collective-permute-start.7 = (bf16[3,88,640]{2,1,0:T(8,128)(2,1)S(1)}, bf16[3,88,640]{2,1,0:T(8,128)(2,1)S(1)}, u32[]{:S(2)}, u32[]{:S(2)}) collective-permute-start(bf16[3,88,640]{2,1,0:T(8,128)(2,1)S(1)} %get-tuple-element.112), channel_id=1, source_target_pairs={{8,0},{16,8},{24,16},{28,24},{20,28},{12,20},{4,12},{0,4},{9,1},{1... | collective-permute-start | bytes 1013768 | tf_op jit(solution)/shard_map/ppermute | solution.py:80
  18.6 9.8 %collective-permute-start.6 = (bf16[3,88,640]{2,1,0:T(8,128)(2,1)S(1)}, bf16[3,88,640]{2,1,0:T(8,128)(2,1)S(1)}, u32[]{:S(2)}, u32[]{:S(2)}) collective-permute-start(bf16[3,88,640]{2,1,0:T(8,128)(2,1)S(1)} %get-tuple-element.113), channel_id=1, source_target_pairs={{0,8},{8,16},{16,24},{24,28},{28,20},{20,12},{12,4},{4,0},{1,9},{9... | collective-permute-start | bytes 1013768 | tf_op jit(solution)/shard_map/ppermute | solution.py:80
  20.3 11.6 %collective-permute-start.5 = (bf16[3,88,384]{2,1,0:T(8,128)(2,1)S(1)}, bf16[3,88,384]{2,1,0:T(8,128)(2,1)S(1)}, u32[]{:S(2)}, u32[]{:S(2)}) collective-permute-start(bf16[3,88,384]{2,1,0:T(8,128)(2,1)S(1)} %get-tuple-element.110), channel_id=1, source_target_pairs={{8,0},{16,8},{24,16},{28,24},{20,28},{12,20},{4,12},{0,4},{9,1},{1... | collective-permute-start | bytes 608264 | tf_op jit(solution)/shard_map/ppermute | solution.py:80
  21.9 10.9 %collective-permute-start.4 = (bf16[3,88,384]{2,1,0:T(8,128)(2,1)S(1)}, bf16[3,88,384]{2,1,0:T(8,128)(2,1)S(1)}, u32[]{:S(2)}, u32[]{:S(2)}) collective-permute-start(bf16[3,88,384]{2,1,0:T(8,128)(2,1)S(1)} %get-tuple-element.111), channel_id=1, source_target_pairs={{0,8},{8,16},{16,24},{24,28},{28,20},{20,12},{12,4},{4,0},{1,9},{9... | collective-permute-start | bytes 608264 | tf_op jit(solution)/shard_map/ppermute | solution.py:80
  29.7 8.8 %collective-permute-start.11 = (bf16[3,88,640]{2,1,0:T(8,128)(2,1)S(1)}, bf16[3,88,640]{2,1,0:T(8,128)(2,1)S(1)}, u32[]{:S(2)}, u32[]{:S(2)}) collective-permute-start(bf16[3,88,640]{2,1,0:T(8,128)(2,1)S(1)} %get-tuple-element.108), channel_id=1, source_target_pairs={{8,0},{16,8},{24,16},{28,24},{20,28},{12,20},{4,12},{0,4},{9,1},{1... | collective-permute-start | bytes 1013768 | tf_op jit(solution)/shard_map/ppermute | solution.py:80
  30.9 9.1 %collective-permute-start.10 = (bf16[3,88,640]{2,1,0:T(8,128)(2,1)S(1)}, bf16[3,88,640]{2,1,0:T(8,128)(2,1)S(1)}, u32[]{:S(2)}, u32[]{:S(2)}) collective-permute-start(bf16[3,88,640]{2,1,0:T(8,128)(2,1)S(1)} %get-tuple-element.109), channel_id=1, source_target_pairs={{0,8},{8,16},{16,24},{24,28},{28,20},{20,12},{12,4},{4,0},{1,9},{9... | collective-permute-start | bytes 1013768 | tf_op jit(solution)/shard_map/ppermute | solution.py:80
  34.0 9.4 %collective-permute-start.9 = (bf16[3,88,384]{2,1,0:T(8,128)(2,1)S(1)}, bf16[3,88,384]{2,1,0:T(8,128)(2,1)S(1)}, u32[]{:S(2)}, u32[]{:S(2)}) collective-permute-start(bf16[3,88,384]{2,1,0:T(8,128)(2,1)S(1)} %get-tuple-element.106), channel_id=1, source_target_pairs={{8,0},{16,8},{24,16},{28,24},{20,28},{12,20},{4,12},{0,4},{9,1},{1... | collective-permute-start | bytes 608264 | tf_op jit(solution)/shard_map/ppermute | solution.py:80
  34.7 9.7 %collective-permute-start.8 = (bf16[3,88,384]{2,1,0:T(8,128)(2,1)S(1)}, bf16[3,88,384]{2,1,0:T(8,128)(2,1)S(1)}, u32[]{:S(2)}, u32[]{:S(2)}) collective-permute-start(bf16[3,88,384]{2,1,0:T(8,128)(2,1)S(1)} %get-tuple-element.107), channel_id=1, source_target_pairs={{0,8},{8,16},{16,24},{24,28},{28,20},{20,12},{12,4},{4,0},{1,9},{9... | collective-permute-start | bytes 608264 | tf_op jit(solution)/shard_map/ppermute | solution.py:80
  41.3 8.8 %collective-permute-start.15 = (bf16[3,88,640]{2,1,0:T(8,128)(2,1)S(1)}, bf16[3,88,640]{2,1,0:T(8,128)(2,1)S(1)}, u32[]{:S(2)}, u32[]{:S(2)}) collective-permute-start(bf16[3,88,640]{2,1,0:T(8,128)(2,1)S(1)} %get-tuple-element.104), channel_id=1, source_target_pairs={{8,0},{16,8},{24,16},{28,24},{20,28},{12,20},{4,12},{0,4},{9,1},{1... | collective-permute-start | bytes 1013768 | tf_op jit(solution)/shard_map/ppermute | solution.py:80
  45.5 9.4 %collective-permute-start.13 = (bf16[3,88,384]{2,1,0:T(8,128)(2,1)S(1)}, bf16[3,88,384]{2,1,0:T(8,128)(2,1)S(1)}, u32[]{:S(2)}, u32[]{:S(2)}) collective-permute-start(bf16[3,88,384]{2,1,0:T(8,128)(2,1)S(1)} %get-tuple-element.102), channel_id=1, source_target_pairs={{8,0},{16,8},{24,16},{28,24},{20,28},{12,20},{4,12},{0,4},{9,1},{1... | collective-permute-start | bytes 608264 | tf_op jit(solution)/shard_map/ppermute | solution.py:80
  47.2 8.8 %collective-permute-start.12 = (bf16[3,88,384]{2,1,0:T(8,128)(2,1)S(1)}, bf16[3,88,384]{2,1,0:T(8,128)(2,1)S(1)}, u32[]{:S(2)}, u32[]{:S(2)}) collective-permute-start(bf16[3,88,384]{2,1,0:T(8,128)(2,1)S(1)} %get-tuple-element.103), channel_id=1, source_target_pairs={{0,8},{8,16},{16,24},{24,28},{28,20},{20,12},{12,4},{4,0},{1,9},{9... | collective-permute-start | bytes 608264 | tf_op jit(solution)/shard_map/ppermute | solution.py:80
  52.9 8.8 %collective-permute-start.19 = (bf16[3,88,640]{2,1,0:T(8,128)(2,1)S(1)}, bf16[3,88,640]{2,1,0:T(8,128)(2,1)S(1)}, u32[]{:S(2)}, u32[]{:S(2)}) collective-permute-start(bf16[3,88,640]{2,1,0:T(8,128)(2,1)S(1)} %get-tuple-element.100), channel_id=1, source_target_pairs={{8,0},{16,8},{24,16},{28,24},{20,28},{12,20},{4,12},{0,4},{9,1},{1... | collective-permute-start | bytes 1013768 | tf_op jit(solution)/shard_map/ppermute | solution.py:80
  57.1 9.4 %collective-permute-start.17 = (bf16[3,88,384]{2,1,0:T(8,128)(2,1)S(1)}, bf16[3,88,384]{2,1,0:T(8,128)(2,1)S(1)}, u32[]{:S(2)}, u32[]{:S(2)}) collective-permute-start(bf16[3,88,384]{2,1,0:T(8,128)(2,1)S(1)} %get-tuple-element.98), channel_id=1, source_target_pairs={{8,0},{16,8},{24,16},{28,24},{20,28},{12,20},{4,12},{0,4},{9,1},{1... | collective-permute-start | bytes 608264 | tf_op jit(solution)/shard_map/ppermute | solution.py:80
  58.8 8.8 %collective-permute-start.16 = (bf16[3,88,384]{2,1,0:T(8,128)(2,1)S(1)}, bf16[3,88,384]{2,1,0:T(8,128)(2,1)S(1)}, u32[]{:S(2)}, u32[]{:S(2)}) collective-permute-start(bf16[3,88,384]{2,1,0:T(8,128)(2,1)S(1)} %get-tuple-element.99), channel_id=1, source_target_pairs={{0,8},{8,16},{16,24},{24,28},{28,20},{20,12},{12,4},{4,0},{1,9},{9... | collective-permute-start | bytes 608264 | tf_op jit(solution)/shard_map/ppermute | solution.py:80
  64.5 8.8 %collective-permute-start.23 = (bf16[3,88,640]{2,1,0:T(8,128)(2,1)S(1)}, bf16[3,88,640]{2,1,0:T(8,128)(2,1)S(1)}, u32[]{:S(2)}, u32[]{:S(2)}) collective-permute-start(bf16[3,88,640]{2,1,0:T(8,128)(2,1)S(1)} %get-tuple-element.96), channel_id=1, source_target_pairs={{8,0},{16,8},{24,16},{28,24},{20,28},{12,20},{4,12},{0,4},{9,1},{1... | collective-permute-start | bytes 1013768 | tf_op jit(solution)/shard_map/ppermute | solution.py:80
  68.7 9.4 %collective-permute-start.21 = (bf16[3,88,384]{2,1,0:T(8,128)(2,1)S(1)}, bf16[3,88,384]{2,1,0:T(8,128)(2,1)S(1)}, u32[]{:S(2)}, u32[]{:S(2)}) collective-permute-start(bf16[3,88,384]{2,1,0:T(8,128)(2,1)S(1)} %get-tuple-element.94), channel_id=1, source_target_pairs={{8,0},{16,8},{24,16},{28,24},{20,28},{12,20},{4,12},{0,4},{9,1},{1... | collective-permute-start | bytes 608264 | tf_op jit(solution)/shard_map/ppermute | solution.py:80
  70.4 8.8 %collective-permute-start.20 = (bf16[3,88,384]{2,1,0:T(8,128)(2,1)S(1)}, bf16[3,88,384]{2,1,0:T(8,128)(2,1)S(1)}, u32[]{:S(2)}, u32[]{:S(2)}) collective-permute-start(bf16[3,88,384]{2,1,0:T(8,128)(2,1)S(1)} %get-tuple-element.95), channel_id=1, source_target_pairs={{0,8},{8,16},{16,24},{24,28},{28,20},{20,12},{12,4},{4,0},{1,9},{9... | collective-permute-start | bytes 608264 | tf_op jit(solution)/shard_map/ppermute | solution.py:80
  104.9 10.0 %collective-permute-start.29 = (bf16[88,2048]{1,0:T(8,128)(2,1)S(1)}, bf16[88,2048]{1,0:T(8,128)(2,1)S(1)}, u32[]{:S(2)}, u32[]{:S(2)}) collective-permute-start(bf16[88,2048]{1,0:T(8,128)(2,1)S(1)} %get-tuple-element.68), channel_id=1, source_target_pairs={{24,8},{0,16},{20,4},{29,13},{5,21},{9,25},{26,10},{2,18},{22,6},{... | collective-permute-start | bytes 1081352 | tf_op jit(solution)/shard_map/ppermute | solution.py:348
  106.3 9.5 %collective-permute-start.30 = (bf16[88,2048]{1,0:T(8,128)(2,1)S(1)}, bf16[88,2048]{1,0:T(8,128)(2,1)S(1)}, u32[]{:S(2)}, u32[]{:S(2)}) collective-permute-start(bf16[88,2048]{1,0:T(8,128)(2,1)S(1)} %get-tuple-element.69), channel_id=1, source_target_pairs={{28,8},{4,16},{16,4},{25,13},{1,21},{13,25},{30,10},{6,18},{18,6},... | collective-permute-start | bytes 1081352 | tf_op jit(solution)/shard_map/ppermute | solution.py:348
  107.0 15.7 %collective-permute-start.31 = (bf16[88,2048]{1,0:T(8,128)(2,1)S(1)}, bf16[88,2048]{1,0:T(8,128)(2,1)S(1)}, u32[]{:S(2)}, u32[]{:S(2)}) collective-permute-start(bf16[88,2048]{1,0:T(8,128)(2,1)S(1)} %get-tuple-element.70), channel_id=1, source_target_pairs={{0,8},{24,16},{12,4},{5,13},{29,21},{17,25},{2,10},{26,18},{14,6},... | collective-permute-start | bytes 1081352 | tf_op jit(solution)/shard_map/ppermute | solution.py:348
  108.9 13.8 %collective-permute-start.32 = (bf16[88,2048]{1,0:T(8,128)(2,1)S(1)}, bf16[88,2048]{1,0:T(8,128)(2,1)S(1)}, u32[]{:S(2)}, u32[]{:S(2)}) collective-permute-start(bf16[88,2048]{1,0:T(8,128)(2,1)S(1)} %get-tuple-element.71), channel_id=1, source_target_pairs={{4,8},{28,16},{8,4},{1,13},{25,21},{21,25},{6,10},{30,18},{10,6},{... | collective-permute-start | bytes 1081352 | tf_op jit(solution)/shard_map/ppermute | solution.py:348
  109.8 14.2 %collective-permute-start.33 = (bf16[88,2048]{1,0:T(8,128)(2,1)S(1)}, bf16[88,2048]{1,0:T(8,128)(2,1)S(1)}, u32[]{:S(2)}, u32[]{:S(2)}) collective-permute-start(bf16[88,2048]{1,0:T(8,128)(2,1)S(1)} %get-tuple-element.75), channel_id=1, source_target_pairs={{16,8},{8,16},{28,4},{21,13},{13,21},{1,25},{18,10},{10,18},{30,6}... | collective-permute-start | bytes 1081352 | tf_op jit(solution)/shard_map/ppermute | solution.py:348
  114.9 9.1 %collective-permute-start.34 = (bf16[88,2048]{1,0:T(8,128)(2,1)S(1)}, bf16[88,2048]{1,0:T(8,128)(2,1)S(1)}, u32[]{:S(2)}, u32[]{:S(2)}) collective-permute-start(bf16[88,2048]{1,0:T(8,128)(2,1)S(1)} %get-tuple-element.77), channel_id=1, source_target_pairs={{20,8},{12,16},{24,4},{17,13},{9,21},{5,25},{22,10},{14,18},{26,6}... | collective-permute-start | bytes 1081352 | tf_op jit(solution)/shard_map/ppermute | solution.py:348
  136.0 26.3 %collective-permute-start.35 = (bf16[176,2048]{1,0:T(8,128)(2,1)S(1)}, bf16[176,2048]{1,0:T(8,128)(2,1)S(1)}, u32[]{:S(2)}, u32[]{:S(2)}) collective-permute-start(bf16[176,2048]{1,0:T(8,128)(2,1)S(1)} %get-tuple-element.81), channel_id=1, source_target_pairs={{8,12},{16,20},{4,0},{13,9},{21,17},{25,29},{10,14},{18,22},{6,2},... | collective-permute-start | bytes 2162696 | tf_op jit(solution)/shard_map/ppermute | solution.py:348
  137.3 27.0 %collective-permute-start.36 = (bf16[88,2048]{1,0:T(8,128)(2,1)S(1)}, bf16[88,2048]{1,0:T(8,128)(2,1)S(1)}, u32[]{:S(2)}, u32[]{:S(2)}) collective-permute-start(bf16[88,2048]{1,0:T(8,128)(2,1)S(1)} %get-tuple-element.82), channel_id=1, source_target_pairs={{8,24},{16,0},{4,20},{13,29},{21,5},{25,9},{10,26},{18,2},{6,22},{... | collective-permute-start | bytes 1081352 | tf_op jit(solution)/shard_map/ppermute | solution.py:348
  138.6 30.1 %collective-permute-start.37 = (bf16[88,2048]{1,0:T(8,128)(2,1)S(1)}, bf16[88,2048]{1,0:T(8,128)(2,1)S(1)}, u32[]{:S(2)}, u32[]{:S(2)}) collective-permute-start(bf16[88,2048]{1,0:T(8,128)(2,1)S(1)} %get-tuple-element.83), channel_id=1, source_target_pairs={{8,28},{16,4},{4,16},{13,25},{21,1},{25,13},{10,30},{18,6},{6,18},... | collective-permute-start | bytes 1081352 | tf_op jit(solution)/shard_map/ppermute | solution.py:348
  139.3 29.4 %collective-permute-start.38 = (bf16[88,2048]{1,0:T(8,128)(2,1)S(1)}, bf16[88,2048]{1,0:T(8,128)(2,1)S(1)}, u32[]{:S(2)}, u32[]{:S(2)}) collective-permute-start(bf16[88,2048]{1,0:T(8,128)(2,1)S(1)} %get-tuple-element.84), channel_id=1, source_target_pairs={{8,16},{16,8},{4,28},{13,21},{21,13},{25,1},{10,18},{18,10},{6,30}... | collective-permute-start | bytes 1081352 | tf_op jit(solution)/shard_map/ppermute | solution.py:348
  162.3 9.8 %collective-permute-start.40 = (bf16[88,2048]{1,0:T(8,128)(2,1)S(1)}, bf16[88,2048]{1,0:T(8,128)(2,1)S(1)}, u32[]{:S(2)}, u32[]{:S(2)}) collective-permute-start(bf16[88,2048]{1,0:T(8,128)(2,1)S(1)} %get-tuple-element.87), channel_id=1, source_target_pairs={{8,0},{16,24},{4,12},{13,5},{21,29},{25,17},{10,2},{18,26},{6,14},... | collective-permute-start | bytes 1081352 | tf_op jit(solution)/shard_map/ppermute | solution.py:348
  (10 other events, 79.7 us)

commit v5 on v4

--- a/solution.py
+++ b/solution.py
@@ -104,7 +104,7 @@
     return sum(x[:, c : c + 128] for c in range(0, x.shape[1], 128))
 
 
-def add_and_square(arrived, own, before, copies, later=()):
+def add_and_square(arrived, own, before, copies, later=(), momentum=None):
     count, fetch = len(arrived), isinstance(own, tuple)
     mats, rows, _ = arrived[0].shape
     partials, axis, columns = own if fetch else (None, None, ())
@@ -117,7 +117,9 @@
         got, (whole,) = take(count), take(1) if fetch else (None,)
         addends = [] if fetch else take(count)
         start = take(1) if before is not None else None
+        store = take(1) if momentum is not None else None
         outs, (squares_out,), extra = take(count), take(1), take(len(later))
+        held = take(1) if momentum is not None else None
         loads = []
         if fetch:
             addends, sems = take(count), refs.pop(0)
@@ -125,6 +127,9 @@
             for i, (ref, c) in enumerate(zip(addends + extra, columns)):
                 source = whole.at[:, pl.ds(first, rows), c : c + ref.shape[2]]
                 loads.append(pltpu.make_async_copy(source, ref, sems.at[i]))
+                loads[-1].start()
+            if store:
+                loads.append(pltpu.make_async_copy(store[0], held[0], sems.at[len(shapes)]))
                 loads[-1].start()
         squares = start[0][...] if start else jnp.zeros((rows, 128), F32)
         for i in range(count):
@@ -144,15 +149,19 @@
     specs = [VMEM] * count + ([HBM] if fetch else [VMEM] * count)
     if before is not None:
         operands, specs = operands + [before], specs + [VMEM]
+    if momentum is not None:
+        operands, specs = operands + [in_hbm(momentum)], specs + [HBM]
+    held = [] if momentum is None else [jax.ShapeDtypeStruct(momentum.shape, momentum.dtype)]
     outs = pl.pallas_call(
         body,
         out_shape=[jax.ShapeDtypeStruct(x.shape, F32) for x in arrived]
         + [jax.ShapeDtypeStruct(shape, F32)]
-        + [jax.ShapeDtypeStruct(shape, BF16) for shape, _ in later],
+        + [jax.ShapeDtypeStruct(shape, BF16) for shape, _ in later]
+        + held,
         in_specs=specs,
-        out_specs=[VMEM] * (count + 1 + len(later)),
+        out_specs=[VMEM] * (count + 1 + len(later) + len(held)),
         scratch_shapes=[pltpu.VMEM(x.shape, BF16) for x in arrived]
-        + [pltpu.SemaphoreType.DMA((len(shapes),))]
+        + [pltpu.SemaphoreType.DMA((len(shapes) + len(held),))]
         if fetch
         else [],
         compiler_params=SMALL,
@@ -161,17 +170,17 @@
     return outs[:count], outs[count], list(outs[count + 1 :])
 
 
-def finish_sums(groups, partials, axis, copies):
+def finish_sums(groups, partials, momentum, axis, copies):
     rows = groups[0][0][0].shape[1]
     streams, squares = [], None
     if rows % 8 == 0:
         first, second = [[x for x, _ in g] for g in groups], [[c for _, c in g] for g in groups]
         later = [(x.shape, c) for x, c in groups[1]]
-        head, squares, own = add_and_square(
-            first[0], (partials, axis, second[0]), None, 0, later
+        head, squares, (*own, momentum) = add_and_square(
+            first[0], (partials, axis, second[0]), None, 0, later, momentum
         )
         tail, squares, _ = add_and_square(first[1], own, squares, copies)
-        return list(head) + list(tail), squares
+        return list(head) + list(tail), squares, momentum
     for g, group in enumerate(groups):
         own = [
             lax.dynamic_slice(partials, (0, lax.axis_index(axis) * rows, c), x.shape)
@@ -180,7 +189,7 @@
         last = copies if g == len(groups) - 1 else 0
         summed, squares, _ = add_and_square([x for x, _ in group], own, squares, last)
         streams += summed
-    return streams, squares
+    return streams, squares, momentum
 
 
 def clip_factor(squares_ref, entries):
@@ -196,15 +205,6 @@
         at += s.shape[-1]
 
 
-def load_rows(source, target, sems):
-    loads = [
-        pltpu.make_async_copy(source.at[m], target.at[m], sems.at[m]) for m in range(target.shape[0])
-    ]
-    for load in loads:
-        load.start()
-    return loads
-
-
 def my_owners(owners, axes):
     odd = lax.axis_index(axes[1]) % 2 == 1
     return lax.axis_index(axes[0]), [jnp.where(odd, b, a) for a, b in zip(*owners)]
@@ -216,12 +216,8 @@
     count = len(streams)
 
     def body(squares_ref, *refs):
-        ins, whole, outs = refs[:count], refs[count], refs[count + 1 : -2]
-        mom, sems = refs[-2:]
-        loads = load_rows(whole, mom, sems)
+        ins, mom, outs = refs[:count], refs[count], refs[count + 1 :]
         factor = jnp.broadcast_to(clip_factor(squares_ref, entries), (rows, 128))
-        for load in loads:
-            load.wait()
         rank, owner = my_owners(owners, axes)
         for step in range(rounds):
             target = partner(rank, order[step], ranks)
@@ -237,12 +233,11 @@
     return pl.pallas_call(
         body,
         out_shape=[jax.ShapeDtypeStruct((rows, columns), BF16)] * rounds,
-        in_specs=[VMEM] * (count + 1) + [HBM],
+        in_specs=[VMEM] * (count + 2),
         out_specs=[VMEM] * rounds,
-        scratch_shapes=[pltpu.VMEM(momentum.shape, F32), pltpu.SemaphoreType.DMA((mats,))],
         compiler_params=SMALL,
         name="direction_pieces",
-    )(squares, *streams, in_hbm(momentum))
+    )(squares, *streams, momentum)
 
 
 def momentum_step(squares, streams, momentum, entries):
@@ -250,23 +245,20 @@
     mats, rows, _ = momentum.shape
 
     def body(squares_ref, *refs):
-        ins, whole, out, mom, sems = refs[:count], *refs[count:]
-        loads = load_rows(whole, mom, sems)
+        ins, mom, out = refs[:count], refs[count], refs[count + 1]
         factor = jnp.broadcast_to(clip_factor(squares_ref, entries), (rows, 128))
         for m in range(mats):
-            loads[m].wait()
             for i, here, there in column_tiles(streams):
                 out[m, :, there] = momentum_decay * mom[m, :, there] + factor * ins[i][m, :, here]
 
     return pl.pallas_call(
         body,
         out_shape=jax.ShapeDtypeStruct(momentum.shape, F32),
-        in_specs=[VMEM] * (count + 1) + [HBM],
+        in_specs=[VMEM] * (count + 2),
         out_specs=VMEM,
-        scratch_shapes=[pltpu.VMEM(momentum.shape, F32), pltpu.SemaphoreType.DMA((mats,))],
         compiler_params=SMALL,
         name="momentum_step",
-    )(squares, *streams, in_hbm(momentum))
+    )(squares, *streams, momentum)
 
 
 def pick_rows(arrived, order, owners, axes):
@@ -274,20 +266,27 @@
     mats, ranks = len(owners[0]), len(order)
 
     def body(*refs):
-        out = refs[-1]
+        out, wide, sems = refs[ranks:]
         rank, owner = my_owners(owners, axes)
+        stores = []
         for m in range(mats):
             for at, step in enumerate(order):
 
                 @pl.when(partner(owner[m], step, ranks, back=True) == rank)
                 def _(m=m, at=at):
-                    out[m] = refs[at][:rows, :].astype(F32)
+                    wide[m] = refs[at][:rows, :].astype(F32)
+
+            stores.append(pltpu.make_async_copy(wide.at[m], out.at[m], sems.at[m]))
+            stores[m].start()
+        for store in stores:
+            store.wait()
 
     return pl.pallas_call(
         body,
         out_shape=jax.ShapeDtypeStruct((mats, rows, columns), F32),
         in_specs=[VMEM] * len(arrived),
-        out_specs=VMEM,
+        out_specs=HBM,
+        scratch_shapes=[pltpu.VMEM((mats, rows, columns), F32), pltpu.SemaphoreType.DMA((mats,))],
         compiler_params=SMALL,
         name="pick_rows",
     )(*arrived)
@@ -539,7 +538,7 @@
     both = ("dp", "expert")
 
     groups = ring_reduce_scatter(partials, "dp")
-    streams, square = finish_sums(groups, partials, "dp", ranks * experts)
+    streams, square, momentum = finish_sums(groups, partials, momentum, "dp", ranks * experts)
     squares = lax.all_to_all(square, both, 0, 0, tiled=True)
     entries = mats * experts * rows_whole * columns
 

time: 177 us -> 175 us (0.989)
  Pallas kernels: 22.7 us -> 20.4 us
where the time goes in v5:
time: 175 us; the launch traced here: 172 us
  waiting for transfers between devices  76.3 us (44%)
  starting transfers between devices  46 us (26%)
  Pallas kernels  20.4 us (12%)
  other arithmetic  14.4 us (8%)
  blocking collectives  11.7 us (7%)
  local copies, waits for them, and re-layouts  2.23 us (1%)
    ppermute x28, waiting for transfers between devices, ring_reduce_scatter(): got = {d: lax.ppermute(acc[g, d], axis, perms[d]) for d in (1, -1)}  38.8 us
    ppermute x14, waiting for transfers between devices, exchange(): out[step] = lax.ppermute(piece, axes, pairs)  37.5 us
    ppermute x28, starting transfers between devices, ring_reduce_scatter(): got = {d: lax.ppermute(acc[g, d], axis, perms[d]) for d in (1, -1)}  30.2 us
    ppermute x14, starting transfers between devices, exchange(): out[step] = lax.ppermute(piece, axes, pairs)  15.8 us
    convert_element_type x12, other arithmetic, ring_reduce_scatter(): (got[d].astype(F32) + piece(g, d, step).astype(F32)).astype(BF16)  14.4 us
    pallas_call x1, Pallas kernels, newton_schulz(): pl.pallas_call(body, out_shape=[jax.ShapeDtypeStruct((whole, columns), BF...  12 us
    all_to_all x1, blocking collectives, local(): squares = lax.all_to_all(square, both, 0, 0, tiled=True)  11.7 us
  transfers between devices with their start and end apart: 42, of which 25 were waited for; matrix products, arithmetic and copies ran while one was open for 9% of the time, Pallas kernels for 4%

profile of v5, /device:TPU:0, one launch (start us, length us, event | category | flops | bytes accessed | tf_op | source)
XLA Modules:
  0.0 172.1 jit_solution(6037348511056726232)
XLA Ops:
  1.9 3.0 %collective-permute-start.3 = (bf16[3,88,640]{2,1,0:T(8,128)(2,1)S(1)}, bf16[3,88,640]{2,1,0:T(8,128)(2,1)S(1)}, u32[]{:S(2)}, u32[]{:S(2)}) collective-permute-start(bf16[3,88,640]{2,1,0:T(8,128)(2,1)S(1)} %get-tuple-element.116), channel_id=1, source_target_pairs={{8,0},{16,8},{24,16},{28,24},{20,28},{12,20},{4,12},{0,4},{9,1},{1... | collective-permute-start | bytes 1013768 | tf_op jit(solution)/shard_map/ppermute | solution.py:80
  6.1 2.0 %collective-permute-start.1 = (bf16[3,88,384]{2,1,0:T(8,128)(2,1)S(1)}, bf16[3,88,384]{2,1,0:T(8,128)(2,1)S(1)}, u32[]{:S(2)}, u32[]{:S(2)}) collective-permute-start(bf16[3,88,384]{2,1,0:T(8,128)(2,1)S(1)} %get-tuple-element.118), channel_id=1, source_target_pairs={{8,0},{16,8},{24,16},{28,24},{20,28},{12,20},{4,12},{0,4},{9,1},{1... | collective-permute-start | bytes 608264 | tf_op jit(solution)/shard_map/ppermute | solution.py:80
  8.2 5.5 %collective-permute-done.3 = bf16[3,88,640]{2,1,0:T(8,128)(2,1)S(1)} collective-permute-done((bf16[3,88,640]{2,1,0:T(8,128)(2,1)S(1)}, bf16[3,88,640]{2,1,0:T(8,128)(2,1)S(1)}, u32[]{:S(2)}, u32[]{:S(2)}) %collective-permute-start.3) | collective-permute-done | bytes 337952 | tf_op jit(solution)/shard_map/ppermute | solution.py:80
  13.7 2.0 %collective-permute-done.2 = bf16[3,88,640]{2,1,0:T(8,128)(2,1)S(1)} collective-permute-done((bf16[3,88,640]{2,1,0:T(8,128)(2,1)S(1)}, bf16[3,88,640]{2,1,0:T(8,128)(2,1)S(1)}, u32[]{:S(2)}, u32[]{:S(2)}) %collective-permute-start.2) | collective-permute-done | bytes 337952 | tf_op jit(solution)/shard_map/ppermute | solution.py:80
  17.0 1.6 collective-permute-start.7
  20.3 1.6 collective-permute-start.5
  22.3 4.3 %collective-permute-done.7 = bf16[3,88,640]{2,1,0:T(8,128)(2,1)S(1)} collective-permute-done((bf16[3,88,640]{2,1,0:T(8,128)(2,1)S(1)}, bf16[3,88,640]{2,1,0:T(8,128)(2,1)S(1)}, u32[]{:S(2)}, u32[]{:S(2)}) %collective-permute-start.7) | collective-permute-done | bytes 337952 | tf_op jit(solution)/shard_map/ppermute | solution.py:80
  26.7 1.8 %collective-permute-done.6 = bf16[3,88,640]{2,1,0:T(8,128)(2,1)S(1)} collective-permute-done((bf16[3,88,640]{2,1,0:T(8,128)(2,1)S(1)}, bf16[3,88,640]{2,1,0:T(8,128)(2,1)S(1)}, u32[]{:S(2)}, u32[]{:S(2)}) %collective-permute-start.6) | collective-permute-done | bytes 337952 | tf_op jit(solution)/shard_map/ppermute | solution.py:80
  36.0 2.5 %collective-permute-done.11 = bf16[3,88,640]{2,1,0:T(8,128)(2,1)S(1)} collective-permute-done((bf16[3,88,640]{2,1,0:T(8,128)(2,1)S(1)}, bf16[3,88,640]{2,1,0:T(8,128)(2,1)S(1)}, u32[]{:S(2)}, u32[]{:S(2)}) %collective-permute-start.11) | collective-permute-done | bytes 337952 | tf_op jit(solution)/shard_map/ppermute | solution.py:80
  38.5 1.5 collective-permute-done.10
  41.3 1.6 collective-permute-start.15
  45.5 1.6 collective-permute-start.13
  47.6 2.5 %collective-permute-done.15 = bf16[3,88,640]{2,1,0:T(8,128)(2,1)S(1)} collective-permute-done((bf16[3,88,640]{2,1,0:T(8,128)(2,1)S(1)}, bf16[3,88,640]{2,1,0:T(8,128)(2,1)S(1)}, u32[]{:S(2)}, u32[]{:S(2)}) %collective-permute-start.15) | collective-permute-done | bytes 337952 | tf_op jit(solution)/shard_map/ppermute | solution.py:80
  52.9 1.6 collective-permute-start.19
  57.1 1.6 collective-permute-start.17
  59.2 2.5 %collective-permute-done.19 = bf16[3,88,640]{2,1,0:T(8,128)(2,1)S(1)} collective-permute-done((bf16[3,88,640]{2,1,0:T(8,128)(2,1)S(1)}, bf16[3,88,640]{2,1,0:T(8,128)(2,1)S(1)}, u32[]{:S(2)}, u32[]{:S(2)}) %collective-permute-start.19) | collective-permute-done | bytes 337952 | tf_op jit(solution)/shard_map/ppermute | solution.py:80
  64.5 1.6 collective-permute-start.23
  68.7 1.6 collective-permute-start.21
  70.8 2.5 %collective-permute-done.23 = bf16[3,88,640]{2,1,0:T(8,128)(2,1)S(1)} collective-permute-done((bf16[3,88,640]{2,1,0:T(8,128)(2,1)S(1)}, bf16[3,88,640]{2,1,0:T(8,128)(2,1)S(1)}, u32[]{:S(2)}, u32[]{:S(2)}) %collective-permute-start.23) | collective-permute-done | bytes 337952 | tf_op jit(solution)/shard_map/ppermute | solution.py:80
  76.1 1.7 collective-permute-start.27
  80.3 1.7 %collective-permute-start.25 = (bf16[3,88,384]{2,1,0:T(8,128)(2,1)S(1)}, bf16[3,88,384]{2,1,0:T(8,128)(2,1)S(1)}, u32[]{:S(2)}, u32[]{:S(2)}) collective-permute-start(bf16[3,88,384]{2,1,0:T(8,128)(2,1)S(1)} %get-tuple-element.92), channel_id=1, source_target_pairs={{8,0},{16,8},{24,16},{28,24},{20,28},{12,20},{4,12},{0,4},{9,1},{1... | collective-permute-start | bytes 608264 | tf_op jit(solution)/shard_map/ppermute | solution.py:80
  82.4 2.2 %collective-permute-done.27.refs_1_ = bf16[3,88,640]{2,1,0:T(8,128)(2,1)S(1)} collective-permute-done((bf16[3,88,640]{2,1,0:T(8,128)(2,1)S(1)}, bf16[3,88,640]{2,1,0:T(8,128)(2,1)S(1)}, u32[]{:S(2)}, u32[]{:S(2)}) %collective-permute-start.27) | collective-permute-done | bytes 337952 | tf_op jit(solution)/shard_map/ppermute | solution.py:80
  86.0 2.0 %add_and_square.2 = (f32[3,88,640]{2,1,0:T(8,128)S(1)}, f32[3,88,640]{2,1,0:T(8,128)S(1)}, f32[88,128]{1,0:T(8,128)S(1)}, bf16[3,88,384]{2,1,0:T(8,128)(2,1)S(1)...) custom-call(bf16[3,88,640]{2,1,0:T(8,128)(2,1)S(1)} %collective-permute-done.26.refs_0_, ...), custom_call_target="tpu_custom_call" | custom-call | tf_op jit(solution)/shard_map/add_and_square/pallas_call | solution.py:155
  88.7 11.7 %all_to_all.5.squares_ref = f32[32,1,128]{2,1,0:T(1,128)S(1)} all-to-all(f32[32,1,128]{2,1,0:T(1,128)S(1)} %get-tuple-element.62), channel_id=1, replica_groups=mesh['dp'=8,'expert'=4] {'dp','expert'}, dimensions={0} | all-to-all | bytes 32768 | tf_op jit(solution)/shard_map/all_to_all | solution.py:542
  100.9 2.5 %collective-permute-start.28 = (bf16[88,2048]{1,0:T(8,128)(2,1)S(1)}, bf16[88,2048]{1,0:T(8,128)(2,1)S(1)}, u32[]{:S(2)}, u32[]{:S(2)}) collective-permute-start(bf16[88,2048]{1,0:T(8,128)(2,1)S(1)} %get-tuple-element.69), channel_id=1, source_target_pairs={{12,8},{20,16},{0,4},{9,13},{17,21},{29,25},{14,10},{22,18},{2,6},... | collective-permute-start | bytes 1081352 | tf_op jit(solution)/shard_map/ppermute | solution.py:347
  105.4 1.9 %collective-permute-start.31 = (bf16[88,2048]{1,0:T(8,128)(2,1)S(1)}, bf16[88,2048]{1,0:T(8,128)(2,1)S(1)}, u32[]{:S(2)}, u32[]{:S(2)}) collective-permute-start(bf16[88,2048]{1,0:T(8,128)(2,1)S(1)} %get-tuple-element.72), channel_id=1, source_target_pairs={{0,8},{24,16},{12,4},{5,13},{29,21},{17,25},{2,10},{26,18},{14,6},... | collective-permute-start | bytes 1081352 | tf_op jit(solution)/shard_map/ppermute | solution.py:347
  109.0 4.4 %collective-permute-done.29.refs_2_ = bf16[88,2048]{1,0:T(8,128)(2,1)S(1)} collective-permute-done((bf16[88,2048]{1,0:T(8,128)(2,1)S(1)}, bf16[88,2048]{1,0:T(8,128)(2,1)S(1)}, u32[]{:S(2)}, u32[]{:S(2)}) %collective-permute-start.29) | collective-permute-done | bytes 360480 | tf_op jit(solution)/shard_map/ppermute | solution.py:347
  114.3 6.9 %collective-permute-done.31.refs_4_ = bf16[88,2048]{1,0:T(8,128)(2,1)S(1)} collective-permute-done((bf16[88,2048]{1,0:T(8,128)(2,1)S(1)}, bf16[88,2048]{1,0:T(8,128)(2,1)S(1)}, u32[]{:S(2)}, u32[]{:S(2)}) %collective-permute-start.31) | collective-permute-done | bytes 360480 | tf_op jit(solution)/shard_map/ppermute | solution.py:347
  122.5 12.0 %newton_schulz.1 = (bf16[704,2048]{1,0:T(8,128)(2,1)S(1)}, bf16[264,704]{1,0:T(8,128)(2,1)S(1)}, bf16[176,2048]{1,0:T(8,128)(2,1)S(1)}, bf16[88,2048]{1,0:T(8,12...) custom-call(bf16[704,2048]{1,0:T(8,128)(2,1)S(1)} %get-tuple-element, ...), custom_call_target="tpu_custom_call", output_to_operand_aliasing={{0}: (0, {})} | custom-call | flops 10340532224 | bytes 5767168 | tf_op jit(solution)/shard_map/newton_schulz/pallas_call | solution.py:493
  139.5 21.3 %collective-permute-done.35.passing_ref.refs_1_ = bf16[176,2048]{1,0:T(8,128)(2,1)S(1)} collective-permute-done((bf16[176,2048]{1,0:T(8,128)(2,1)S(1)}, bf16[176,2048]{1,0:T(8,128)(2,1)S(1)}, u32[]{:S(2)}, u32[]{:S(2)}) %collective-permute-start.35) | collective-permute-done | bytes 720928 | tf_op jit(solution)/shard_map/ppermute | solution.py:347
  164.2 1.7 momentum_step.1
  165.9 4.7 %collective-permute-done.40.refs_6_ = bf16[88,2048]{1,0:T(8,128)(2,1)S(1)} collective-permute-done((bf16[88,2048]{1,0:T(8,128)(2,1)S(1)}, bf16[88,2048]{1,0:T(8,128)(2,1)S(1)}, u32[]{:S(2)}, u32[]{:S(2)}) %collective-permute-start.40) | collective-permute-done | bytes 360480 | tf_op jit(solution)/shard_map/ppermute | solution.py:347
  (76 shorter events, 53.1 us)
Async XLA Ops:
  1.9 11.8 %collective-permute-start.3 = (bf16[3,88,640]{2,1,0:T(8,128)(2,1)S(1)}, bf16[3,88,640]{2,1,0:T(8,128)(2,1)S(1)}, u32[]{:S(2)}, u32[]{:S(2)}) collective-permute-start(bf16[3,88,640]{2,1,0:T(8,128)(2,1)S(1)} %get-tuple-element.116), channel_id=1, source_target_pairs={{8,0},{16,8},{24,16},{28,24},{20,28},{12,20},{4,12},{0,4},{9,1},{1... | collective-permute-start | bytes 1013768 | tf_op jit(solution)/shard_map/ppermute | solution.py:80
  4.9 10.9 %collective-permute-start.2 = (bf16[3,88,640]{2,1,0:T(8,128)(2,1)S(1)}, bf16[3,88,640]{2,1,0:T(8,128)(2,1)S(1)}, u32[]{:S(2)}, u32[]{:S(2)}) collective-permute-start(bf16[3,88,640]{2,1,0:T(8,128)(2,1)S(1)} %get-tuple-element.117), channel_id=1, source_target_pairs={{0,8},{8,16},{16,24},{24,28},{28,20},{20,12},{12,4},{4,0},{1,9},{9... | collective-permute-start | bytes 1013768 | tf_op jit(solution)/shard_map/ppermute | solution.py:80
  6.1 13.0 %collective-permute-start.1 = (bf16[3,88,384]{2,1,0:T(8,128)(2,1)S(1)}, bf16[3,88,384]{2,1,0:T(8,128)(2,1)S(1)}, u32[]{:S(2)}, u32[]{:S(2)}) collective-permute-start(bf16[3,88,384]{2,1,0:T(8,128)(2,1)S(1)} %get-tuple-element.118), channel_id=1, source_target_pairs={{8,0},{16,8},{24,16},{28,24},{20,28},{12,20},{4,12},{0,4},{9,1},{1... | collective-permute-start | bytes 608264 | tf_op jit(solution)/shard_map/ppermute | solution.py:80
  8.1 11.0 %collective-permute-start = (bf16[3,88,384]{2,1,0:T(8,128)(2,1)S(1)}, bf16[3,88,384]{2,1,0:T(8,128)(2,1)S(1)}, u32[]{:S(2)}, u32[]{:S(2)}) collective-permute-start(bf16[3,88,384]{2,1,0:T(8,128)(2,1)S(1)} %get-tuple-element.119), channel_id=1, source_target_pairs={{0,8},{8,16},{16,24},{24,28},{28,20},{20,12},{12,4},{4,0},{1,9},{9... | collective-permute-start | bytes 608264 | tf_op jit(solution)/shard_map/ppermute | solution.py:80
  17.0 9.6 %collective-permute-start.7 = (bf16[3,88,640]{2,1,0:T(8,128)(2,1)S(1)}, bf16[3,88,640]{2,1,0:T(8,128)(2,1)S(1)}, u32[]{:S(2)}, u32[]{:S(2)}) collective-permute-start(bf16[3,88,640]{2,1,0:T(8,128)(2,1)S(1)} %get-tuple-element.114), channel_id=1, source_target_pairs={{8,0},{16,8},{24,16},{28,24},{20,28},{12,20},{4,12},{0,4},{9,1},{1... | collective-permute-start | bytes 1013768 | tf_op jit(solution)/shard_map/ppermute | solution.py:80
  18.6 9.8 %collective-permute-start.6 = (bf16[3,88,640]{2,1,0:T(8,128)(2,1)S(1)}, bf16[3,88,640]{2,1,0:T(8,128)(2,1)S(1)}, u32[]{:S(2)}, u32[]{:S(2)}) collective-permute-start(bf16[3,88,640]{2,1,0:T(8,128)(2,1)S(1)} %get-tuple-element.115), channel_id=1, source_target_pairs={{0,8},{8,16},{16,24},{24,28},{28,20},{20,12},{12,4},{4,0},{1,9},{9... | collective-permute-start | bytes 1013768 | tf_op jit(solution)/shard_map/ppermute | solution.py:80
  20.3 11.6 %collective-permute-start.5 = (bf16[3,88,384]{2,1,0:T(8,128)(2,1)S(1)}, bf16[3,88,384]{2,1,0:T(8,128)(2,1)S(1)}, u32[]{:S(2)}, u32[]{:S(2)}) collective-permute-start(bf16[3,88,384]{2,1,0:T(8,128)(2,1)S(1)} %get-tuple-element.112), channel_id=1, source_target_pairs={{8,0},{16,8},{24,16},{28,24},{20,28},{12,20},{4,12},{0,4},{9,1},{1... | collective-permute-start | bytes 608264 | tf_op jit(solution)/shard_map/ppermute | solution.py:80
  21.9 10.9 %collective-permute-start.4 = (bf16[3,88,384]{2,1,0:T(8,128)(2,1)S(1)}, bf16[3,88,384]{2,1,0:T(8,128)(2,1)S(1)}, u32[]{:S(2)}, u32[]{:S(2)}) collective-permute-start(bf16[3,88,384]{2,1,0:T(8,128)(2,1)S(1)} %get-tuple-element.113), channel_id=1, source_target_pairs={{0,8},{8,16},{16,24},{24,28},{28,20},{20,12},{12,4},{4,0},{1,9},{9... | collective-permute-start | bytes 608264 | tf_op jit(solution)/shard_map/ppermute | solution.py:80
  29.7 8.8 %collective-permute-start.11 = (bf16[3,88,640]{2,1,0:T(8,128)(2,1)S(1)}, bf16[3,88,640]{2,1,0:T(8,128)(2,1)S(1)}, u32[]{:S(2)}, u32[]{:S(2)}) collective-permute-start(bf16[3,88,640]{2,1,0:T(8,128)(2,1)S(1)} %get-tuple-element.110), channel_id=1, source_target_pairs={{8,0},{16,8},{24,16},{28,24},{20,28},{12,20},{4,12},{0,4},{9,1},{1... | collective-permute-start | bytes 1013768 | tf_op jit(solution)/shard_map/ppermute | solution.py:80
  30.9 9.1 %collective-permute-start.10 = (bf16[3,88,640]{2,1,0:T(8,128)(2,1)S(1)}, bf16[3,88,640]{2,1,0:T(8,128)(2,1)S(1)}, u32[]{:S(2)}, u32[]{:S(2)}) collective-permute-start(bf16[3,88,640]{2,1,0:T(8,128)(2,1)S(1)} %get-tuple-element.111), channel_id=1, source_target_pairs={{0,8},{8,16},{16,24},{24,28},{28,20},{20,12},{12,4},{4,0},{1,9},{9... | collective-permute-start | bytes 1013768 | tf_op jit(solution)/shard_map/ppermute | solution.py:80
  34.0 9.4 %collective-permute-start.9 = (bf16[3,88,384]{2,1,0:T(8,128)(2,1)S(1)}, bf16[3,88,384]{2,1,0:T(8,128)(2,1)S(1)}, u32[]{:S(2)}, u32[]{:S(2)}) collective-permute-start(bf16[3,88,384]{2,1,0:T(8,128)(2,1)S(1)} %get-tuple-element.108), channel_id=1, source_target_pairs={{8,0},{16,8},{24,16},{28,24},{20,28},{12,20},{4,12},{0,4},{9,1},{1... | collective-permute-start | bytes 608264 | tf_op jit(solution)/shard_map/ppermute | solution.py:80
  34.7 9.7 %collective-permute-start.8 = (bf16[3,88,384]{2,1,0:T(8,128)(2,1)S(1)}, bf16[3,88,384]{2,1,0:T(8,128)(2,1)S(1)}, u32[]{:S(2)}, u32[]{:S(2)}) collective-permute-start(bf16[3,88,384]{2,1,0:T(8,128)(2,1)S(1)} %get-tuple-element.109), channel_id=1, source_target_pairs={{0,8},{8,16},{16,24},{24,28},{28,20},{20,12},{12,4},{4,0},{1,9},{9... | collective-permute-start | bytes 608264 | tf_op jit(solution)/shard_map/ppermute | solution.py:80
  41.3 8.8 %collective-permute-start.15 = (bf16[3,88,640]{2,1,0:T(8,128)(2,1)S(1)}, bf16[3,88,640]{2,1,0:T(8,128)(2,1)S(1)}, u32[]{:S(2)}, u32[]{:S(2)}) collective-permute-start(bf16[3,88,640]{2,1,0:T(8,128)(2,1)S(1)} %get-tuple-element.106), channel_id=1, source_target_pairs={{8,0},{16,8},{24,16},{28,24},{20,28},{12,20},{4,12},{0,4},{9,1},{1... | collective-permute-start | bytes 1013768 | tf_op jit(solution)/shard_map/ppermute | solution.py:80
  45.5 9.4 %collective-permute-start.13 = (bf16[3,88,384]{2,1,0:T(8,128)(2,1)S(1)}, bf16[3,88,384]{2,1,0:T(8,128)(2,1)S(1)}, u32[]{:S(2)}, u32[]{:S(2)}) collective-permute-start(bf16[3,88,384]{2,1,0:T(8,128)(2,1)S(1)} %get-tuple-element.104), channel_id=1, source_target_pairs={{8,0},{16,8},{24,16},{28,24},{20,28},{12,20},{4,12},{0,4},{9,1},{1... | collective-permute-start | bytes 608264 | tf_op jit(solution)/shard_map/ppermute | solution.py:80
  47.2 8.8 %collective-permute-start.12 = (bf16[3,88,384]{2,1,0:T(8,128)(2,1)S(1)}, bf16[3,88,384]{2,1,0:T(8,128)(2,1)S(1)}, u32[]{:S(2)}, u32[]{:S(2)}) collective-permute-start(bf16[3,88,384]{2,1,0:T(8,128)(2,1)S(1)} %get-tuple-element.105), channel_id=1, source_target_pairs={{0,8},{8,16},{16,24},{24,28},{28,20},{20,12},{12,4},{4,0},{1,9},{9... | collective-permute-start | bytes 608264 | tf_op jit(solution)/shard_map/ppermute | solution.py:80
  52.9 8.8 %collective-permute-start.19 = (bf16[3,88,640]{2,1,0:T(8,128)(2,1)S(1)}, bf16[3,88,640]{2,1,0:T(8,128)(2,1)S(1)}, u32[]{:S(2)}, u32[]{:S(2)}) collective-permute-start(bf16[3,88,640]{2,1,0:T(8,128)(2,1)S(1)} %get-tuple-element.102), channel_id=1, source_target_pairs={{8,0},{16,8},{24,16},{28,24},{20,28},{12,20},{4,12},{0,4},{9,1},{1... | collective-permute-start | bytes 1013768 | tf_op jit(solution)/shard_map/ppermute | solution.py:80
  57.1 9.4 %collective-permute-start.17 = (bf16[3,88,384]{2,1,0:T(8,128)(2,1)S(1)}, bf16[3,88,384]{2,1,0:T(8,128)(2,1)S(1)}, u32[]{:S(2)}, u32[]{:S(2)}) collective-permute-start(bf16[3,88,384]{2,1,0:T(8,128)(2,1)S(1)} %get-tuple-element.100), channel_id=1, source_target_pairs={{8,0},{16,8},{24,16},{28,24},{20,28},{12,20},{4,12},{0,4},{9,1},{1... | collective-permute-start | bytes 608264 | tf_op jit(solution)/shard_map/ppermute | solution.py:80
  58.8 8.8 %collective-permute-start.16 = (bf16[3,88,384]{2,1,0:T(8,128)(2,1)S(1)}, bf16[3,88,384]{2,1,0:T(8,128)(2,1)S(1)}, u32[]{:S(2)}, u32[]{:S(2)}) collective-permute-start(bf16[3,88,384]{2,1,0:T(8,128)(2,1)S(1)} %get-tuple-element.101), channel_id=1, source_target_pairs={{0,8},{8,16},{16,24},{24,28},{28,20},{20,12},{12,4},{4,0},{1,9},{9... | collective-permute-start | bytes 608264 | tf_op jit(solution)/shard_map/ppermute | solution.py:80
  64.5 8.8 %collective-permute-start.23 = (bf16[3,88,640]{2,1,0:T(8,128)(2,1)S(1)}, bf16[3,88,640]{2,1,0:T(8,128)(2,1)S(1)}, u32[]{:S(2)}, u32[]{:S(2)}) collective-permute-start(bf16[3,88,640]{2,1,0:T(8,128)(2,1)S(1)} %get-tuple-element.98), channel_id=1, source_target_pairs={{8,0},{16,8},{24,16},{28,24},{20,28},{12,20},{4,12},{0,4},{9,1},{1... | collective-permute-start | bytes 1013768 | tf_op jit(solution)/shard_map/ppermute | solution.py:80
  68.7 9.4 %collective-permute-start.21 = (bf16[3,88,384]{2,1,0:T(8,128)(2,1)S(1)}, bf16[3,88,384]{2,1,0:T(8,128)(2,1)S(1)}, u32[]{:S(2)}, u32[]{:S(2)}) collective-permute-start(bf16[3,88,384]{2,1,0:T(8,128)(2,1)S(1)} %get-tuple-element.96), channel_id=1, source_target_pairs={{8,0},{16,8},{24,16},{28,24},{20,28},{12,20},{4,12},{0,4},{9,1},{1... | collective-permute-start | bytes 608264 | tf_op jit(solution)/shard_map/ppermute | solution.py:80
  70.4 8.8 %collective-permute-start.20 = (bf16[3,88,384]{2,1,0:T(8,128)(2,1)S(1)}, bf16[3,88,384]{2,1,0:T(8,128)(2,1)S(1)}, u32[]{:S(2)}, u32[]{:S(2)}) collective-permute-start(bf16[3,88,384]{2,1,0:T(8,128)(2,1)S(1)} %get-tuple-element.97), channel_id=1, source_target_pairs={{0,8},{8,16},{16,24},{24,28},{28,20},{20,12},{12,4},{4,0},{1,9},{9... | collective-permute-start | bytes 608264 | tf_op jit(solution)/shard_map/ppermute | solution.py:80
  103.4 10.0 %collective-permute-start.29 = (bf16[88,2048]{1,0:T(8,128)(2,1)S(1)}, bf16[88,2048]{1,0:T(8,128)(2,1)S(1)}, u32[]{:S(2)}, u32[]{:S(2)}) collective-permute-start(bf16[88,2048]{1,0:T(8,128)(2,1)S(1)} %get-tuple-element.70), channel_id=1, source_target_pairs={{24,8},{0,16},{20,4},{29,13},{5,21},{9,25},{26,10},{2,18},{22,6},{... | collective-permute-start | bytes 1081352 | tf_op jit(solution)/shard_map/ppermute | solution.py:347
  104.7 9.5 %collective-permute-start.30 = (bf16[88,2048]{1,0:T(8,128)(2,1)S(1)}, bf16[88,2048]{1,0:T(8,128)(2,1)S(1)}, u32[]{:S(2)}, u32[]{:S(2)}) collective-permute-start(bf16[88,2048]{1,0:T(8,128)(2,1)S(1)} %get-tuple-element.71), channel_id=1, source_target_pairs={{28,8},{4,16},{16,4},{25,13},{1,21},{13,25},{30,10},{6,18},{18,6},... | collective-permute-start | bytes 1081352 | tf_op jit(solution)/shard_map/ppermute | solution.py:347
  105.4 15.7 %collective-permute-start.31 = (bf16[88,2048]{1,0:T(8,128)(2,1)S(1)}, bf16[88,2048]{1,0:T(8,128)(2,1)S(1)}, u32[]{:S(2)}, u32[]{:S(2)}) collective-permute-start(bf16[88,2048]{1,0:T(8,128)(2,1)S(1)} %get-tuple-element.72), channel_id=1, source_target_pairs={{0,8},{24,16},{12,4},{5,13},{29,21},{17,25},{2,10},{26,18},{14,6},... | collective-permute-start | bytes 1081352 | tf_op jit(solution)/shard_map/ppermute | solution.py:347
  107.3 13.8 %collective-permute-start.32 = (bf16[88,2048]{1,0:T(8,128)(2,1)S(1)}, bf16[88,2048]{1,0:T(8,128)(2,1)S(1)}, u32[]{:S(2)}, u32[]{:S(2)}) collective-permute-start(bf16[88,2048]{1,0:T(8,128)(2,1)S(1)} %get-tuple-element.73), channel_id=1, source_target_pairs={{4,8},{28,16},{8,4},{1,13},{25,21},{21,25},{6,10},{30,18},{10,6},{... | collective-permute-start | bytes 1081352 | tf_op jit(solution)/shard_map/ppermute | solution.py:347
  108.3 14.2 %collective-permute-start.33 = (bf16[88,2048]{1,0:T(8,128)(2,1)S(1)}, bf16[88,2048]{1,0:T(8,128)(2,1)S(1)}, u32[]{:S(2)}, u32[]{:S(2)}) collective-permute-start(bf16[88,2048]{1,0:T(8,128)(2,1)S(1)} %get-tuple-element.77), channel_id=1, source_target_pairs={{16,8},{8,16},{28,4},{21,13},{13,21},{1,25},{18,10},{10,18},{30,6}... | collective-permute-start | bytes 1081352 | tf_op jit(solution)/shard_map/ppermute | solution.py:347
  113.4 9.1 %collective-permute-start.34 = (bf16[88,2048]{1,0:T(8,128)(2,1)S(1)}, bf16[88,2048]{1,0:T(8,128)(2,1)S(1)}, u32[]{:S(2)}, u32[]{:S(2)}) collective-permute-start(bf16[88,2048]{1,0:T(8,128)(2,1)S(1)} %get-tuple-element.79), channel_id=1, source_target_pairs={{20,8},{12,16},{24,4},{17,13},{9,21},{5,25},{22,10},{14,18},{26,6}... | collective-permute-start | bytes 1081352 | tf_op jit(solution)/shard_map/ppermute | solution.py:347
  134.5 26.3 %collective-permute-start.35 = (bf16[176,2048]{1,0:T(8,128)(2,1)S(1)}, bf16[176,2048]{1,0:T(8,128)(2,1)S(1)}, u32[]{:S(2)}, u32[]{:S(2)}) collective-permute-start(bf16[176,2048]{1,0:T(8,128)(2,1)S(1)} %get-tuple-element.83), channel_id=1, source_target_pairs={{8,12},{16,20},{4,0},{13,9},{21,17},{25,29},{10,14},{18,22},{6,2},... | collective-permute-start | bytes 2162696 | tf_op jit(solution)/shard_map/ppermute | solution.py:347
  135.8 27.0 %collective-permute-start.36 = (bf16[88,2048]{1,0:T(8,128)(2,1)S(1)}, bf16[88,2048]{1,0:T(8,128)(2,1)S(1)}, u32[]{:S(2)}, u32[]{:S(2)}) collective-permute-start(bf16[88,2048]{1,0:T(8,128)(2,1)S(1)} %get-tuple-element.84), channel_id=1, source_target_pairs={{8,24},{16,0},{4,20},{13,29},{21,5},{25,9},{10,26},{18,2},{6,22},{... | collective-permute-start | bytes 1081352 | tf_op jit(solution)/shard_map/ppermute | solution.py:347
  137.1 28.8 %collective-permute-start.37 = (bf16[88,2048]{1,0:T(8,128)(2,1)S(1)}, bf16[88,2048]{1,0:T(8,128)(2,1)S(1)}, u32[]{:S(2)}, u32[]{:S(2)}) collective-permute-start(bf16[88,2048]{1,0:T(8,128)(2,1)S(1)} %get-tuple-element.85), channel_id=1, source_target_pairs={{8,28},{16,4},{4,16},{13,25},{21,1},{25,13},{10,30},{18,6},{6,18},... | collective-permute-start | bytes 1081352 | tf_op jit(solution)/shard_map/ppermute | solution.py:347
  137.8 28.1 %collective-permute-start.38 = (bf16[88,2048]{1,0:T(8,128)(2,1)S(1)}, bf16[88,2048]{1,0:T(8,128)(2,1)S(1)}, u32[]{:S(2)}, u32[]{:S(2)}) collective-permute-start(bf16[88,2048]{1,0:T(8,128)(2,1)S(1)} %get-tuple-element.86), channel_id=1, source_target_pairs={{8,16},{16,8},{4,28},{13,21},{21,13},{25,1},{10,18},{18,10},{6,30}... | collective-permute-start | bytes 1081352 | tf_op jit(solution)/shard_map/ppermute | solution.py:347
  160.8 9.7 %collective-permute-start.40 = (bf16[88,2048]{1,0:T(8,128)(2,1)S(1)}, bf16[88,2048]{1,0:T(8,128)(2,1)S(1)}, u32[]{:S(2)}, u32[]{:S(2)}) collective-permute-start(bf16[88,2048]{1,0:T(8,128)(2,1)S(1)} %get-tuple-element.89), channel_id=1, source_target_pairs={{8,0},{16,24},{4,12},{13,5},{21,29},{25,17},{10,2},{18,26},{6,14},... | collective-permute-start | bytes 1081352 | tf_op jit(solution)/shard_map/ppermute | solution.py:347
  (10 other events, 80.4 us)

commit v6 on v5

--- a/solution.py
+++ b/solution.py
@@ -323,13 +323,14 @@
 def rounds_of(ranks, back):
     if ranks != 8:
         return list(range(ranks)), {}
-    return ([0, 1, 4, 5, 6, 7, 2, 3], {2: (1,), 3: (1,)}) if back else ([0, 1, 4, 5, 6, 7, 2, 3], {6: (1,), 7: (1,)})
+    return ([0, 1, 7, 4, 5, 6, 2, 3], {2: (1,), 3: (1,)}) if back else ([0, 1, 4, 5, 6, 7, 2, 3], {6: (1,), 7: (1,)})
 
 
 def exchange(pieces, axes, owners, ranks, experts, relays=None):
     back = relays is not None
     order, after = rounds_of(ranks, back)
     by_way = back and any(relays)
+    passed = []
     out = {0: pieces[0]}
     for at, step in enumerate(order):
         if step == 0:
@@ -342,8 +343,10 @@
             hops = {o * experts + e: (o ^ 1) * experts + e for e in range(experts) for o in relays[e % 2]}
             pairs = [(hops.get(a, a), b) for a, b in pairs]
             piece = relay_rows(out[1], piece, relays, axes)
+            passed = [piece]
         if step in after:
-            piece, *_ = lax.optimization_barrier((piece, *[out[x] for x in after[step]]))
+            waits = [out[x] for x in after[step]] + passed
+            piece, *_ = lax.optimization_barrier((piece, *waits))
         out[step] = lax.ppermute(piece, axes, pairs)
     return [out[step] for step in order]
 
@@ -456,7 +459,12 @@
         diagonal = lax.broadcasted_iota(jnp.int32, a.shape, 0) == lax.broadcasted_iota(
             jnp.int32, a.shape, 1
         )
-        norm = jnp.sqrt(jnp.sum(jnp.where(diagonal, a[...], 0.0)))
+        squares = jnp.zeros((1, 1), F32)
+        for c in range(0, whole, 128):
+            n = min(128, whole - c)
+            block = jnp.where(diagonal[:n, :n], a[c : c + n, c : c + n], 0.0)
+            squares = squares + jnp.sum(block, keepdims=True)
+        norm = jnp.sqrt(squares)
         inv = 1.0 / (norm + 1e-07)
         a[...] = (a[...] * inv) * inv
         for step in range(NS_ITERS):

time: 175 us -> 175 us (level)
  transfers between devices with their start and end apart: 42 -> 42, of which waited for: 25 -> 26; matrix products, arithmetic and copies ran while one was open for 9% -> 9% of each run, Pallas kernels for 4% -> 4%
where the time goes in v6:
time: 175 us; the launch traced here: 172 us
  waiting for transfers between devices  76.3 us (44%)
  starting transfers between devices  46 us (26%)
  Pallas kernels  20.4 us (12%)
  other arithmetic  14.4 us (8%)
  blocking collectives  11.7 us (7%)
  local copies, waits for them, and re-layouts  2.23 us (1%)
    ppermute x28, waiting for transfers between devices, ring_reduce_scatter(): got = {d: lax.ppermute(acc[g, d], axis, perms[d]) for d in (1, -1)}  38.8 us
    ppermute x14, waiting for transfers between devices, exchange(): out[step] = lax.ppermute(piece, axes, pairs)  37.5 us
    ppermute x28, starting transfers between devices, ring_reduce_scatter(): got = {d: lax.ppermute(acc[g, d], axis, perms[d]) for d in (1, -1)}  30.2 us
    ppermute x14, starting transfers between devices, exchange(): out[step] = lax.ppermute(piece, axes, pairs)  15.8 us
    convert_element_type x12, other arithmetic, ring_reduce_scatter(): (got[d].astype(F32) + piece(g, d, step).astype(F32)).astype(BF16)  14.4 us
    pallas_call x1, Pallas kernels, newton_schulz(): pl.pallas_call(body, out_shape=[jax.ShapeDtypeStruct((whole, columns), BF...  12 us
    all_to_all x1, blocking collectives, local(): squares = lax.all_to_all(square, both, 0, 0, tiled=True)  11.7 us
  transfers between devices with their start and end apart: 42, of which 26 were waited for; matrix products, arithmetic and copies ran while one was open for 9% of the time, Pallas kernels for 4%

profile of v6, /device:TPU:0, one launch (start us, length us, event | category | flops | bytes accessed | tf_op | source)
XLA Modules:
  0.0 172.1 jit_solution(4478222012901485201)
XLA Ops:
  1.9 3.0 %collective-permute-start.3 = (bf16[3,88,640]{2,1,0:T(8,128)(2,1)S(1)}, bf16[3,88,640]{2,1,0:T(8,128)(2,1)S(1)}, u32[]{:S(2)}, u32[]{:S(2)}) collective-permute-start(bf16[3,88,640]{2,1,0:T(8,128)(2,1)S(1)} %get-tuple-element.116), channel_id=1, source_target_pairs={{8,0},{16,8},{24,16},{28,24},{20,28},{12,20},{4,12},{0,4},{9,1},{1... | collective-permute-start | bytes 1013768 | tf_op jit(solution)/shard_map/ppermute | solution.py:80
  6.1 2.0 %collective-permute-start.1 = (bf16[3,88,384]{2,1,0:T(8,128)(2,1)S(1)}, bf16[3,88,384]{2,1,0:T(8,128)(2,1)S(1)}, u32[]{:S(2)}, u32[]{:S(2)}) collective-permute-start(bf16[3,88,384]{2,1,0:T(8,128)(2,1)S(1)} %get-tuple-element.118), channel_id=1, source_target_pairs={{8,0},{16,8},{24,16},{28,24},{20,28},{12,20},{4,12},{0,4},{9,1},{1... | collective-permute-start | bytes 608264 | tf_op jit(solution)/shard_map/ppermute | solution.py:80
  8.2 5.5 %collective-permute-done.3 = bf16[3,88,640]{2,1,0:T(8,128)(2,1)S(1)} collective-permute-done((bf16[3,88,640]{2,1,0:T(8,128)(2,1)S(1)}, bf16[3,88,640]{2,1,0:T(8,128)(2,1)S(1)}, u32[]{:S(2)}, u32[]{:S(2)}) %collective-permute-start.3) | collective-permute-done | bytes 337952 | tf_op jit(solution)/shard_map/ppermute | solution.py:80
  13.7 2.0 %collective-permute-done.2 = bf16[3,88,640]{2,1,0:T(8,128)(2,1)S(1)} collective-permute-done((bf16[3,88,640]{2,1,0:T(8,128)(2,1)S(1)}, bf16[3,88,640]{2,1,0:T(8,128)(2,1)S(1)}, u32[]{:S(2)}, u32[]{:S(2)}) %collective-permute-start.2) | collective-permute-done | bytes 337952 | tf_op jit(solution)/shard_map/ppermute | solution.py:80
  17.0 1.6 collective-permute-start.7
  20.3 1.6 collective-permute-start.5
  22.3 4.3 %collective-permute-done.7 = bf16[3,88,640]{2,1,0:T(8,128)(2,1)S(1)} collective-permute-done((bf16[3,88,640]{2,1,0:T(8,128)(2,1)S(1)}, bf16[3,88,640]{2,1,0:T(8,128)(2,1)S(1)}, u32[]{:S(2)}, u32[]{:S(2)}) %collective-permute-start.7) | collective-permute-done | bytes 337952 | tf_op jit(solution)/shard_map/ppermute | solution.py:80
  26.7 1.8 %collective-permute-done.6 = bf16[3,88,640]{2,1,0:T(8,128)(2,1)S(1)} collective-permute-done((bf16[3,88,640]{2,1,0:T(8,128)(2,1)S(1)}, bf16[3,88,640]{2,1,0:T(8,128)(2,1)S(1)}, u32[]{:S(2)}, u32[]{:S(2)}) %collective-permute-start.6) | collective-permute-done | bytes 337952 | tf_op jit(solution)/shard_map/ppermute | solution.py:80
  36.0 2.5 %collective-permute-done.11 = bf16[3,88,640]{2,1,0:T(8,128)(2,1)S(1)} collective-permute-done((bf16[3,88,640]{2,1,0:T(8,128)(2,1)S(1)}, bf16[3,88,640]{2,1,0:T(8,128)(2,1)S(1)}, u32[]{:S(2)}, u32[]{:S(2)}) %collective-permute-start.11) | collective-permute-done | bytes 337952 | tf_op jit(solution)/shard_map/ppermute | solution.py:80
  41.3 1.6 collective-permute-start.15
  45.5 1.6 collective-permute-start.13
  47.6 2.5 %collective-permute-done.15 = bf16[3,88,640]{2,1,0:T(8,128)(2,1)S(1)} collective-permute-done((bf16[3,88,640]{2,1,0:T(8,128)(2,1)S(1)}, bf16[3,88,640]{2,1,0:T(8,128)(2,1)S(1)}, u32[]{:S(2)}, u32[]{:S(2)}) %collective-permute-start.15) | collective-permute-done | bytes 337952 | tf_op jit(solution)/shard_map/ppermute | solution.py:80
  52.9 1.6 collective-permute-start.19
  57.1 1.6 collective-permute-start.17
  59.2 2.5 %collective-permute-done.19 = bf16[3,88,640]{2,1,0:T(8,128)(2,1)S(1)} collective-permute-done((bf16[3,88,640]{2,1,0:T(8,128)(2,1)S(1)}, bf16[3,88,640]{2,1,0:T(8,128)(2,1)S(1)}, u32[]{:S(2)}, u32[]{:S(2)}) %collective-permute-start.19) | collective-permute-done | bytes 337952 | tf_op jit(solution)/shard_map/ppermute | solution.py:80
  61.7 1.5 collective-permute-done.18
  64.5 1.6 collective-permute-start.23
  68.7 1.6 collective-permute-start.21
  70.8 2.5 %collective-permute-done.23 = bf16[3,88,640]{2,1,0:T(8,128)(2,1)S(1)} collective-permute-done((bf16[3,88,640]{2,1,0:T(8,128)(2,1)S(1)}, bf16[3,88,640]{2,1,0:T(8,128)(2,1)S(1)}, u32[]{:S(2)}, u32[]{:S(2)}) %collective-permute-start.23) | collective-permute-done | bytes 337952 | tf_op jit(solution)/shard_map/ppermute | solution.py:80
  76.1 1.7 collective-permute-start.27
  80.3 1.7 %collective-permute-start.25 = (bf16[3,88,384]{2,1,0:T(8,128)(2,1)S(1)}, bf16[3,88,384]{2,1,0:T(8,128)(2,1)S(1)}, u32[]{:S(2)}, u32[]{:S(2)}) collective-permute-start(bf16[3,88,384]{2,1,0:T(8,128)(2,1)S(1)} %get-tuple-element.92), channel_id=1, source_target_pairs={{8,0},{16,8},{24,16},{28,24},{20,28},{12,20},{4,12},{0,4},{9,1},{1... | collective-permute-start | bytes 608264 | tf_op jit(solution)/shard_map/ppermute | solution.py:80
  82.4 2.2 %collective-permute-done.27.refs_1_ = bf16[3,88,640]{2,1,0:T(8,128)(2,1)S(1)} collective-permute-done((bf16[3,88,640]{2,1,0:T(8,128)(2,1)S(1)}, bf16[3,88,640]{2,1,0:T(8,128)(2,1)S(1)}, u32[]{:S(2)}, u32[]{:S(2)}) %collective-permute-start.27) | collective-permute-done | bytes 337952 | tf_op jit(solution)/shard_map/ppermute | solution.py:80
  86.0 2.0 %add_and_square.2 = (f32[3,88,640]{2,1,0:T(8,128)S(1)}, f32[3,88,640]{2,1,0:T(8,128)S(1)}, f32[88,128]{1,0:T(8,128)S(1)}, bf16[3,88,384]{2,1,0:T(8,128)(2,1)S(1)...) custom-call(bf16[3,88,640]{2,1,0:T(8,128)(2,1)S(1)} %collective-permute-done.26.refs_0_, ...), custom_call_target="tpu_custom_call" | custom-call | tf_op jit(solution)/shard_map/add_and_square/pallas_call | solution.py:155
  88.7 11.7 %all_to_all.5.squares_ref = f32[32,1,128]{2,1,0:T(1,128)S(1)} all-to-all(f32[32,1,128]{2,1,0:T(1,128)S(1)} %get-tuple-element.62), channel_id=1, replica_groups=mesh['dp'=8,'expert'=4] {'dp','expert'}, dimensions={0} | all-to-all | bytes 32768 | tf_op jit(solution)/shard_map/all_to_all | solution.py:550
  100.9 2.5 %collective-permute-start.28 = (bf16[88,2048]{1,0:T(8,128)(2,1)S(1)}, bf16[88,2048]{1,0:T(8,128)(2,1)S(1)}, u32[]{:S(2)}, u32[]{:S(2)}) collective-permute-start(bf16[88,2048]{1,0:T(8,128)(2,1)S(1)} %get-tuple-element.69), channel_id=1, source_target_pairs={{12,8},{20,16},{0,4},{9,13},{17,21},{29,25},{14,10},{22,18},{2,6},... | collective-permute-start | bytes 1081352 | tf_op jit(solution)/shard_map/ppermute | solution.py:350
  105.4 1.9 %collective-permute-start.31 = (bf16[88,2048]{1,0:T(8,128)(2,1)S(1)}, bf16[88,2048]{1,0:T(8,128)(2,1)S(1)}, u32[]{:S(2)}, u32[]{:S(2)}) collective-permute-start(bf16[88,2048]{1,0:T(8,128)(2,1)S(1)} %get-tuple-element.72), channel_id=1, source_target_pairs={{0,8},{24,16},{12,4},{5,13},{29,21},{17,25},{2,10},{26,18},{14,6},... | collective-permute-start | bytes 1081352 | tf_op jit(solution)/shard_map/ppermute | solution.py:350
  109.0 4.4 %collective-permute-done.29.refs_2_ = bf16[88,2048]{1,0:T(8,128)(2,1)S(1)} collective-permute-done((bf16[88,2048]{1,0:T(8,128)(2,1)S(1)}, bf16[88,2048]{1,0:T(8,128)(2,1)S(1)}, u32[]{:S(2)}, u32[]{:S(2)}) %collective-permute-start.29) | collective-permute-done | bytes 360480 | tf_op jit(solution)/shard_map/ppermute | solution.py:350
  114.3 6.9 %collective-permute-done.31.refs_4_ = bf16[88,2048]{1,0:T(8,128)(2,1)S(1)} collective-permute-done((bf16[88,2048]{1,0:T(8,128)(2,1)S(1)}, bf16[88,2048]{1,0:T(8,128)(2,1)S(1)}, u32[]{:S(2)}, u32[]{:S(2)}) %collective-permute-start.31) | collective-permute-done | bytes 360480 | tf_op jit(solution)/shard_map/ppermute | solution.py:350
  122.5 12.0 %newton_schulz.1 = (bf16[704,2048]{1,0:T(8,128)(2,1)S(1)}, bf16[264,704]{1,0:T(8,128)(2,1)S(1)}, bf16[176,2048]{1,0:T(8,128)(2,1)S(1)}, bf16[88,2048]{1,0:T(8,12...) custom-call(bf16[704,2048]{1,0:T(8,128)(2,1)S(1)} %get-tuple-element, ...), custom_call_target="tpu_custom_call", output_to_operand_aliasing={{0}: (0, {})} | custom-call | flops 10340532224 | bytes 5767168 | tf_op jit(solution)/shard_map/newton_schulz/pallas_call | solution.py:501
  139.5 21.2 %collective-permute-done.35.passing_ref.refs_1_ = bf16[176,2048]{1,0:T(8,128)(2,1)S(1)} collective-permute-done((bf16[176,2048]{1,0:T(8,128)(2,1)S(1)}, bf16[176,2048]{1,0:T(8,128)(2,1)S(1)}, u32[]{:S(2)}, u32[]{:S(2)}) %collective-permute-start.35) | collective-permute-done | bytes 720928 | tf_op jit(solution)/shard_map/ppermute | solution.py:350
  164.1 1.7 momentum_step.1
  165.8 4.7 %collective-permute-done.40.refs_6_ = bf16[88,2048]{1,0:T(8,128)(2,1)S(1)} collective-permute-done((bf16[88,2048]{1,0:T(8,128)(2,1)S(1)}, bf16[88,2048]{1,0:T(8,128)(2,1)S(1)}, u32[]{:S(2)}, u32[]{:S(2)}) %collective-permute-start.40) | collective-permute-done | bytes 360480 | tf_op jit(solution)/shard_map/ppermute | solution.py:350
  (76 shorter events, 53.1 us)
Async XLA Ops:
  1.9 11.8 %collective-permute-start.3 = (bf16[3,88,640]{2,1,0:T(8,128)(2,1)S(1)}, bf16[3,88,640]{2,1,0:T(8,128)(2,1)S(1)}, u32[]{:S(2)}, u32[]{:S(2)}) collective-permute-start(bf16[3,88,640]{2,1,0:T(8,128)(2,1)S(1)} %get-tuple-element.116), channel_id=1, source_target_pairs={{8,0},{16,8},{24,16},{28,24},{20,28},{12,20},{4,12},{0,4},{9,1},{1... | collective-permute-start | bytes 1013768 | tf_op jit(solution)/shard_map/ppermute | solution.py:80
  4.9 10.9 %collective-permute-start.2 = (bf16[3,88,640]{2,1,0:T(8,128)(2,1)S(1)}, bf16[3,88,640]{2,1,0:T(8,128)(2,1)S(1)}, u32[]{:S(2)}, u32[]{:S(2)}) collective-permute-start(bf16[3,88,640]{2,1,0:T(8,128)(2,1)S(1)} %get-tuple-element.117), channel_id=1, source_target_pairs={{0,8},{8,16},{16,24},{24,28},{28,20},{20,12},{12,4},{4,0},{1,9},{9... | collective-permute-start | bytes 1013768 | tf_op jit(solution)/shard_map/ppermute | solution.py:80
  6.1 13.0 %collective-permute-start.1 = (bf16[3,88,384]{2,1,0:T(8,128)(2,1)S(1)}, bf16[3,88,384]{2,1,0:T(8,128)(2,1)S(1)}, u32[]{:S(2)}, u32[]{:S(2)}) collective-permute-start(bf16[3,88,384]{2,1,0:T(8,128)(2,1)S(1)} %get-tuple-element.118), channel_id=1, source_target_pairs={{8,0},{16,8},{24,16},{28,24},{20,28},{12,20},{4,12},{0,4},{9,1},{1... | collective-permute-start | bytes 608264 | tf_op jit(solution)/shard_map/ppermute | solution.py:80
  8.1 11.0 %collective-permute-start = (bf16[3,88,384]{2,1,0:T(8,128)(2,1)S(1)}, bf16[3,88,384]{2,1,0:T(8,128)(2,1)S(1)}, u32[]{:S(2)}, u32[]{:S(2)}) collective-permute-start(bf16[3,88,384]{2,1,0:T(8,128)(2,1)S(1)} %get-tuple-element.119), channel_id=1, source_target_pairs={{0,8},{8,16},{16,24},{24,28},{28,20},{20,12},{12,4},{4,0},{1,9},{9... | collective-permute-start | bytes 608264 | tf_op jit(solution)/shard_map/ppermute | solution.py:80
  17.0 9.6 %collective-permute-start.7 = (bf16[3,88,640]{2,1,0:T(8,128)(2,1)S(1)}, bf16[3,88,640]{2,1,0:T(8,128)(2,1)S(1)}, u32[]{:S(2)}, u32[]{:S(2)}) collective-permute-start(bf16[3,88,640]{2,1,0:T(8,128)(2,1)S(1)} %get-tuple-element.114), channel_id=1, source_target_pairs={{8,0},{16,8},{24,16},{28,24},{20,28},{12,20},{4,12},{0,4},{9,1},{1... | collective-permute-start | bytes 1013768 | tf_op jit(solution)/shard_map/ppermute | solution.py:80
  18.6 9.8 %collective-permute-start.6 = (bf16[3,88,640]{2,1,0:T(8,128)(2,1)S(1)}, bf16[3,88,640]{2,1,0:T(8,128)(2,1)S(1)}, u32[]{:S(2)}, u32[]{:S(2)}) collective-permute-start(bf16[3,88,640]{2,1,0:T(8,128)(2,1)S(1)} %get-tuple-element.115), channel_id=1, source_target_pairs={{0,8},{8,16},{16,24},{24,28},{28,20},{20,12},{12,4},{4,0},{1,9},{9... | collective-permute-start | bytes 1013768 | tf_op jit(solution)/shard_map/ppermute | solution.py:80
  20.3 11.6 %collective-permute-start.5 = (bf16[3,88,384]{2,1,0:T(8,128)(2,1)S(1)}, bf16[3,88,384]{2,1,0:T(8,128)(2,1)S(1)}, u32[]{:S(2)}, u32[]{:S(2)}) collective-permute-start(bf16[3,88,384]{2,1,0:T(8,128)(2,1)S(1)} %get-tuple-element.112), channel_id=1, source_target_pairs={{8,0},{16,8},{24,16},{28,24},{20,28},{12,20},{4,12},{0,4},{9,1},{1... | collective-permute-start | bytes 608264 | tf_op jit(solution)/shard_map/ppermute | solution.py:80
  21.9 10.9 %collective-permute-start.4 = (bf16[3,88,384]{2,1,0:T(8,128)(2,1)S(1)}, bf16[3,88,384]{2,1,0:T(8,128)(2,1)S(1)}, u32[]{:S(2)}, u32[]{:S(2)}) collective-permute-start(bf16[3,88,384]{2,1,0:T(8,128)(2,1)S(1)} %get-tuple-element.113), channel_id=1, source_target_pairs={{0,8},{8,16},{16,24},{24,28},{28,20},{20,12},{12,4},{4,0},{1,9},{9... | collective-permute-start | bytes 608264 | tf_op jit(solution)/shard_map/ppermute | solution.py:80
  29.7 8.8 %collective-permute-start.11 = (bf16[3,88,640]{2,1,0:T(8,128)(2,1)S(1)}, bf16[3,88,640]{2,1,0:T(8,128)(2,1)S(1)}, u32[]{:S(2)}, u32[]{:S(2)}) collective-permute-start(bf16[3,88,640]{2,1,0:T(8,128)(2,1)S(1)} %get-tuple-element.110), channel_id=1, source_target_pairs={{8,0},{16,8},{24,16},{28,24},{20,28},{12,20},{4,12},{0,4},{9,1},{1... | collective-permute-start | bytes 1013768 | tf_op jit(solution)/shard_map/ppermute | solution.py:80
  30.9 9.1 %collective-permute-start.10 = (bf16[3,88,640]{2,1,0:T(8,128)(2,1)S(1)}, bf16[3,88,640]{2,1,0:T(8,128)(2,1)S(1)}, u32[]{:S(2)}, u32[]{:S(2)}) collective-permute-start(bf16[3,88,640]{2,1,0:T(8,128)(2,1)S(1)} %get-tuple-element.111), channel_id=1, source_target_pairs={{0,8},{8,16},{16,24},{24,28},{28,20},{20,12},{12,4},{4,0},{1,9},{9... | collective-permute-start | bytes 1013768 | tf_op jit(solution)/shard_map/ppermute | solution.py:80
  34.0 9.4 %collective-permute-start.9 = (bf16[3,88,384]{2,1,0:T(8,128)(2,1)S(1)}, bf16[3,88,384]{2,1,0:T(8,128)(2,1)S(1)}, u32[]{:S(2)}, u32[]{:S(2)}) collective-permute-start(bf16[3,88,384]{2,1,0:T(8,128)(2,1)S(1)} %get-tuple-element.108), channel_id=1, source_target_pairs={{8,0},{16,8},{24,16},{28,24},{20,28},{12,20},{4,12},{0,4},{9,1},{1... | collective-permute-start | bytes 608264 | tf_op jit(solution)/shard_map/ppermute | solution.py:80
  34.7 9.7 %collective-permute-start.8 = (bf16[3,88,384]{2,1,0:T(8,128)(2,1)S(1)}, bf16[3,88,384]{2,1,0:T(8,128)(2,1)S(1)}, u32[]{:S(2)}, u32[]{:S(2)}) collective-permute-start(bf16[3,88,384]{2,1,0:T(8,128)(2,1)S(1)} %get-tuple-element.109), channel_id=1, source_target_pairs={{0,8},{8,16},{16,24},{24,28},{28,20},{20,12},{12,4},{4,0},{1,9},{9... | collective-permute-start | bytes 608264 | tf_op jit(solution)/shard_map/ppermute | solution.py:80
  41.3 8.8 %collective-permute-start.15 = (bf16[3,88,640]{2,1,0:T(8,128)(2,1)S(1)}, bf16[3,88,640]{2,1,0:T(8,128)(2,1)S(1)}, u32[]{:S(2)}, u32[]{:S(2)}) collective-permute-start(bf16[3,88,640]{2,1,0:T(8,128)(2,1)S(1)} %get-tuple-element.106), channel_id=1, source_target_pairs={{8,0},{16,8},{24,16},{28,24},{20,28},{12,20},{4,12},{0,4},{9,1},{1... | collective-permute-start | bytes 1013768 | tf_op jit(solution)/shard_map/ppermute | solution.py:80
  45.5 9.4 %collective-permute-start.13 = (bf16[3,88,384]{2,1,0:T(8,128)(2,1)S(1)}, bf16[3,88,384]{2,1,0:T(8,128)(2,1)S(1)}, u32[]{:S(2)}, u32[]{:S(2)}) collective-permute-start(bf16[3,88,384]{2,1,0:T(8,128)(2,1)S(1)} %get-tuple-element.104), channel_id=1, source_target_pairs={{8,0},{16,8},{24,16},{28,24},{20,28},{12,20},{4,12},{0,4},{9,1},{1... | collective-permute-start | bytes 608264 | tf_op jit(solution)/shard_map/ppermute | solution.py:80
  47.2 8.8 %collective-permute-start.12 = (bf16[3,88,384]{2,1,0:T(8,128)(2,1)S(1)}, bf16[3,88,384]{2,1,0:T(8,128)(2,1)S(1)}, u32[]{:S(2)}, u32[]{:S(2)}) collective-permute-start(bf16[3,88,384]{2,1,0:T(8,128)(2,1)S(1)} %get-tuple-element.105), channel_id=1, source_target_pairs={{0,8},{8,16},{16,24},{24,28},{28,20},{20,12},{12,4},{4,0},{1,9},{9... | collective-permute-start | bytes 608264 | tf_op jit(solution)/shard_map/ppermute | solution.py:80
  52.9 8.8 %collective-permute-start.19 = (bf16[3,88,640]{2,1,0:T(8,128)(2,1)S(1)}, bf16[3,88,640]{2,1,0:T(8,128)(2,1)S(1)}, u32[]{:S(2)}, u32[]{:S(2)}) collective-permute-start(bf16[3,88,640]{2,1,0:T(8,128)(2,1)S(1)} %get-tuple-element.102), channel_id=1, source_target_pairs={{8,0},{16,8},{24,16},{28,24},{20,28},{12,20},{4,12},{0,4},{9,1},{1... | collective-permute-start | bytes 1013768 | tf_op jit(solution)/shard_map/ppermute | solution.py:80
  57.1 9.4 %collective-permute-start.17 = (bf16[3,88,384]{2,1,0:T(8,128)(2,1)S(1)}, bf16[3,88,384]{2,1,0:T(8,128)(2,1)S(1)}, u32[]{:S(2)}, u32[]{:S(2)}) collective-permute-start(bf16[3,88,384]{2,1,0:T(8,128)(2,1)S(1)} %get-tuple-element.100), channel_id=1, source_target_pairs={{8,0},{16,8},{24,16},{28,24},{20,28},{12,20},{4,12},{0,4},{9,1},{1... | collective-permute-start | bytes 608264 | tf_op jit(solution)/shard_map/ppermute | solution.py:80
  58.8 8.8 %collective-permute-start.16 = (bf16[3,88,384]{2,1,0:T(8,128)(2,1)S(1)}, bf16[3,88,384]{2,1,0:T(8,128)(2,1)S(1)}, u32[]{:S(2)}, u32[]{:S(2)}) collective-permute-start(bf16[3,88,384]{2,1,0:T(8,128)(2,1)S(1)} %get-tuple-element.101), channel_id=1, source_target_pairs={{0,8},{8,16},{16,24},{24,28},{28,20},{20,12},{12,4},{4,0},{1,9},{9... | collective-permute-start | bytes 608264 | tf_op jit(solution)/shard_map/ppermute | solution.py:80
  64.5 8.8 %collective-permute-start.23 = (bf16[3,88,640]{2,1,0:T(8,128)(2,1)S(1)}, bf16[3,88,640]{2,1,0:T(8,128)(2,1)S(1)}, u32[]{:S(2)}, u32[]{:S(2)}) collective-permute-start(bf16[3,88,640]{2,1,0:T(8,128)(2,1)S(1)} %get-tuple-element.98), channel_id=1, source_target_pairs={{8,0},{16,8},{24,16},{28,24},{20,28},{12,20},{4,12},{0,4},{9,1},{1... | collective-permute-start | bytes 1013768 | tf_op jit(solution)/shard_map/ppermute | solution.py:80
  68.7 9.4 %collective-permute-start.21 = (bf16[3,88,384]{2,1,0:T(8,128)(2,1)S(1)}, bf16[3,88,384]{2,1,0:T(8,128)(2,1)S(1)}, u32[]{:S(2)}, u32[]{:S(2)}) collective-permute-start(bf16[3,88,384]{2,1,0:T(8,128)(2,1)S(1)} %get-tuple-element.96), channel_id=1, source_target_pairs={{8,0},{16,8},{24,16},{28,24},{20,28},{12,20},{4,12},{0,4},{9,1},{1... | collective-permute-start | bytes 608264 | tf_op jit(solution)/shard_map/ppermute | solution.py:80
  70.4 8.8 %collective-permute-start.20 = (bf16[3,88,384]{2,1,0:T(8,128)(2,1)S(1)}, bf16[3,88,384]{2,1,0:T(8,128)(2,1)S(1)}, u32[]{:S(2)}, u32[]{:S(2)}) collective-permute-start(bf16[3,88,384]{2,1,0:T(8,128)(2,1)S(1)} %get-tuple-element.97), channel_id=1, source_target_pairs={{0,8},{8,16},{16,24},{24,28},{28,20},{20,12},{12,4},{4,0},{1,9},{9... | collective-permute-start | bytes 608264 | tf_op jit(solution)/shard_map/ppermute | solution.py:80
  103.4 10.0 %collective-permute-start.29 = (bf16[88,2048]{1,0:T(8,128)(2,1)S(1)}, bf16[88,2048]{1,0:T(8,128)(2,1)S(1)}, u32[]{:S(2)}, u32[]{:S(2)}) collective-permute-start(bf16[88,2048]{1,0:T(8,128)(2,1)S(1)} %get-tuple-element.70), channel_id=1, source_target_pairs={{24,8},{0,16},{20,4},{29,13},{5,21},{9,25},{26,10},{2,18},{22,6},{... | collective-permute-start | bytes 1081352 | tf_op jit(solution)/shard_map/ppermute | solution.py:350
  104.7 9.5 %collective-permute-start.30 = (bf16[88,2048]{1,0:T(8,128)(2,1)S(1)}, bf16[88,2048]{1,0:T(8,128)(2,1)S(1)}, u32[]{:S(2)}, u32[]{:S(2)}) collective-permute-start(bf16[88,2048]{1,0:T(8,128)(2,1)S(1)} %get-tuple-element.71), channel_id=1, source_target_pairs={{28,8},{4,16},{16,4},{25,13},{1,21},{13,25},{30,10},{6,18},{18,6},... | collective-permute-start | bytes 1081352 | tf_op jit(solution)/shard_map/ppermute | solution.py:350
  105.4 15.7 %collective-permute-start.31 = (bf16[88,2048]{1,0:T(8,128)(2,1)S(1)}, bf16[88,2048]{1,0:T(8,128)(2,1)S(1)}, u32[]{:S(2)}, u32[]{:S(2)}) collective-permute-start(bf16[88,2048]{1,0:T(8,128)(2,1)S(1)} %get-tuple-element.72), channel_id=1, source_target_pairs={{0,8},{24,16},{12,4},{5,13},{29,21},{17,25},{2,10},{26,18},{14,6},... | collective-permute-start | bytes 1081352 | tf_op jit(solution)/shard_map/ppermute | solution.py:350
  107.3 13.8 %collective-permute-start.32 = (bf16[88,2048]{1,0:T(8,128)(2,1)S(1)}, bf16[88,2048]{1,0:T(8,128)(2,1)S(1)}, u32[]{:S(2)}, u32[]{:S(2)}) collective-permute-start(bf16[88,2048]{1,0:T(8,128)(2,1)S(1)} %get-tuple-element.73), channel_id=1, source_target_pairs={{4,8},{28,16},{8,4},{1,13},{25,21},{21,25},{6,10},{30,18},{10,6},{... | collective-permute-start | bytes 1081352 | tf_op jit(solution)/shard_map/ppermute | solution.py:350
  108.3 14.2 %collective-permute-start.33 = (bf16[88,2048]{1,0:T(8,128)(2,1)S(1)}, bf16[88,2048]{1,0:T(8,128)(2,1)S(1)}, u32[]{:S(2)}, u32[]{:S(2)}) collective-permute-start(bf16[88,2048]{1,0:T(8,128)(2,1)S(1)} %get-tuple-element.77), channel_id=1, source_target_pairs={{16,8},{8,16},{28,4},{21,13},{13,21},{1,25},{18,10},{10,18},{30,6}... | collective-permute-start | bytes 1081352 | tf_op jit(solution)/shard_map/ppermute | solution.py:350
  113.4 9.1 %collective-permute-start.34 = (bf16[88,2048]{1,0:T(8,128)(2,1)S(1)}, bf16[88,2048]{1,0:T(8,128)(2,1)S(1)}, u32[]{:S(2)}, u32[]{:S(2)}) collective-permute-start(bf16[88,2048]{1,0:T(8,128)(2,1)S(1)} %get-tuple-element.79), channel_id=1, source_target_pairs={{20,8},{12,16},{24,4},{17,13},{9,21},{5,25},{22,10},{14,18},{26,6}... | collective-permute-start | bytes 1081352 | tf_op jit(solution)/shard_map/ppermute | solution.py:350
  134.5 26.2 %collective-permute-start.35 = (bf16[176,2048]{1,0:T(8,128)(2,1)S(1)}, bf16[176,2048]{1,0:T(8,128)(2,1)S(1)}, u32[]{:S(2)}, u32[]{:S(2)}) collective-permute-start(bf16[176,2048]{1,0:T(8,128)(2,1)S(1)} %get-tuple-element.83), channel_id=1, source_target_pairs={{8,12},{16,20},{4,0},{13,9},{21,17},{25,29},{10,14},{18,22},{6,2},... | collective-permute-start | bytes 2162696 | tf_op jit(solution)/shard_map/ppermute | solution.py:350
  135.8 27.0 %collective-permute-start.37 = (bf16[88,2048]{1,0:T(8,128)(2,1)S(1)}, bf16[88,2048]{1,0:T(8,128)(2,1)S(1)}, u32[]{:S(2)}, u32[]{:S(2)}) collective-permute-start(bf16[88,2048]{1,0:T(8,128)(2,1)S(1)} %get-tuple-element.85), channel_id=1, source_target_pairs={{8,24},{16,0},{4,20},{13,29},{21,5},{25,9},{10,26},{18,2},{6,22},{... | collective-permute-start | bytes 1081352 | tf_op jit(solution)/shard_map/ppermute | solution.py:350
  137.1 28.7 %collective-permute-start.38 = (bf16[88,2048]{1,0:T(8,128)(2,1)S(1)}, bf16[88,2048]{1,0:T(8,128)(2,1)S(1)}, u32[]{:S(2)}, u32[]{:S(2)}) collective-permute-start(bf16[88,2048]{1,0:T(8,128)(2,1)S(1)} %get-tuple-element.86), channel_id=1, source_target_pairs={{8,28},{16,4},{4,16},{13,25},{21,1},{25,13},{10,30},{18,6},{6,18},... | collective-permute-start | bytes 1081352 | tf_op jit(solution)/shard_map/ppermute | solution.py:350
  137.8 28.0 %collective-permute-start.39 = (bf16[88,2048]{1,0:T(8,128)(2,1)S(1)}, bf16[88,2048]{1,0:T(8,128)(2,1)S(1)}, u32[]{:S(2)}, u32[]{:S(2)}) collective-permute-start(bf16[88,2048]{1,0:T(8,128)(2,1)S(1)} %get-tuple-element.87), channel_id=1, source_target_pairs={{8,16},{16,8},{4,28},{13,21},{21,13},{25,1},{10,18},{18,10},{6,30}... | collective-permute-start | bytes 1081352 | tf_op jit(solution)/shard_map/ppermute | solution.py:350
  160.8 9.8 %collective-permute-start.40 = (bf16[88,2048]{1,0:T(8,128)(2,1)S(1)}, bf16[88,2048]{1,0:T(8,128)(2,1)S(1)}, u32[]{:S(2)}, u32[]{:S(2)}) collective-permute-start(bf16[88,2048]{1,0:T(8,128)(2,1)S(1)} %get-tuple-element.89), channel_id=1, source_target_pairs={{8,0},{16,24},{4,12},{13,5},{21,29},{25,17},{10,2},{18,26},{6,14},... | collective-permute-start | bytes 1081352 | tf_op jit(solution)/shard_map/ppermute | solution.py:350
  (10 other events, 80.5 us)
